TPU v7x, 32 devices: a whole 2x2x4 slice. The times are simulated.
32 devices in a mesh: seq: 16 (over z, y, x), ch: 2 (over core).
Axes of the slice: x: 2, y: 2, z: 4, core: 2. Of those that a mesh axis runs over, the one named last changes fastest.
Arguments:
- tokens: bfloat16 [16384, 768], P('seq', 'ch'), may hold values from -6 to 6
- seg_ids: int32 [16384], replicated, may hold values from 0 to 7, never falling along the last dimension, each value on 1 to 8192 neighbouring positions
- norm1_gain: float32 [768], P('ch'), may hold values from 0.5 to 1.5
- in_weight: bfloat16 [768, 3, 768], P(None, None, 'ch'), may hold values from -0.21875 to 0.21875
- short_weight: float32 [3, 3, 768], P(None, None, 'ch'), may hold values from -3.5 to 3.5
- filt_w1: float32 [33, 64], replicated, may hold values from -1 to 1
- filt_b1: float32 [64], replicated, may hold values from -3.140625 to 3.140625
- filt_w2: float32 [64, 64], replicated, may hold values from -0.75 to 0.75
- filt_w3: float32 [64, 768], P(None, 'ch'), may hold values from -0.25 to 0.25
- long_bias: float32 [768], P('ch'), may hold values from -6 to 6
- tail_gain: float32 [768], P('ch'), may hold values from -6 to 6
- tail_rate: float32 [768], P('ch'), may hold values from 1.2207031e-05 to 0.05
- out_weight: bfloat16 [768, 768], P('ch'), may hold values from -0.21875 to 0.21875
- norm2_gain: float32 [768], P('ch'), may hold values from 0.5 to 1.5
- up_weight: bfloat16 [768, 3072], P(None, 'ch'), may hold values from -0.21875 to 0.21875
- down_weight: bfloat16 [3072, 768], P('ch'), may hold values from -0.109375 to 0.109375
- grad_out: bfloat16 [16384, 768], P('seq', 'ch'), may hold values from -8 to 8
Outputs:
- output: float32 [16384, 768], P('seq', 'ch')
- grad_tokens: float32 [16384, 768], P('seq', 'ch')
- grad_norm1_gain: float32 [768], replicated
- grad_in_weight: float32 [768, 3, 768], P('seq', None, 'ch')
- grad_short_weight: float32 [3, 3, 768], replicated
- grad_filt_w1: float32 [33, 64], replicated
- grad_filt_b1: float32 [64], replicated
- grad_filt_w2: float32 [64, 64], replicated
- grad_filt_w3: float32 [64, 768], replicated
- grad_long_bias: float32 [768], replicated
- grad_tail_gain: float32 [768], replicated
- grad_tail_rate: float32 [768], replicated
- grad_out_weight: float32 [768, 768], P('ch', 'seq')
- grad_norm2_gain: float32 [768], replicated
- grad_up_weight: float32 [768, 3072], P('seq', 'ch')
- grad_down_weight: float32 [3072, 768], P('ch', 'seq')
Inputs may be any that keep to these rules, and one draw needn't show every extreme that they name: `seg_ids`: document numbers over all 16384 tokens: never falling, rising by one where a new document starts; each document has 1 to 8192 tokens and one has exactly 8192.
All inputs are finite; a program needn't handle non-finite values.
Results may differ from a plain program's by a relative error of at most 0.013.
Values may be sent and summed in bfloat16 or wider, within the bound.
A program may use at most 256 MiB of HBM per device.

v0:
```python
import functools

import jax
import jax.numpy as jnp
from jax import lax
from jax.experimental import pallas as pl
from jax.experimental.pallas import tpu as pltpu
from jax.sharding import PartitionSpec as P

FIR = 32
SEQ_LEN = 16384
DOC_MOST = 8192
EPSILON = 1e-05
FREQUENCY = 0.4
HIGHEST = lax.Precision.HIGHEST
MESH = pl.DeviceIdType.MESH
F32, BF16 = jnp.float32, jnp.bfloat16

BEFORE = 48
AFTER = 80
LANES = 128
BLOCK = 256
CHUNK = 64
SUMS = 48
HEAD = 16
VMEM_LIMIT = 56 << 20
ROOT_TWO_OVER_PI = 0.7978845608028654


def position_table(filter_len, band_count):
    places = jnp.arange(filter_len, dtype=F32)
    harmonics = jnp.arange(1, band_count + 1, dtype=F32)
    angles = FREQUENCY * places[:, None] * harmonics[None, :]
    return jnp.concatenate([places[:, None] / filter_len, jnp.cos(angles), jnp.sin(angles)], axis=1)


def of(ref, start, size):
    return pl.ds(pl.multiple_of(start, size), size)


def exchange_kernel(sizes, tokens, gout, w_in, w_out, w_up, w_down, head, taps, filt,
                    tok_o, g_o, in_o, out_o, up_o, down_o, vec_o, local_sem, send_sem, recv_sem):
    n, rows, width, hidden = sizes
    block = rows // 2
    s, c = lax.axis_index("seq"), lax.axis_index("ch")
    barrier = pltpu.get_barrier_semaphore()
    pl.semaphore_signal(barrier, inc=1, device_id=(s, 1 - c), device_id_type=MESH)

    @pl.when((c == 0) & (s > 0))
    def _():
        for k in range(2):
            pl.semaphore_signal(barrier, inc=1, device_id=(s - 1, k), device_id_type=MESH)

    @pl.when(s < n - 1)
    def _():
        pl.semaphore_wait(barrier, 2)

    @pl.when(s == n - 1)
    def _():
        pl.semaphore_wait(barrier, 1)

    cols = pl.ds(pl.multiple_of(c * width, width), width)
    hid = pl.ds(pl.multiple_of(c * hidden, hidden), hidden)
    pairs = [
        (w_in, in_o.at[:, :, cols]),
        (head, vec_o.at[pl.ds(0, HEAD), cols]),
        (taps, vec_o.at[pl.ds(HEAD, FIR), cols]),
        (filt, vec_o.at[pl.ds(HEAD + FIR, filt.shape[0]), cols]),
        (w_out, out_o.at[cols, :]),
        (w_up, up_o.at[:, hid]),
        (w_down, down_o.at[hid, :]),
    ]

    def remote(src, dst, k, target):
        return pltpu.make_async_remote_copy(
            src_ref=src, dst_ref=dst, send_sem=send_sem.at[k], recv_sem=recv_sem.at[k],
            device_id=target, device_id_type=MESH)

    partner = (s, 1 - c)
    left, right = pl.ds(0, width), pl.ds(width, width)
    first, second = pl.ds(0, block), pl.ds(block, block)
    early = pl.ds(block - BEFORE, block + BEFORE)
    tail = pl.ds(rows - BEFORE, BEFORE)

    @pl.when(c == 0)
    def _():
        remote(tokens.at[early, :], tok_o.at[:, left], 0, partner).start()
        remote(gout.at[second, :], g_o.at[:, left], 1, partner).start()
        pltpu.make_async_copy(tokens.at[first, :], tok_o.at[pl.ds(BEFORE, block), left], local_sem.at[0]).start()
        pltpu.make_async_copy(gout.at[first, :], g_o.at[:, left], local_sem.at[1]).start()

        @pl.when(s < n - 1)
        def _():
            remote(tokens.at[tail, :], tok_o.at[pl.ds(0, BEFORE), left], 2, (s + 1, 0)).start()

    @pl.when(c == 1)
    def _():
        remote(tokens.at[first, :], tok_o.at[pl.ds(BEFORE, block), right], 0, partner).start()
        remote(gout.at[first, :], g_o.at[:, right], 1, partner).start()
        pltpu.make_async_copy(tokens.at[early, :], tok_o.at[:, right], local_sem.at[0]).start()
        pltpu.make_async_copy(gout.at[second, :], g_o.at[:, right], local_sem.at[1]).start()

        @pl.when(s < n - 1)
        def _():
            remote(tokens.at[tail, :], tok_o.at[pl.ds(0, BEFORE), right], 3, (s + 1, 0)).start()

    for k, (src, dst) in enumerate(pairs):
        remote(src, dst, 4 + k, partner).start()
        pltpu.make_async_copy(src, dst, local_sem.at[2 + k]).start()

    for k, (src, dst) in enumerate(pairs):
        pltpu.make_async_copy(src, dst, local_sem.at[2 + k]).wait()
        remote(src, dst, 4 + k, partner).wait()

    @pl.when(c == 0)
    def _():
        remote(tokens.at[early, :], tok_o.at[:, left], 0, partner).wait_send()
        remote(gout.at[second, :], g_o.at[:, left], 1, partner).wait_send()
        remote(tokens.at[first, :], tok_o.at[pl.ds(BEFORE, block), right], 0, partner).wait_recv()
        remote(gout.at[first, :], g_o.at[:, right], 1, partner).wait_recv()
        pltpu.make_async_copy(tokens.at[first, :], tok_o.at[pl.ds(BEFORE, block), left], local_sem.at[0]).wait()
        pltpu.make_async_copy(gout.at[first, :], g_o.at[:, left], local_sem.at[1]).wait()

        @pl.when(s < n - 1)
        def _():
            remote(tokens.at[tail, :], tok_o.at[pl.ds(0, BEFORE), left], 2, (s + 1, 0)).wait_send()

        @pl.when(s > 0)
        def _():
            remote(tokens.at[tail, :], tok_o.at[pl.ds(0, BEFORE), left], 2, partner).wait_recv()
            remote(tokens.at[tail, :], tok_o.at[pl.ds(0, BEFORE), right], 3, partner).wait_recv()

    @pl.when(c == 1)
    def _():
        remote(tokens.at[first, :], tok_o.at[pl.ds(BEFORE, block), right], 0, partner).wait_send()
        remote(gout.at[first, :], g_o.at[:, right], 1, partner).wait_send()
        remote(tokens.at[early, :], tok_o.at[:, left], 0, partner).wait_recv()
        remote(gout.at[second, :], g_o.at[:, left], 1, partner).wait_recv()
        pltpu.make_async_copy(tokens.at[early, :], tok_o.at[:, right], local_sem.at[0]).wait()
        pltpu.make_async_copy(gout.at[second, :], g_o.at[:, right], local_sem.at[1]).wait()

        @pl.when(s < n - 1)
        def _():
            remote(tokens.at[tail, :], tok_o.at[pl.ds(0, BEFORE), right], 3, (s + 1, 0)).wait_send()


def exchange(n, tokens, gout, w_in, w_out, w_up, w_down, *vec):
    rows, width = tokens.shape
    hidden = w_up.shape[1]
    full, block = 2 * width, rows // 2
    anywhere = pl.BlockSpec(memory_space=pl.ANY)
    return pl.pallas_call(
        functools.partial(exchange_kernel, (n, rows, width, hidden)),
        name="exchange",
        out_shape=(
            jax.ShapeDtypeStruct((BEFORE + block, full), BF16),
            jax.ShapeDtypeStruct((block, full), BF16),
            jax.ShapeDtypeStruct((3, full, full), BF16),
            jax.ShapeDtypeStruct((full, full), BF16),
            jax.ShapeDtypeStruct((full, 2 * hidden), BF16),
            jax.ShapeDtypeStruct((2 * hidden, full), BF16),
            jax.ShapeDtypeStruct((sum(part.shape[0] for part in vec), full), F32),
        ),
        in_specs=[anywhere] * 9,
        out_specs=[pl.BlockSpec(memory_space=pltpu.VMEM)] * 7,
        scratch_shapes=[pltpu.SemaphoreType.DMA((9,)), pltpu.SemaphoreType.DMA((11,)), pltpu.SemaphoreType.DMA((11,))],
        compiler_params=pltpu.CompilerParams(collective_id=0, has_side_effects=True, vmem_limit_bytes=VMEM_LIMIT),
    )(tokens, gout, w_in, w_out, w_up, w_down, *vec)


def row_stats(values):
    center = jnp.mean(values, axis=1, keepdims=True)
    shifted = values - center
    inverse = lax.rsqrt(jnp.mean(shifted * shifted, axis=1, keepdims=True) + EPSILON)
    return shifted * inverse, inverse


def mixer_kernel(block, ids_s, tok, win, vec, vblk, ids, n1_o, proj_o, v_o, x0_o, x1_o, u_o, long_o, car_o, end_o,
                 n1_s, proj_s, u_s, state_s):
    rows = BEFORE + block
    lane_blocks = BLOCK // LANES

    @pl.when(pl.program_id(0) == 0)
    def _():
        gain = vec[0:1, :]

        def normed(j, _):
            at = pl.ds(pl.multiple_of(j * 16, 16), 16)
            values = jnp.where(ids[at, 0:1] >= 0.0, tok[at, :].astype(F32), 0.0)
            n1_s[at, :] = (row_stats(values)[0] * gain).astype(BF16)
            return 0

        lax.fori_loop(0, rows // 16, normed, 0)
        n1_o[...] = n1_s[pl.ds(BEFORE, block), :]

    for s in range(3):
        part = jnp.dot(n1_s[...], win[s], preferred_element_type=F32).astype(BF16)
        proj_o[s] = part
        for b in range(lane_blocks):
            proj_s[s, b] = part[:, b * LANES : (b + 1) * LANES].astype(F32)

    def convolved(start, size):
        own = ids[pl.ds(start, size), :]
        same = [None] + [own == ids[pl.ds(start - j, size), :] for j in (1, 2)]
        results = []
        for b in range(lane_blocks):
            lanes = slice(b * LANES, (b + 1) * LANES)
            streams = []
            for s in range(3):
                value = vblk[6 + s : 7 + s, lanes] * proj_s[s, b, pl.ds(start, size), :]
                for j in (1, 2):
                    tap = vblk[6 + 3 * j + s : 7 + 3 * j + s, lanes]
                    value += jnp.where(same[j], tap * proj_s[s, b, pl.ds(start - j, size), :], 0.0)
                streams.append(value)
            gated = (streams[0] * streams[2]).astype(BF16)
            u_s[b, pl.ds(start, size), :] = gated.astype(F32)
            results.append((streams, gated))
        return results

    head = convolved(16, 32)
    for b in range(lane_blocks):
        lanes = slice(b * LANES, (b + 1) * LANES)
        u_o[0:16, lanes] = jnp.zeros((16, LANES), BF16)
        u_o[16:48, lanes] = head[b][1]

    def conv_chunk(j, _):
        start = pl.multiple_of(BEFORE + j * 32, 16)
        to = pl.ds(pl.multiple_of(j * 32, 32), 32)
        for b, (streams, gated) in enumerate(convolved(start, 32)):
            lanes = slice(b * LANES, (b + 1) * LANES)
            v_o[to, lanes] = streams[0]
            x0_o[to, lanes] = streams[1]
            x1_o[to, lanes] = streams[2]
            u_o[pl.ds(start, 32), lanes] = gated
        return 0

    lax.fori_loop(0, block // 32, conv_chunk, 0)

    row_id = lax.broadcasted_iota(jnp.int32, (8, LANES), 0)
    rates = [vblk[4:5, b * LANES : (b + 1) * LANES] for b in range(lane_blocks)]
    powers = [jnp.exp(-rate * (row_id + 1).astype(F32)) for rate in rates]
    lams = [[jnp.exp(-rate * float(step)) for step in (1, 2, 4)] for rate in rates]
    for b in range(lane_blocks):
        state_s[b, 0:8, :] = jnp.zeros((8, LANES), F32)

    def scan_group(g, carry):
        start = pl.multiple_of(BEFORE + g * 8, 8)
        own = ids[pl.ds(start, 8), :]
        masks = [(own == ids[pl.ds(start - step, 8), :]) & (row_id >= step) for step in (1, 2, 4)]
        joined = own == jnp.broadcast_to(ids[pl.ds(start - 1, 1), :], (8, LANES))
        result = []
        for b in range(lane_blocks):
            value = u_s[b, pl.ds(start, 8), :]
            for mask, lam, step in zip(masks, lams[b], (1, 2, 4)):
                value += jnp.where(mask, lam * pltpu.roll(value, step, 0), 0.0)
            value += jnp.where(joined, powers[b] * carry[b], 0.0)
            state_s[b, pl.ds(pl.multiple_of(8 + g * 8, 8), 8), :] = value
            result.append(jnp.broadcast_to(value[7:8, :], (8, LANES)))
        return tuple(result)

    zero = jnp.zeros((8, LANES), F32)
    final = lax.fori_loop(0, block // 8, scan_group, (zero,) * lane_blocks, unroll=4)
    for b in range(lane_blocks):
        end_o[:, b * LANES : (b + 1) * LANES] = final[b][0:1, :]

    for b in range(lane_blocks):
        lanes = slice(b * LANES, (b + 1) * LANES)
        bias, gain, lam = vblk[2:3, lanes], vblk[3:4, lanes], lams[b][0]
        nu = vblk[5:6, lanes]

        def long_chunk(j, _):
            start = pl.multiple_of(BEFORE + j * CHUNK, 16)
            to = pl.ds(pl.multiple_of(j * CHUNK, CHUNK), CHUNK)
            own = ids[pl.ds(start, CHUNK), :]
            here = u_s[b, pl.ds(start, CHUNK), :]
            previous = state_s[b, pl.ds(7 + j * CHUNK, CHUNK), :]
            carried = jnp.where(own == ids[pl.ds(start - 1, CHUNK), :], lam * previous, 0.0)
            car_o[to, lanes] = carried
            base = bias * here + (gain * nu) * carried
            whole = ids_s[start + CHUNK - 1] == ids_s[start - FIR + 1]

            @pl.when(whole)
            def _():
                total = base
                for k in range(FIR):
                    total += vblk[16 + k : 17 + k, lanes] * u_s[b, pl.ds(start - k, CHUNK), :]
                long_o[to, lanes] = total

            @pl.when(jnp.logical_not(whole))
            def _():
                total = base
                for k in range(FIR):
                    term = vblk[16 + k : 17 + k, lanes] * u_s[b, pl.ds(start - k, CHUNK), :]
                    total += jnp.where(own == ids[pl.ds(start - k, CHUNK), :], term, 0.0)
                long_o[to, lanes] = total

            return 0

        lax.fori_loop(0, block // CHUNK, long_chunk, 0)


def mixer(ids_s, tok, win, vec, ids):
    rows, full = tok.shape
    block = rows - BEFORE
    lane_blocks = BLOCK // LANES
    whole = lambda *shape: pl.BlockSpec(shape, lambda i: (0,) * len(shape))
    by_channel = lambda count: pl.BlockSpec((count, BLOCK), lambda i: (0, i))
    return pl.pallas_call(
        functools.partial(mixer_kernel, block),
        name="mixer",
        grid=(full // BLOCK,),
        out_shape=(
            jax.ShapeDtypeStruct((block, full), BF16),
            jax.ShapeDtypeStruct((3, rows, full), BF16),
            jax.ShapeDtypeStruct((block, full), F32),
            jax.ShapeDtypeStruct((block, full), F32),
            jax.ShapeDtypeStruct((block, full), F32),
            jax.ShapeDtypeStruct((rows, full), BF16),
            jax.ShapeDtypeStruct((block, full), F32),
            jax.ShapeDtypeStruct((block, full), F32),
            jax.ShapeDtypeStruct((1, full), F32),
        ),
        in_specs=[
            pl.BlockSpec(memory_space=pltpu.SMEM),
            whole(rows, full),
            pl.BlockSpec((3, full, BLOCK), lambda i: (0, 0, i)),
            whole(*vec.shape),
            by_channel(vec.shape[0]),
            whole(*ids.shape),
        ],
        out_specs=(
            whole(block, full),
            pl.BlockSpec((3, rows, BLOCK), lambda i: (0, 0, i)),
            by_channel(block),
            by_channel(block),
            by_channel(block),
            by_channel(rows),
            by_channel(block),
            by_channel(block),
            by_channel(1),
        ),
        scratch_shapes=[
            pltpu.VMEM((rows, full), BF16),
            pltpu.VMEM((3, lane_blocks, rows, LANES), F32),
            pltpu.VMEM((lane_blocks, rows, LANES), F32),
            pltpu.VMEM((lane_blocks, 8 + block, LANES), F32),
        ],
        compiler_params=pltpu.CompilerParams(vmem_limit_bytes=VMEM_LIMIT),
    )(ids_s, tok, win, vec, vec, ids)


def push_kernel(n, reach, backward, halo_in, *refs):
    if halo_in:
        end, halo, weights, joined_o, halo_o, slots, send_sem, recv_sem, halo_sem = refs
    else:
        end, weights, joined_o, slots, send_sem, recv_sem = refs
    s, c = lax.axis_index("seq"), lax.axis_index("ch")
    total, me = 2 * n, 2 * s + c
    ahead = -1 if backward else 1
    place = total - 1 - me if backward else me
    barrier = pltpu.get_barrier_semaphore()

    def device(index):
        return (index // 2, index % 2)

    for k in range(reach):

        @pl.when(place - 1 - k >= 0)
        def _():
            pl.semaphore_signal(barrier, inc=1, device_id=device(me - ahead * (1 + k)), device_id_type=MESH)

    for count in range(1, reach + 1):

        @pl.when((total - 1 - place >= count) if count == reach else (total - 1 - place == count))
        def _():
            pl.semaphore_wait(barrier, count)

    def copy(k):
        return pltpu.make_async_remote_copy(
            src_ref=end, dst_ref=slots.at[k], send_sem=send_sem.at[k], recv_sem=recv_sem.at[k],
            device_id=device(me + ahead * (1 + k)), device_id_type=MESH)

    def halo_copy():
        return pltpu.make_async_remote_copy(
            src_ref=halo, dst_ref=halo_o, send_sem=halo_sem.at[0], recv_sem=halo_sem.at[1],
            device_id=device(me + ahead), device_id_type=MESH)

    for k in range(reach):

        @pl.when(place + 1 + k < total)
        def _():
            copy(k).start()
            if halo_in and k == 0:
                halo_copy().start()

    joined_o[...] = jnp.zeros_like(joined_o)
    for k in range(reach):

        @pl.when(place - 1 - k >= 0)
        def _():
            copy(k).wait_recv()
            for row in range(joined_o.shape[0]):
                joined_o[row : row + 1, :] += weights[row, k : k + 1, :] * slots[k]

    for k in range(reach):

        @pl.when(place + 1 + k < total)
        def _():
            copy(k).wait_send()

    if halo_in:

        @pl.when(place + 1 < total)
        def _():
            halo_copy().wait_send()

        @pl.when(place - 1 >= 0)
        def _():
            halo_copy().wait_recv()


def push(n, end, weights, backward, collective_id, halo=None):
    results, reach, full = weights.shape
    vmem = pl.BlockSpec(memory_space=pltpu.VMEM)
    out_shape = [jax.ShapeDtypeStruct((results, full), F32)]
    scratch = [pltpu.VMEM((reach, 1, full), F32), pltpu.SemaphoreType.DMA((reach,)), pltpu.SemaphoreType.DMA((reach,))]
    operands = [end]
    if halo is not None:
        out_shape.append(jax.ShapeDtypeStruct(halo.shape, halo.dtype))
        scratch.append(pltpu.SemaphoreType.DMA((2,)))
        operands.append(halo)
    operands.append(weights)
    return pl.pallas_call(
        functools.partial(push_kernel, n, reach, backward, halo is not None),
        name="push_back" if backward else "push_on",
        out_shape=out_shape,
        in_specs=[vmem] * len(operands),
        out_specs=[vmem] * len(out_shape),
        scratch_shapes=scratch,
        compiler_params=pltpu.CompilerParams(collective_id=collective_id, has_side_effects=True),
    )(*operands)


TILE = 512
PART = TILE // 2
STAGES = 5


class Summing:
    def __init__(self, tiles, rows, staged, first, second, third, fourth, fifth, send_sem, recv_sem):
        self.tiles, self.rows, self.staged = tiles, rows, staged
        self.first, self.second, self.third, self.fourth, self.fifth = first, second, third, fourth, fifth
        self.send_sem, self.recv_sem = send_sem, recv_sem
        self.s, self.c = lax.axis_index("seq"), lax.axis_index("ch")
        self.bits = [(self.s // (1 << b)) % 2 for b in range(4)]
        self.peers = [(self.s + (1 - 2 * bit) * (1 << b), self.c) for b, bit in enumerate(self.bits)]
        self.partner = (self.s, 1 - self.c)
        self.order = ((0, 1, 2, 3), (1, 0, 2, 3))

    @staticmethod
    def scratch(tiles, rows):
        return [
            pltpu.VMEM((2, 2, 2, 2, 2, 2, rows, TILE), BF16),
            pltpu.VMEM((tiles, 2, 2, 2, 2, rows, TILE), BF16),
            pltpu.VMEM((tiles, 2, 2, 2, 2, rows, PART), BF16),
            pltpu.VMEM((tiles, 2, 2, 2, rows, PART), BF16),
            pltpu.VMEM((tiles, 2, 2, rows, PART), BF16),
            pltpu.VMEM((tiles, 2, rows, PART), BF16),
            pltpu.SemaphoreType.DMA((tiles, 1 + 2 * 4)),
            pltpu.SemaphoreType.DMA((tiles, 1 + 2 * 4)),
        ]

    def greet(self, barrier):
        for peer in [self.partner] + self.peers:
            pl.semaphore_signal(barrier, inc=1, device_id=peer, device_id_type=MESH)
        pl.semaphore_wait(barrier, 5)

    def remote(self, src, dst, tile, k, target):
        return pltpu.make_async_remote_copy(
            src_ref=src, dst_ref=dst, send_sem=self.send_sem.at[tile, k], recv_sem=self.recv_sem.at[tile, k],
            device_id=target, device_id_type=MESH)

    def copies(self, tile, stage):
        if stage == 0:
            return [self.remote(self.staged.at[tile % 2, 1], self.first.at[tile], tile, 0, self.partner)]
        result = []
        for part in range(2):
            bit = self.order[part][stage - 1]
            away = 1 - self.bits[bit]
            at = pl.ds(part * PART, PART)
            if stage == 1:
                src = self.first.at[tile, :, :, :, away, :, at] if part == 0 else self.first.at[tile, :, :, away, :, :, at]
                dst = self.second.at[tile, part]
            elif stage == 2:
                src, dst = self.second.at[tile, part, :, :, away], self.third.at[tile, part]
            elif stage == 3:
                src, dst = self.third.at[tile, part, :, away], self.fourth.at[tile, part]
            else:
                src, dst = self.fourth.at[tile, part, away], self.fifth.at[tile, part]
            result.append(self.remote(src, dst, tile, 1 + 2 * (stage - 1) + part, self.peers[bit]))
        return result

    def start(self, tile, stage):
        for copy in self.copies(tile, stage):
            copy.start()

    def advance(self, tile, stage, total):
        for copy in self.copies(tile, stage):
            copy.wait()
        x, y, low, high = self.bits
        if stage == 0:
            def add(i, _):
                for h in range(2):
                    for j in range(2):
                        for k in range(2):
                            self.first[tile, h, i, j, k] += self.staged[tile % 2, 0, h, i, j, k]
                return 0
            lax.fori_loop(0, 2, add, 0)
        elif stage == 1:
            def add(i, _):
                for h in range(2):
                    for k in range(2):
                        self.second[tile, 0, h, i, k] += self.first[tile, h, i, k, x, :, 0:PART]
                        self.second[tile, 1, h, i, k] += self.first[tile, h, i, y, k, :, PART:TILE]
                return 0
            lax.fori_loop(0, 2, add, 0)
        elif stage == 2:
            for i in range(2):
                for k in range(2):
                    self.third[tile, 0, i, k] += self.second[tile, 0, i, k, y]
                    self.third[tile, 1, i, k] += self.second[tile, 1, i, k, x]
        elif stage == 3:
            for part in range(2):
                for i in range(2):
                    self.fourth[tile, part, i] += self.third[tile, part, i, low]
        else:
            for part in range(2):
                mine = self.fourth[tile, part, high].astype(F32)
                total(tile, part, mine + self.fifth[tile, part].astype(F32))
            return
        self.start(tile, stage + 1)


def contract(left, right, dims):
    return lax.dot_general(left, right, (dims, ((), ())), preferred_element_type=F32)


def ffn_kernel(block, tiles, summed, tok, x0, base, car, ids, enter, g, vec, wout, *refs):
    if summed:
        (wup_a, wup_b, wdn_a, wdn_b, out_o, long_o, car_o, gmid_o, gmix_o, gout_w_o, gup_o, gdn_o, gain_o,
         mixed_s, middle_s, n2_s, gn2_s, gout_s, *buffers) = refs
    else:
        (wup, wdn, out_o, long_o, car_o, gmid_o, gmix_o, gout_w_o, gup_o, gdn_o, gain_o,
         mixed_s, middle_s, n2_s, gn2_s, gout_s) = refs
    step = pl.program_id(0)
    rows16 = block // 32

    if summed:
        full = g.shape[1]
        sums = Summing(tiles, full // 16, *buffers)

        @pl.when(step == 0)
        def _():
            sums.greet(pltpu.get_barrier_semaphore())

        def total(tile, part, value):
            ref = (gup_o, gdn_o)[part]
            ref[:, pl.ds(pl.multiple_of(tile * PART, PART), PART)] = value

        for stage in range(STAGES - 1, -1, -1):

            @pl.when((step - 1 - stage >= 0) & (step - 1 - stage < tiles))
            def _():
                sums.advance(step - 1 - stage, stage, total)

    @pl.when(step == 0)
    def _():
        rate, tail = vec[4:5, :], vec[3:4, :] * vec[5:6, :]
        state = enter[0:1, :]
        last = ids[pl.ds(BEFORE - 1, 1), 0:1]

        def mix(j, _):
            at = pl.ds(pl.multiple_of(j * 32, 32), 32)
            steps = (lax.broadcasted_iota(jnp.int32, (32, 1), 0) + (j * 32 + 1)).astype(F32)
            same = ids[pl.ds(pl.multiple_of(BEFORE + j * 32, 16), 32), 0:1] == last
            entered = jnp.where(same, jnp.exp(-rate * steps) * state, 0.0)
            car_o[at, :] = car[at, :] + entered
            long = base[at, :] + tail * entered
            long_o[at, :] = long
            mixed_s[at, :] = (long * x0[at, :]).astype(BF16)
            return 0

        lax.fori_loop(0, rows16, mix, 0)
        middle_s[...] = jnp.dot(mixed_s[...], wout[...], preferred_element_type=F32)

        def norm(j, _):
            at = pl.ds(pl.multiple_of(j * 32, 32), 32)
            values = middle_s[at, :] + tok[pl.ds(pl.multiple_of(BEFORE + j * 32, 16), 32), :].astype(F32)
            middle_s[at, :] = values
            out_o[at, :] = values
            n2_s[at, :] = (row_stats(values)[0] * vec[1:2, :]).astype(BF16)
            gn2_s[at, :] = jnp.zeros_like(values)
            return 0

        lax.fori_loop(0, rows16, norm, 0)

    def feed(wup, wdn):
        n2, rows = n2_s[...], g[...]
        up = jnp.dot(n2, wup[...], preferred_element_type=F32)
        pulled = contract(rows, wdn[...], ((1,), (1,)))
        square = up * up
        inner = ROOT_TWO_OVER_PI * up * (1.0 + 0.044715 * square)
        bent = jnp.tanh(inner)
        half = 0.5 * (1.0 + bent)
        active = (up * half).astype(BF16)
        slope = half + (0.5 * ROOT_TWO_OVER_PI) * up * (1.0 - bent * bent) * (1.0 + 0.134145 * square)
        g_up = (pulled * slope).astype(BF16)
        out_o[...] += jnp.dot(active, wdn[...], preferred_element_type=F32)
        gn2_s[...] += contract(g_up, wup[...], ((1,), (1,)))
        return contract(n2, g_up, ((0,), (0,))).astype(BF16), contract(rows, active, ((0,), (0,))).astype(BF16)

    if summed:

        @pl.when(step < tiles)
        def _():
            for half, (wup, wdn) in enumerate(((wup_a, wdn_a), (wup_b, wdn_b))):
                whose = (half + sums.c) % 2
                for part, grad in enumerate(feed(wup, wdn)):
                    cols = slice(part * PART, (part + 1) * PART)
                    for q in range(16):
                        at = (step % 2, whose, q // 8, q // 4 % 2, q // 2 % 2, q % 2, slice(None), cols)
                        sums.staged[at] = grad[q * sums.rows : (q + 1) * sums.rows]
            sums.start(step, 0)
    else:
        gup_o[...], gdn_o[...] = feed(wup, wdn)

    @pl.when(step == (tiles if summed else tiles - 1))
    def _():
        def back(j, total):
            at = pl.ds(pl.multiple_of(j * 32, 32), 32)
            normal, inverse = row_stats(middle_s[at, :])
            grad = gn2_s[at, :]
            total += jnp.sum(grad * normal, axis=0, keepdims=True)
            scaled = grad * vec[1:2, :]
            cross = jnp.mean(scaled * normal, axis=1, keepdims=True)
            result = g[at, :].astype(F32) + inverse * (
                scaled - jnp.mean(scaled, axis=1, keepdims=True) - normal * cross)
            gmid_o[at, :] = result
            gout_s[at, :] = result.astype(BF16)
            return total

        gain_o[...] = lax.fori_loop(0, rows16, back, jnp.zeros_like(gain_o))
        gmix_o[...] = contract(gout_s[...], wout[...], ((1,), (1,)))
        gout_w_o[...] = contract(gout_s[...], mixed_s[...], ((0,), (0,))).astype(BF16)


def ffn(summed, tok, x0, base, car, ids, enter, g, vec, wout, wup, wdn):
    block, full = g.shape
    hidden = wup.shape[1]
    tiles = hidden // TILE
    whole = lambda *shape: pl.BlockSpec(shape, lambda i: (0,) * len(shape), pipeline_mode=pl.Buffered(1))
    wide = lambda dtype: jax.ShapeDtypeStruct((block, full), dtype)
    if summed:
        rows = full // 16
        at = lambda i, half: jnp.minimum(i, tiles - 1) + half * tiles
        weight_specs = [pl.BlockSpec((full, PART), lambda i, half=half: (0, at(i, half))) for half in range(2)]
        weight_specs += [pl.BlockSpec((PART, full), lambda i, half=half: (at(i, half), 0)) for half in range(2)]
        grads = [jax.ShapeDtypeStruct((rows, hidden // 2), F32)] * 2
        grad_specs = [whole(rows, hidden // 2)] * 2
        scratch = Summing.scratch(tiles, rows)
        params = dict(collective_id=4, has_side_effects=True)
        weights = (wup, wup, wdn, wdn)
    else:
        weight_specs = [pl.BlockSpec((full, TILE), lambda i: (0, i)), pl.BlockSpec((TILE, full), lambda i: (i, 0))]
        grads = [jax.ShapeDtypeStruct((full, hidden), BF16)] * 2
        grad_specs = [pl.BlockSpec((full, TILE), lambda i: (0, i))] * 2
        scratch, params, weights = [], {}, (wup, wdn)
    return pl.pallas_call(
        functools.partial(ffn_kernel, block, tiles, summed),
        name="ffn",
        grid=(tiles + STAGES if summed else tiles,),
        out_shape=(
            wide(F32), wide(F32), wide(F32), wide(F32), wide(F32),
            jax.ShapeDtypeStruct((full, full), BF16),
            *grads,
            jax.ShapeDtypeStruct((1, full), F32),
        ),
        in_specs=[
            whole(*tok.shape), whole(block, full), whole(block, full), whole(block, full), whole(*ids.shape),
            whole(*enter.shape), whole(block, full), whole(*vec.shape), whole(full, full),
            *weight_specs,
        ],
        out_specs=(
            whole(block, full), whole(block, full), whole(block, full), whole(block, full), whole(block, full),
            whole(full, full),
            *grad_specs,
            whole(1, full),
        ),
        scratch_shapes=[
            pltpu.VMEM((block, full), BF16),
            pltpu.VMEM((block, full), F32),
            pltpu.VMEM((block, full), BF16),
            pltpu.VMEM((block, full), F32),
            pltpu.VMEM((block, full), BF16),
            *scratch,
        ],
        compiler_params=pltpu.CompilerParams(vmem_limit_bytes=VMEM_LIMIT, **params),
    )(tok, x0, base, car, ids, enter, g, vec, wout, *weights)


def gate_kernel(block, gmix, x0, x1, v, long, car, u, vblk, ids, glong_o, q_o, first_o, halo_o, sums_o, gc_s):
    lane_blocks = BLOCK // LANES
    row_id = lax.broadcasted_iota(jnp.int32, (8, LANES), 0)
    lam_of, power_of, zero = [], [], jnp.zeros((8, LANES), F32)
    for b in range(lane_blocks):
        lanes = slice(b * LANES, (b + 1) * LANES)
        rate = vblk[4:5, lanes]
        tail = vblk[3:4, lanes] * vblk[5:6, lanes]
        lam_of.append([jnp.exp(-rate * float(step)) for step in (1, 2, 4)])
        power_of.append(jnp.exp(-rate * (8 - row_id).astype(F32)))

        def gated(j, totals):
            at = pl.ds(pl.multiple_of(j * 32, 32), 32)
            grad = gmix[at, lanes] * x0[at, lanes]
            glong_o[at, lanes] = grad
            gc_s[b, at, :] = grad * tail
            here = u[pl.ds(pl.multiple_of(BEFORE + j * 32, 16), 32), lanes].astype(F32)
            return (
                totals[0] + jnp.sum((grad * here).reshape(4, 8, LANES), axis=0),
                totals[1] + jnp.sum((grad * car[at, lanes]).reshape(4, 8, LANES), axis=0),
            )

        for row, total in enumerate(lax.fori_loop(0, block // 32, gated, (zero, zero))):
            sums_o[row : row + 1, lanes] = jnp.sum(total, axis=0, keepdims=True)
        halo_o[56:64, lanes] = x1[0:8, lanes]
        halo_o[64:72, lanes] = v[0:8, lanes]
        halo_o[72:80, lanes] = gmix[0:8, lanes] * long[0:8, lanes]

    def scan_group(i, carry):
        g = block // 8 - 1 - i
        to = pl.ds(pl.multiple_of(g * 8, 8), 8)
        start = pl.multiple_of(BEFORE + g * 8, 8)
        own = ids[pl.ds(start, 8), :]
        masks = [(own == ids[pl.ds(start + step, 8), :]) & (row_id < 8 - step) for step in (1, 2, 4)]
        joined = own == jnp.broadcast_to(ids[pl.ds(start + 8, 1), :], (8, LANES))
        result = []
        for b in range(lane_blocks):
            value = gc_s[b, to, :]
            for mask, lam, step in zip(masks, lam_of[b], (1, 2, 4)):
                value += jnp.where(mask, lam * pltpu.roll(value, 8 - step, 0), 0.0)
            value += jnp.where(joined, power_of[b] * carry[b], 0.0)
            q_o[to, b * LANES : (b + 1) * LANES] = value
            result.append(jnp.broadcast_to(value[0:1, :], (8, LANES)))
        return tuple(result)

    final = lax.fori_loop(0, block // 8, scan_group, (zero,) * lane_blocks, unroll=4)
    for b in range(lane_blocks):
        first_o[:, b * LANES : (b + 1) * LANES] = final[b][0:1, :]
    halo_o[0:48, :] = glong_o[0:48, :]
    halo_o[48:56, :] = q_o[0:8, :]


def gate(gmix, x0, x1, v, long, car, u, vec, ids):
    block, full = gmix.shape
    by_channel = lambda count: pl.BlockSpec((count, BLOCK), lambda i: (0, i))
    return pl.pallas_call(
        functools.partial(gate_kernel, block),
        name="gate",
        grid=(full // BLOCK,),
        out_shape=(
            jax.ShapeDtypeStruct((block, full), F32),
            jax.ShapeDtypeStruct((block, full), F32),
            jax.ShapeDtypeStruct((1, full), F32),
            jax.ShapeDtypeStruct((80, full), F32),
            jax.ShapeDtypeStruct((2, full), F32),
        ),
        in_specs=[by_channel(block)] * 6 + [
            by_channel(u.shape[0]), by_channel(vec.shape[0]), pl.BlockSpec(ids.shape, lambda i: (0, 0))],
        out_specs=(by_channel(block), by_channel(block), by_channel(1), by_channel(80), by_channel(2)),
        scratch_shapes=[pltpu.VMEM((BLOCK // LANES, block, LANES), F32)],
        compiler_params=pltpu.CompilerParams(vmem_limit_bytes=VMEM_LIMIT),
    )(gmix, x0, x1, v, long, car, u, vec, ids)


def back_kernel(block, steps, ids_s, glong, q, halo, joined, gmix, long, car, x1, v, u, proj, vec, vblk, ids,
                n1, win, tok, gmid, gw_o, gtok_o, sums_o, gain_o, gl_s, u_s, proj_s, gc_s, gp_s, gn1_s, taps_s):
    lane_blocks = BLOCK // LANES
    step = pl.program_id(0)
    zero = jnp.zeros((8, LANES), F32)

    @pl.when(step == 0)
    def _():
        gn1_s[...] = jnp.zeros_like(gn1_s)

    for b in range(lane_blocks):
        lanes = slice(b * LANES, (b + 1) * LANES)
        gl_s[b, 0:block, :] = glong[:, lanes]
        gl_s[b, block : block + 48, :] = halo[0:48, lanes]
        u_s[b] = u[:, lanes].astype(F32)
        for s in range(3):
            proj_s[s, b] = proj[s, :, lanes].astype(F32)
        taps_s[b] = jnp.zeros_like(taps_s[b])

    for b in range(lane_blocks):
        lanes = slice(b * LANES, (b + 1) * LANES)
        rate, bias = vblk[4:5, lanes], vblk[2:3, lanes]
        tail = vblk[3:4, lanes] * vblk[5:6, lanes]
        mine, following = joined[0:1, lanes], joined[1:2, lanes]
        last = ids[pl.ds(BEFORE + block - 1, 1), :]

        def chunk(j, total):
            at = pl.ds(pl.multiple_of(j * CHUNK, CHUNK), CHUNK)
            start = pl.multiple_of(BEFORE + j * CHUNK, 16)
            own = ids[pl.ds(start, CHUNK), :]
            here = gl_s[b, at, :]
            left = (block - 1 - j * CHUNK - lax.broadcasted_iota(jnp.int32, (CHUNK, LANES), 0)).astype(F32)
            state = q[at, lanes] + jnp.where(own == last, jnp.exp(-rate * left) * mine, 0.0)
            total += jnp.sum((car[at, lanes] * state).reshape(CHUNK // 8, 8, LANES), axis=0)
            base = (bias - tail) * here + state
            after = ids_s[start] == ids_s[start + CHUNK - 1 + FIR - 1]
            before = ids_s[start + CHUNK - 1] == ids_s[start - FIR + 1]

            def finish(grad):
                gc_s[0, b, at, :] = grad * x1[at, lanes]
                gc_s[1, b, at, :] = gmix[at, lanes] * long[at, lanes]
                gc_s[2, b, at, :] = grad * v[at, lanes]

            @pl.when(after)
            def _():
                grad = base
                for k in range(FIR):
                    grad += vblk[16 + k : 17 + k, lanes] * gl_s[b, pl.ds(j * CHUNK + k, CHUNK), :]
                finish(grad)

            @pl.when(jnp.logical_not(after))
            def _():
                grad = base
                for k in range(FIR):
                    term = vblk[16 + k : 17 + k, lanes] * gl_s[b, pl.ds(j * CHUNK + k, CHUNK), :]
                    grad += jnp.where(own == ids[pl.ds(start + k, CHUNK), :], term, 0.0)
                finish(grad)

            @pl.when(before)
            def _():
                for k in range(FIR):
                    term = here * u_s[b, pl.ds(start - k, CHUNK), :]
                    taps_s[b, k] += jnp.sum(term.reshape(CHUNK // 8, 8, LANES), axis=0)

            @pl.when(jnp.logical_not(before))
            def _():
                for k in range(FIR):
                    term = here * u_s[b, pl.ds(start - k, CHUNK), :]
                    term = jnp.where(own == ids[pl.ds(start - k, CHUNK), :], term, 0.0)
                    taps_s[b, k] += jnp.sum(term.reshape(CHUNK // 8, 8, LANES), axis=0)

            return total

        total = lax.fori_loop(0, block // CHUNK, chunk, zero)
        sums_o[41:42, lanes] = jnp.sum(total, axis=0, keepdims=True)
        for k in range(FIR):
            sums_o[k : k + 1, lanes] = jnp.sum(taps_s[b, k], axis=0, keepdims=True)

        start = BEFORE + block
        own = ids[pl.ds(start, 8), :]
        end_id = ids_s[BEFORE + block + AFTER].astype(F32)
        left = (block - 1 - lax.broadcasted_iota(jnp.int32, (8, LANES), 0)).astype(F32)
        state = halo[48:56, lanes] + jnp.where(own == end_id, jnp.exp(-rate * left) * following, 0.0)
        grad = (bias - tail) * gl_s[b, block : block + 8, :] + state
        for k in range(FIR):
            term = vblk[16 + k : 17 + k, lanes] * gl_s[b, block + k : block + k + 8, :]
            grad += jnp.where(own == ids[pl.ds(start + k, 8), :], term, 0.0)
        gc_s[0, b, block : block + 8, :] = grad * halo[56:64, lanes]
        gc_s[1, b, block : block + 8, :] = halo[72:80, lanes]
        gc_s[2, b, block : block + 8, :] = grad * halo[64:72, lanes]

        def short(j, totals):
            at = pl.ds(pl.multiple_of(j * 32, 32), 32)
            start = pl.multiple_of(BEFORE + j * 32, 16)
            own = ids[pl.ds(start, 32), :]
            same = [own == ids[pl.ds(start - k, 32), :] for k in (1, 2)]
            later = [own == ids[pl.ds(start + k, 32), :] for k in (1, 2)]
            result = []
            for s in range(3):
                here = gc_s[s, b, at, :]
                value = vblk[6 + s : 7 + s, lanes] * here
                for k in (1, 2):
                    tap = vblk[6 + 3 * k + s : 7 + 3 * k + s, lanes]
                    value += jnp.where(later[k - 1], tap * gc_s[s, b, pl.ds(j * 32 + k, 32), :], 0.0)
                gp_s[s, at, lanes] = value.astype(BF16)
                for k in range(3):
                    term = here * proj_s[s, b, pl.ds(start - k, 32), :]
                    if k:
                        term = jnp.where(same[k - 1], term, 0.0)
                    result.append(totals[3 * s + k] + jnp.sum(term.reshape(4, 8, LANES), axis=0))
            return tuple(result)

        totals = lax.fori_loop(0, block // 32, short, (zero,) * 9)
        for s in range(3):
            for k in range(3):
                sums_o[32 + 3 * k + s : 33 + 3 * k + s, lanes] = jnp.sum(totals[3 * s + k], axis=0, keepdims=True)
        sums_o[42:SUMS, lanes] = jnp.zeros((SUMS - 42, LANES), F32)

    for s in range(3):
        part = gp_s[s]
        gw_o[s] = contract(n1[...], part, ((0,), (0,))).astype(BF16)
        gn1_s[...] += contract(part, win[s], ((1,), (1,)))

    @pl.when(step == steps - 1)
    def _():
        def back(j, total):
            at = pl.ds(pl.multiple_of(j * 32, 32), 32)
            normal, inverse = row_stats(tok[pl.ds(pl.multiple_of(BEFORE + j * 32, 16), 32), :].astype(F32))
            grad = gn1_s[at, :]
            total += jnp.sum(grad * normal, axis=0, keepdims=True)
            scaled = grad * vec[0:1, :]
            cross = jnp.mean(scaled * normal, axis=1, keepdims=True)
            gtok_o[at, :] = gmid[at, :] + inverse * (
                scaled - jnp.mean(scaled, axis=1, keepdims=True) - normal * cross)
            return total

        gain_o[...] = lax.fori_loop(0, block // 32, back, jnp.zeros_like(gain_o))


def back(ids_s, glong, q, halo, joined, gmix, long, car, x1, v, u, proj, vec, ids, n1, win, tok, gmid):
    block, full = glong.shape
    rows, steps = BEFORE + block, full // BLOCK
    lane_blocks = BLOCK // LANES
    whole = lambda *shape: pl.BlockSpec(shape, lambda i: (0,) * len(shape))
    by_channel = lambda count: pl.BlockSpec((count, BLOCK), lambda i: (0, i))
    stacked = lambda count: pl.BlockSpec((3, count, BLOCK), lambda i: (0, 0, i))
    return pl.pallas_call(
        functools.partial(back_kernel, block, steps),
        name="back",
        grid=(steps,),
        out_shape=(
            jax.ShapeDtypeStruct((3, full, full), BF16),
            jax.ShapeDtypeStruct((block, full), F32),
            jax.ShapeDtypeStruct((SUMS, full), F32),
            jax.ShapeDtypeStruct((1, full), F32),
        ),
        in_specs=[
            pl.BlockSpec(memory_space=pltpu.SMEM),
            by_channel(block), by_channel(block), by_channel(80), by_channel(2),
            by_channel(block), by_channel(block), by_channel(block), by_channel(block), by_channel(block),
            by_channel(rows), stacked(rows), whole(*vec.shape), by_channel(vec.shape[0]), whole(*ids.shape),
            whole(block, full), stacked(full), whole(*tok.shape), whole(block, full),
        ],
        out_specs=(stacked(full), whole(block, full), by_channel(SUMS), whole(1, full)),
        scratch_shapes=[
            pltpu.VMEM((lane_blocks, block + 48, LANES), F32),
            pltpu.VMEM((lane_blocks, rows, LANES), F32),
            pltpu.VMEM((3, lane_blocks, rows, LANES), F32),
            pltpu.VMEM((3, lane_blocks, block + 8, LANES), F32),
            pltpu.VMEM((3, block, BLOCK), BF16),
            pltpu.VMEM((block, full), F32),
            pltpu.VMEM((lane_blocks, FIR, 8, LANES), F32),
        ],
        compiler_params=pltpu.CompilerParams(vmem_limit_bytes=VMEM_LIMIT),
    )(ids_s, glong, q, halo, joined, gmix, long, car, x1, v, u, proj, vec, vec, ids, n1, win, tok, gmid)


def reduce_kernel(sizes, g_in, g_out, small, out, gtok,
                  total_o, small_o, out_full, gtok_full,
                  held, first, arrived, small_s, small_r, local_sem, send_sem, recv_sem, block_send, block_recv):
    n, width, block = sizes
    bits = n.bit_length() - 1
    s, c = lax.axis_index("seq"), lax.axis_index("ch")
    half = held.shape[2] // 2
    partner = (s, 1 - c)
    peers = []
    for bit in range(bits):
        flipped = s + (1 - 2 * ((s // (1 << bit)) % 2)) * (1 << bit)
        peers.append((flipped, c))
    barrier = pltpu.get_barrier_semaphore()
    for peer in [partner] + peers:
        pl.semaphore_signal(barrier, inc=1, device_id=peer, device_id_type=MESH)
    pl.semaphore_wait(barrier, 1 + bits)

    def columns(which, size):
        return pl.ds(pl.multiple_of(which * size, size), size)

    def remote(src, dst, k, target):
        return pltpu.make_async_remote_copy(
            src_ref=src, dst_ref=dst, send_sem=send_sem.at[k], recv_sem=recv_sem.at[k],
            device_id=target, device_id_type=MESH)

    def segments(which):
        parts, start = [], 0
        for stream in range(3):
            parts.append((g_in.at[stream, :, :, columns(which, width)], pl.ds(start, width)))
            start += width
        parts.append((g_out.at[:, :, columns(which, width)], pl.ds(start, width)))
        return parts

    started = []
    for k, (src, at) in enumerate(segments(1 - c)):
        copy = remote(src, first.at[:, :, at], k, partner)
        copy.start()
        started.append(copy)
    copies = [remote(small, small_r.at[0], 6, partner)]
    copies[0].start()
    own_rows = columns(c, block)
    tails = []
    for k, (src, dst) in enumerate(((out, out_full), (gtok, gtok_full))):
        copy = remote(src.at[:, columns(1 - c, width)], dst.at[own_rows, :], 7 + k, partner)
        copy.start()
        tails.append(copy)
    locals_ = []
    for k, (src, at) in enumerate(segments(c)):
        copy = pltpu.make_async_copy(src, held.at[:, :, at], local_sem.at[k])
        copy.start()
        locals_.append(copy)
    for k, (src, dst) in enumerate(((out, out_full), (gtok, gtok_full))):
        copy = pltpu.make_async_copy(src.at[:, columns(c, width)], dst.at[own_rows, :], local_sem.at[6 + k])
        copy.start()
        locals_.append(copy)
    copies[0].wait()
    small_s[0] = small[...] + small_r[0]
    for copy in locals_ + started:
        copy.wait()

    def add_first(b, _):
        held[b] = (held[b].astype(F32) + first[b].astype(F32)).astype(BF16)
        return 0

    lax.fori_loop(0, n, add_first, 0)

    orders = [list(range(bits)), [1, 0] + list(range(2, bits))]
    slot_of, count = [], 0
    for k in range(bits):
        slot_of.append(count)
        count += n >> (k + 1)

    def places(part, k, mine):
        order = orders[part]
        bit, open_bits = order[k], order[k + 1 :]
        fixed = 0
        for done in order[:k]:
            fixed += ((s // (1 << done)) % 2) * (1 << done)
        own = (s // (1 << bit)) % 2
        fixed += (own if mine else 1 - own) * (1 << bit)
        return [fixed + sum(((e >> i) & 1) << b for i, b in enumerate(open_bits)) for e in range(1 << len(open_bits))]

    def block_copy(part, k, e, place):
        slot = slot_of[k] + e
        return pltpu.make_async_remote_copy(
            src_ref=held.at[place, :, pl.ds(part * half, half)], dst_ref=arrived.at[part, slot],
            send_sem=block_send.at[part, slot], recv_sem=block_recv.at[part, slot],
            device_id=peers[orders[part][k]], device_id_type=MESH)

    sent = []
    for k in range(bits):
        for part in range(2):
            if k:
                for e, place in enumerate(places(part, k - 1, True)):
                    block_copy(part, k - 1, e, place).wait_recv()
                    mine = held.at[place, :, pl.ds(part * half, half)]
                    mine[...] = (mine[...].astype(F32) + arrived[part, slot_of[k - 1] + e].astype(F32)).astype(BF16)
            for e, place in enumerate(places(part, k, False)):
                copy = block_copy(part, k, e, place)
                copy.start()
                sent.append(copy)
        if k:
            copies[k].wait()
            small_s[k] = small_s[k - 1] + small_r[k]
        copy = remote(small_s.at[k], small_r.at[k + 1], 9 + k, peers[k])
        copy.start()
        copies.append(copy)
    copies[bits].wait()
    small_o[...] = small_s[bits - 1] + small_r[bits]
    for part in range(2):
        place = places(part, bits - 1, True)[0]
        block_copy(part, bits - 1, 0, place).wait_recv()
        at = pl.ds(part * half, half)
        total_o[:, at] = held[place, :, at].astype(F32) + arrived[part, slot_of[bits - 1]].astype(F32)
    for copy in sent:
        copy.wait_send()
    for copy in tails:
        copy.wait()


def reduce(n, g_in, g_out, small, out, gtok):
    full, block = out.shape[1], out.shape[0]
    width = full // 2
    rows = full // n
    columns = 4 * width
    bits = n.bit_length() - 1
    anywhere = pl.BlockSpec(memory_space=pl.ANY)
    vmem = pl.BlockSpec(memory_space=pltpu.VMEM)
    return pl.pallas_call(
        functools.partial(reduce_kernel, (n, width, block)),
        name="reduce",
        out_shape=(
            jax.ShapeDtypeStruct((rows, columns), F32),
            jax.ShapeDtypeStruct(small.shape, F32),
            jax.ShapeDtypeStruct((2 * block, width), F32),
            jax.ShapeDtypeStruct((2 * block, width), F32),
        ),
        in_specs=[anywhere] * 2 + [vmem] + [anywhere] * 2,
        out_specs=(vmem, vmem, vmem, vmem),
        scratch_shapes=[
            pltpu.VMEM((n, rows, columns), BF16),
            pltpu.VMEM((n, rows, columns), BF16),
            pltpu.VMEM((2, n - 1, rows, columns // 2), BF16),
            pltpu.VMEM((bits,) + small.shape, F32),
            pltpu.VMEM((bits + 1,) + small.shape, F32),
            pltpu.SemaphoreType.DMA((8,)),
            pltpu.SemaphoreType.DMA((9 + bits,)),
            pltpu.SemaphoreType.DMA((9 + bits,)),
            pltpu.SemaphoreType.DMA((2, n - 1)),
            pltpu.SemaphoreType.DMA((2, n - 1)),
        ],
        compiler_params=pltpu.CompilerParams(collective_id=3, has_side_effects=True, vmem_limit_bytes=VMEM_LIMIT),
    )(g_in.reshape(3, n, rows, full), g_out.reshape(n, rows, full), small, out, gtok)


def reduce_plain(n, g_in, g_out, g_up, g_dn, small, out, gtok):
    full = out.shape[1]
    width, hidden = full // 2, g_up.shape[1] // 2
    parts = []
    for stream in range(3):
        parts.append((g_in[stream], width))
    parts += [(g_out, width), (g_up, hidden), (g_dn, hidden)]
    halves = [
        jnp.concatenate([part[:, k * size : (k + 1) * size] for part, size in parts], axis=1).astype(F32)
        for k in range(2)
    ]
    both = lax.psum_scatter(jnp.stack(halves), "ch", scatter_dimension=0, tiled=False)
    total = lax.psum_scatter(both, "seq", scatter_dimension=0, tiled=True)
    swap = lambda whole: lax.all_to_all(whole, "ch", split_axis=1, concat_axis=0, tiled=True)
    return total, lax.psum(small, ("seq", "ch")), swap(out), swap(gtok)


def on_device(tokens, seg_ids, norm1_gain, in_weight, short_weight, filt_w1, filt_b1, filt_w2, filt_w3,
              long_bias, tail_gain, tail_rate, out_weight, norm2_gain, up_weight, down_weight, grad_out):
    rows, width = tokens.shape
    full, block = 2 * width, rows // 2
    n = lax.axis_size("seq")
    devices = 2 * n
    me = 2 * lax.axis_index("seq") + lax.axis_index("ch")
    row_start = me * block
    total_rows = seg_ids.shape[0]
    length = min(SEQ_LEN, total_rows)

    keys = seg_ids + (jnp.arange(total_rows, dtype=jnp.int32) // length) * 65536
    padded = jnp.concatenate([jnp.full((BEFORE,), -1, jnp.int32), keys, jnp.full((block + AFTER,), -2, jnp.int32)])
    near = lax.dynamic_slice_in_dim(padded, row_start, BEFORE + 2 * block)
    window = near[: BEFORE + block + AFTER]
    ids_s = jnp.concatenate([window, jnp.full((8,), 1, jnp.int32) * near[BEFORE + 2 * block - 1]])
    ids = jnp.broadcast_to(window.astype(F32)[:, None], (window.shape[0], LANES))

    channel_start = lax.axis_index("ch") * width
    pos_table = position_table(FIR, (filt_w1.shape[0] - 1) // 2)
    pre_one = jnp.dot(pos_table, filt_w1, precision=HIGHEST) + filt_b1
    hidden_one = jnp.sin(pre_one)
    pre_two = jnp.dot(hidden_one, filt_w2, precision=HIGHEST)
    hidden_two = jnp.sin(pre_two)
    channel = channel_start.astype(F32) + jnp.arange(width, dtype=F32)
    window_of = lambda channels: jnp.exp(
        -(0.5 + 3.0 * channels / full)[None, :] * jnp.arange(FIR, dtype=F32)[:, None] / FIR)
    taps = jnp.dot(hidden_two, filt_w3, precision=HIGHEST) * window_of(channel)
    norm_tail = jnp.sqrt(-jnp.expm1(-2.0 * tail_rate))
    rows_of = [norm1_gain, norm2_gain, long_bias, tail_gain, tail_rate, norm_tail]
    rows_of += [short_weight[j, s] for j in range(3) for s in range(3)]
    row_index = jnp.arange(HEAD)[:, None]
    head = jnp.zeros((HEAD, width), F32)
    for k, row in enumerate(rows_of):
        head = jnp.where(row_index == k, row[None, :], head)

    tok, g, win, wout, wup, wdn, vec = exchange(
        n, tokens, grad_out, jnp.transpose(in_weight, (1, 0, 2)), out_weight, up_weight, down_weight, head, taps, filt_w3)
    rate, gain, nu = vec[4], vec[3], vec[5]

    n1, proj, v, x0, x1, u, base, car, end = mixer(ids_s, tok, win, vec, ids)

    summed = n == 16 and full % (16 * 16) == 0
    firsts, lasts = keys[::block], keys[block - 1 :: block]
    reach = min(DOC_MOST // block, devices - 1)
    order = jnp.arange(reach)
    source = jnp.clip(me - 1 - order, 0, devices - 1)
    valid = (me - 1 - order >= 0) & (lasts[source] == lasts[jnp.clip(me - 1, 0, devices - 1)])
    weights = jnp.where(valid[:, None], jnp.exp(-rate[None, :] * (block * order.astype(F32))[:, None]), 0.0)
    (enter,) = push(n, end, weights[None], False, 1)

    out, long, car, gmid, gmix, gw_out, gw_up, gw_dn, gain_two = ffn(summed, tok, x0, base, car, ids, enter, g, vec, wout, wup, wdn)

    glong, q, first, halo, sums = gate(gmix, x0, x1, v, long, car, u, vec, ids)
    reach = min(DOC_MOST // block + 1, devices - 1)
    order = jnp.arange(reach)
    source = jnp.clip(me + 1 + order, 0, devices - 1)
    weights = []
    for later in range(2):
        valid = (me + 1 + order < devices) & (order >= later) & (
            firsts[source] == lasts[jnp.clip(me + later, 0, devices - 1)])
        distance = (block * (order - later) + 1).astype(F32)
        weights.append(jnp.where(valid[:, None], jnp.exp(-rate[None, :] * jnp.maximum(distance, 0.0)[:, None]), 0.0))
    joined, halo = push(n, first, jnp.stack(weights), True, 2, halo)

    gw_in, gtok, sums_two, gain_one = back(
        ids_s, glong, q, halo, joined, gmix, long, car, x1, v, u, proj, vec, ids, n1, win, tok, gmid)

    small = jnp.concatenate([sums_two[:42], sums, gain_one, gain_two, jnp.zeros((2, full), F32)])
    hidden = up_weight.shape[1]
    if summed:
        total, small, out, gtok = reduce(n, gw_in, gw_out, small, out, gtok)
    else:
        total, small, out, gtok = reduce_plain(n, gw_in, gw_out, gw_up, gw_dn, small, out, gtok)
        gw_up, gw_dn = total[:, 4 * width : 4 * width + hidden], total[:, 4 * width + hidden :]

    taps_grad, short_grad = small[:FIR], small[FIR : FIR + 9].reshape(3, 3, full)
    carried_q, bias_grad, long_car = small[41], small[42], small[43]
    factor = jnp.exp(-rate)
    rate_grad = gain * long_car * factor * factor / nu - carried_q
    raw_grad = taps_grad * window_of(jnp.arange(full, dtype=F32))
    w3_grad = jnp.dot(hidden_two.T, raw_grad, precision=HIGHEST)
    pre_two_grad = jnp.dot(raw_grad, vec[48:].T, precision=HIGHEST) * jnp.cos(pre_two)
    w2_grad = jnp.dot(hidden_one.T, pre_two_grad, precision=HIGHEST)
    pre_one_grad = jnp.dot(pre_two_grad, filt_w2.T, precision=HIGHEST) * jnp.cos(pre_one)
    w1_grad = jnp.dot(pos_table.T, pre_one_grad, precision=HIGHEST)
    in_grad = jnp.stack([total[:, k * width : (k + 1) * width] for k in range(3)], axis=1)
    return (
        out,
        gtok,
        small[44],
        in_grad,
        short_grad,
        w1_grad,
        jnp.sum(pre_one_grad, axis=0),
        w2_grad,
        w3_grad,
        bias_grad,
        nu * long_car,
        rate_grad,
        total[:, 3 * width : 4 * width].T,
        small[45],
        gw_up,
        gw_dn.T,
    )


def solution(mesh):
    placed = (
        P("seq", "ch"),
        P(),
        P("ch"),
        P(None, None, "ch"),
        P(None, None, "ch"),
        P(),
        P(),
        P(),
        P(None, "ch"),
        P("ch"),
        P("ch"),
        P("ch"),
        P("ch", None),
        P("ch"),
        P(None, "ch"),
        P("ch", None),
        P("seq", "ch"),
    )
    return jax.shard_map(
        on_device,
        mesh=mesh,
        in_specs=placed,
        out_specs=(
            P("seq", "ch"),
            P("seq", "ch"),
            P(),
            P("seq", None, "ch"),
            P(),
            P(),
            P(),
            P(),
            P(),
            P(),
            P(),
            P(),
            P("ch", "seq"),
            P(),
            P("seq", "ch"),
            P("ch", "seq"),
        ),
        check_vma=False,
    )
```

profile of v0, /device:TPU:0, one launch (start us, length us, event | category | flops | bytes accessed | tf_op | source)
XLA Modules:
  0.0 271.4 jit_solution(7132481760903958544)
XLA Ops:
  0.6 0.0 copy-start
  0.7 0.9 slice_reduce_fusion.15
  1.6 0.7 negate_sqrt_fusion
  2.4 1.5 select_select_fusion.head
  3.9 0.1 multiply_cosine_fusion
  4.0 1.0 fusion.20
  5.1 0.0 copy-done
  5.1 0.2 fusion.21
  5.3 1.7 convolution_multiply_fusion.taps
  7.0 0.0 copy-start.6
  7.0 0.0 copy-start.9
  7.0 21.3 %exchange.1 = (bf16[560,768]{1,0:T(8,128)(2,1)}, bf16[512,768]{1,0:T(8,128)(2,1)}, bf16[3,768,768]{2,1,0:T(8,128)(2,1)}, bf16[768,768]{1,0:T(8,128)(2,1)}, bf16[...) custom-call(bf16[1024,384]{1,0:T(8,128)(2,1)} %tokens.1, bf16[1024,384]{1,0:T(8,128)(2,1)} %gout.1, ...), custom_call_target="tpu_custom_call" | custom-call | tf_op jit(solution)/shard_map/exchange/pallas_call | solution.py:152
  28.3 0.0 copy-done.6
  28.4 0.1 concatenate.12
  28.5 0.6 dynamic-slice.1
  29.1 0.0 copy-done.9
  29.1 1.3 dynamic-slice_select_fusion.ids_s
  30.4 0.1 dynamic-slice_convert_fusion
  30.5 0.9 broadcast_in_dim.289.ids
  31.4 24.9 %mixer.1 = (bf16[512,768]{1,0:T(8,128)(2,1)}, bf16[3,560,768]{2,1,0:T(8,128)(2,1)}, f32[512,768]{1,0:T(8,128)}, f32[512,768]{1,0:T(8,128)}, f32[512,768]{1,0:T(8...) custom-call(s32[648]{0:T(1024)} %dynamic-slice_select_fusion.ids_s, ...), custom_call_target="tpu_custom_call" | custom-call | tf_op jit(solution)/shard_map/mixer/pallas_call | solution.py:308
  56.2 0.9 slice_reduce_fusion.2
  57.1 0.1 slice.102
  57.2 0.6 fusion.19
  57.9 0.7 gather_fusion
  58.5 0.7 compare_and_fusion.2
  59.2 0.7 exponential_select_fusion.2.refs_1_
  59.9 6.2 %push_on.1.enter = f32[1,768]{1,0:T(1,128)} custom-call(f32[1,768]{1,0:T(1,128)} %get-tuple-element.62.refs_0_, f32[1,16,768]{2,1,0:T(8,128)} %exponential_select_fusion.2.refs_1_), custom_call_target="tpu_custom_call" | custom-call | tf_op jit(solution)/shard_map/push_on/pallas_call | solution.py:433
  66.2 79.4 %ffn.1 = (f32[512,768]{1,0:T(8,128)}, f32[512,768]{1,0:T(8,128)}, f32[512,768]{1,0:T(8,128)}, f32[512,768]{1,0:T(8,128)}, f32[512,768]{1,0:T(8,128)}, /*index=5*...) custom-call(bf16[560,768]{1,0:T(8,128)(2,1)} %get-tuple-element.56.tok, ...), custom_call_target="tpu_custom_call" | custom-call | tf_op jit(solution)/shard_map/ffn/pallas_call | solution.py:678
  145.6 8.3 %gate.1 = (f32[512,768]{1,0:T(8,128)}, f32[512,768]{1,0:T(8,128)}, f32[1,768]{1,0:T(1,128)}, f32[80,768]{1,0:T(8,128)}, f32[2,768]{1,0:T(2,128)}) custom-call(f32[512,768]{1,0:T(8,128)} %get-tuple-element.67.gmix, f32[512,768]{1,0:T(8,128)} %get-tuple-element.59.x0, f32[512,768]{1,0:T(8,128)} %get-tuple-element.68.x1, f32[512,768]{1,0:T(8,128)} %get-tuple-element.69.v, ...), custom_call_target="tpu_custom_call" | custom-call | tf_op jit(solution)/shard_map/gate/pallas_call | solution.py:766
  153.9 0.1 slice.104
  154.0 0.7 gather_fusion.1
  154.7 1.3 compare_and_fusion.1
  156.1 0.1 exponential_select_fusion.1
  156.2 0.7 pad_maximum_fusion.1.refs_2_
  156.8 11.6 %push_back.1 = (f32[2,768]{1,0:T(2,128)}, f32[80,768]{1,0:T(8,128)}) custom-call(f32[1,768]{1,0:T(1,128)} %get-tuple-element.75.refs_0_, f32[80,768]{1,0:T(8,128)} %get-tuple-element.76.refs_1_, f32[2,17,768]{2,1,0:T(8,128)} %pad_maximum_fusion.1.refs_2_), custom_call_target="tpu_custom_call" | custom-call | tf_op jit(solution)/shard_map/push_back/pallas_call | solution.py:433
  168.5 0.0 copy-start.7
  168.5 0.0 copy-start.8
  168.5 29.7 %back.1 = (bf16[3,768,768]{2,1,0:T(8,128)(2,1)}, f32[512,768]{1,0:T(8,128)}, f32[48,768]{1,0:T(8,128)}, f32[1,768]{1,0:T(1,128)}) custom-call(s32[648]{0:T(1024)} %dynamic-slice_select_fusion.ids_s, f32[512,768]{1,0:T(8,128)} %get-tuple-element.73.glong, f32[512,768]{1,0:T(8,128)} %get-tuple-element.74.q, f32[80,768]{1,0:T(8,128)} %get-tuple-element.77.halo, ...), custom_call_target="tpu_custom_call" | custom-call | tf_op jit(solution)/shard_map/back/pallas_call | solution.py:931
  198.2 0.0 copy-done.7
  198.2 0.0 copy-done.8
  198.2 3.0 %concatenate.15.small = f32[48,768]{1,0:T(8,128)} concatenate(f32[42,768]{1,0:T(8,128)} %bitcast.36, f32[2,768]{1,0:T(2,128)S(1)} %copy-done.7, f32[1,768]{1,0:T(1,128)} %get-tuple-element.86, f32[1,768]{1,0:T(1,128)S(1)} %copy-done.8, f32[2,768]{1,0:T(2,128)S(1)} %broadcast_in_dim.295), dimensions={0} | concatenate | bytes 294912 | tf_op jit(solution)/shard_map/concatenate | solution.py:1202
  201.2 0.0 copy-start.1
  201.2 54.1 %reduce.37 = (f32[48,1536]{1,0:T(8,128)}, f32[48,768]{1,0:T(8,128)}, f32[1024,384]{1,0:T(8,128)}, f32[1024,384]{1,0:T(8,128)}) custom-call(bf16[3,16,48,768]{3,2,1,0:T(8,128)(2,1)} %bitcast.32, bf16[16,48,768]{2,1,0:T(8,128)(2,1)} %bitcast.34, f32[48,768]{1,0:T(8,128)} %concatenate.15.small, f32[512,768]{1,0:T(8,128)} %get-tuple-element.88.out, ...), custom_call_target="tpu_custom_call" | custom-call | tf_op jit(solution)/shard_map/reduce/pallas_call | solution.py:1090
  255.3 0.0 copy-start.3
  255.3 1.6 slice_reduce_fusion
  256.9 0.6 fusion.12
  257.5 0.0 copy-done.1
  257.5 1.2 convolution_multiply_fusion.2
  258.6 0.9 fusion.23
  259.5 0.7 fusion.22
  260.2 0.9 fusion.18
  261.1 1.6 slice_bitcast_fusion
  262.8 0.7 pad_maximum_fusion
  263.5 1.9 fusion.1
  265.4 0.8 slice.110
  266.2 0.6 reshape.464
  266.8 0.0 copy-done.3
  266.8 1.1 copy.37
  268.0 0.8 copy-done.2
  268.8 1.1 copy.38
  270.0 0.0 copy-done.5
  270.0 0.7 copy.39
  270.7 0.0 copy-done.4
  270.7 0.7 copy.40
  (26 shorter events, 0.2 us)
Async XLA Ops:
  0.6 4.4 %copy-start = (f32[64,64]{1,0:T(8,128)S(1)}, f32[64,64]{1,0:T(8,128)}, u32[]{:S(2)}) copy-start(f32[64,64]{1,0:T(8,128)} %param.24) | copy-start | bytes 49156
  7.0 21.3 %copy-start.6 = (s32[16384]{0:T(1024)S(1)}, s32[16384]{0:T(1024)}, u32[]{:S(2)}) copy-start(s32[16384]{0:T(1024)} %param.18) | copy-start | bytes 196612
  7.0 22.1 %copy-start.9 = (pred[648]{0:T(1024)(128)(4,1)S(1)}, pred[648]{0:T(1024)(128)(4,1)}, u32[]{:S(2)}) copy-start(pred[648]{0:T(1024)(128)(4,1)} %constant.35.clone.1) | copy-start | bytes 1948
  168.5 29.7 %copy-start.7 = (f32[2,768]{1,0:T(2,128)S(1)}, f32[2,768]{1,0:T(2,128)}, u32[]{:S(2)}) copy-start(f32[2,768]{1,0:T(2,128)} %get-tuple-element.85) | copy-start | bytes 18436
  168.5 29.7 %copy-start.8 = (f32[1,768]{1,0:T(1,128)S(1)}, f32[1,768]{1,0:T(1,128)}, u32[]{:S(2)}) copy-start(f32[1,768]{1,0:T(1,128)} %get-tuple-element.87) | copy-start | bytes 9220
  201.2 56.3 %copy-start.1 = (f32[112,768]{1,0:T(8,128)S(1)}, f32[112,768]{1,0:T(8,128)}, u32[]{:S(2)}) copy-start(f32[112,768]{1,0:T(8,128)} %get-tuple-element.58.vec.vblk) | copy-start | bytes 1032196
  255.3 11.6 %copy-start.3 = (f32[1024,384]{1,0:T(8,128)S(1)}, f32[1024,384]{1,0:T(8,128)}, u32[]{:S(2)}) copy-start(f32[1024,384]{1,0:T(8,128)} %get-tuple-element.167) | copy-start | bytes 4718596
  266.8 2.0 copy-start.2
  268.8 1.1 copy-start.5
  268.8 1.9 copy-start.4
where the time goes:
time: 273 us; the launch traced here: 271 us
  Pallas kernels  236 us (86%)
  local copies, waits for them, and re-layouts  16.8 us (6%)
  other arithmetic  9.51 us (3%)
  matrix products  8.49 us (3%)
    pallas_call x1, Pallas kernels, ffn(): pl.pallas_call(functools.partial(ffn_kernel, block, tiles, summed), name=...  79.4 us
    pallas_call x1, Pallas kernels, reduce(): pl.pallas_call(functools.partial(reduce_kernel, (n, width, block)), name=...  54.1 us
    pallas_call x1, Pallas kernels, back(): pl.pallas_call(functools.partial(back_kernel, block, steps), name='back',...  29.7 us
    pallas_call x1, Pallas kernels, mixer(): pl.pallas_call(functools.partial(mixer_kernel, block), name='mixer', grid...  24.9 us
    pallas_call x1, Pallas kernels, exchange(): pl.pallas_call(functools.partial(exchange_kernel, (n, rows, width, hidden...  21.3 us
    pallas_call x2, Pallas kernels, push(): pl.pallas_call(functools.partial(push_kernel, n, reach, backward, halo is...  17.9 us
    pallas_call x1, Pallas kernels, gate(): pl.pallas_call(functools.partial(gate_kernel, block), name='gate', grid=(...  8.34 us

commit v1 on v0

v1 whole, which is shorter than its diff:
```python
import functools

import jax
import jax.numpy as jnp
from jax import lax
from jax.experimental import pallas as pl
from jax.experimental.pallas import tpu as pltpu
from jax.sharding import PartitionSpec as P

FIR = 32
SEQ_LEN = 16384
DOC_MOST = 8192
EPSILON = 1e-05
FREQUENCY = 0.4
HIGHEST = lax.Precision.HIGHEST
MESH = pl.DeviceIdType.MESH
F32, BF16 = jnp.float32, jnp.bfloat16

BEFORE = 48
AFTER = 80
LANES = 128
BLOCK = 256
CHUNK = 64
SUMS = 48
HEAD = 16
VMEM_LIMIT = 56 << 20
ROOT_TWO_OVER_PI = 0.7978845608028654


def position_table(filter_len, band_count):
    places = jnp.arange(filter_len, dtype=F32)
    harmonics = jnp.arange(1, band_count + 1, dtype=F32)
    angles = FREQUENCY * places[:, None] * harmonics[None, :]
    return jnp.concatenate([places[:, None] / filter_len, jnp.cos(angles), jnp.sin(angles)], axis=1)


def of(ref, start, size):
    return pl.ds(pl.multiple_of(start, size), size)


def exchange_kernel(sizes, tokens, gout, w_in, w_out, w_up, w_down, gains, head, taps,
                    tok_o, g_o, in_o, out_o, up_o, down_o, gains_o, vec_o, local_sem, send_sem, recv_sem):
    n, rows, width, hidden = sizes
    block = rows // 2
    s, c = lax.axis_index("seq"), lax.axis_index("ch")
    barrier = pltpu.get_barrier_semaphore()
    pl.semaphore_signal(barrier, inc=1, device_id=(s, 1 - c), device_id_type=MESH)

    @pl.when((c == 0) & (s > 0))
    def _():
        for k in range(2):
            pl.semaphore_signal(barrier, inc=1, device_id=(s - 1, k), device_id_type=MESH)

    @pl.when(s < n - 1)
    def _():
        pl.semaphore_wait(barrier, 2)

    @pl.when(s == n - 1)
    def _():
        pl.semaphore_wait(barrier, 1)

    cols = pl.ds(pl.multiple_of(c * width, width), width)
    hid = pl.ds(pl.multiple_of(c * hidden, hidden), hidden)
    pairs = [
        (gains, gains_o.at[:, cols]),
        (w_up, up_o.at[:, hid]),
        (w_down, down_o.at[hid, :]),
    ]
    for i in range(width // LANES):
        source = pl.ds(i * LANES, LANES)
        paired = pl.ds(pl.multiple_of((2 * i + c) * LANES, LANES), LANES)
        pairs += [
            (w_in.at[:, :, source], in_o.at[:, :, paired]),
            (w_out.at[source, :], out_o.at[paired, :]),
            (head.at[:, source], vec_o.at[pl.ds(0, HEAD), paired]),
            (taps.at[:, source], vec_o.at[pl.ds(HEAD, FIR), paired]),
        ]

    def remote(src, dst, k, target):
        return pltpu.make_async_remote_copy(
            src_ref=src, dst_ref=dst, send_sem=send_sem.at[k], recv_sem=recv_sem.at[k],
            device_id=target, device_id_type=MESH)

    partner = (s, 1 - c)
    left, right = pl.ds(0, width), pl.ds(width, width)
    first, second = pl.ds(0, block), pl.ds(block, block)
    early = pl.ds(block - BEFORE, block + BEFORE)
    tail = pl.ds(rows - BEFORE, BEFORE)

    @pl.when(c == 0)
    def _():
        remote(tokens.at[early, :], tok_o.at[:, left], 0, partner).start()
        remote(gout.at[second, :], g_o.at[:, left], 1, partner).start()
        pltpu.make_async_copy(tokens.at[first, :], tok_o.at[pl.ds(BEFORE, block), left], local_sem.at[0]).start()
        pltpu.make_async_copy(gout.at[first, :], g_o.at[:, left], local_sem.at[1]).start()

        @pl.when(s < n - 1)
        def _():
            remote(tokens.at[tail, :], tok_o.at[pl.ds(0, BEFORE), left], 2, (s + 1, 0)).start()

    @pl.when(c == 1)
    def _():
        remote(tokens.at[first, :], tok_o.at[pl.ds(BEFORE, block), right], 0, partner).start()
        remote(gout.at[first, :], g_o.at[:, right], 1, partner).start()
        pltpu.make_async_copy(tokens.at[early, :], tok_o.at[:, right], local_sem.at[0]).start()
        pltpu.make_async_copy(gout.at[second, :], g_o.at[:, right], local_sem.at[1]).start()

        @pl.when(s < n - 1)
        def _():
            remote(tokens.at[tail, :], tok_o.at[pl.ds(0, BEFORE), right], 3, (s + 1, 0)).start()

    for k, (src, dst) in enumerate(pairs):
        remote(src, dst, 4 + k, partner).start()
        pltpu.make_async_copy(src, dst, local_sem.at[2 + k]).start()

    for k, (src, dst) in enumerate(pairs):
        pltpu.make_async_copy(src, dst, local_sem.at[2 + k]).wait()
        remote(src, dst, 4 + k, partner).wait()

    @pl.when(c == 0)
    def _():
        remote(tokens.at[early, :], tok_o.at[:, left], 0, partner).wait_send()
        remote(gout.at[second, :], g_o.at[:, left], 1, partner).wait_send()
        remote(tokens.at[first, :], tok_o.at[pl.ds(BEFORE, block), right], 0, partner).wait_recv()
        remote(gout.at[first, :], g_o.at[:, right], 1, partner).wait_recv()
        pltpu.make_async_copy(tokens.at[first, :], tok_o.at[pl.ds(BEFORE, block), left], local_sem.at[0]).wait()
        pltpu.make_async_copy(gout.at[first, :], g_o.at[:, left], local_sem.at[1]).wait()

        @pl.when(s < n - 1)
        def _():
            remote(tokens.at[tail, :], tok_o.at[pl.ds(0, BEFORE), left], 2, (s + 1, 0)).wait_send()

        @pl.when(s > 0)
        def _():
            remote(tokens.at[tail, :], tok_o.at[pl.ds(0, BEFORE), left], 2, partner).wait_recv()
            remote(tokens.at[tail, :], tok_o.at[pl.ds(0, BEFORE), right], 3, partner).wait_recv()

    @pl.when(c == 1)
    def _():
        remote(tokens.at[first, :], tok_o.at[pl.ds(BEFORE, block), right], 0, partner).wait_send()
        remote(gout.at[first, :], g_o.at[:, right], 1, partner).wait_send()
        remote(tokens.at[early, :], tok_o.at[:, left], 0, partner).wait_recv()
        remote(gout.at[second, :], g_o.at[:, left], 1, partner).wait_recv()
        pltpu.make_async_copy(tokens.at[early, :], tok_o.at[:, right], local_sem.at[0]).wait()
        pltpu.make_async_copy(gout.at[second, :], g_o.at[:, right], local_sem.at[1]).wait()

        @pl.when(s < n - 1)
        def _():
            remote(tokens.at[tail, :], tok_o.at[pl.ds(0, BEFORE), right], 3, (s + 1, 0)).wait_send()


def exchange(n, tokens, gout, w_in, w_out, w_up, w_down, *vec):
    rows, width = tokens.shape
    hidden = w_up.shape[1]
    full, block = 2 * width, rows // 2
    pieces = 3 + 4 * (width // LANES)
    anywhere = pl.BlockSpec(memory_space=pl.ANY)
    return pl.pallas_call(
        functools.partial(exchange_kernel, (n, rows, width, hidden)),
        name="exchange",
        out_shape=(
            jax.ShapeDtypeStruct((BEFORE + block, full), BF16),
            jax.ShapeDtypeStruct((block, full), BF16),
            jax.ShapeDtypeStruct((3, full, full), BF16),
            jax.ShapeDtypeStruct((full, full), BF16),
            jax.ShapeDtypeStruct((full, 2 * hidden), BF16),
            jax.ShapeDtypeStruct((2 * hidden, full), BF16),
            jax.ShapeDtypeStruct((vec[0].shape[0], full), F32),
            jax.ShapeDtypeStruct((HEAD + FIR, full), F32),
        ),
        in_specs=[anywhere] * 9,
        out_specs=[pl.BlockSpec(memory_space=pltpu.VMEM)] * 8,
        scratch_shapes=[pltpu.SemaphoreType.DMA((2 + pieces,))] + [pltpu.SemaphoreType.DMA((4 + pieces,))] * 2,
        compiler_params=pltpu.CompilerParams(collective_id=0, has_side_effects=True, vmem_limit_bytes=VMEM_LIMIT),
    )(tokens, gout, w_in, w_out, w_up, w_down, *vec)


def row_stats(values):
    center = jnp.mean(values, axis=1, keepdims=True)
    shifted = values - center
    inverse = lax.rsqrt(jnp.mean(shifted * shifted, axis=1, keepdims=True) + EPSILON)
    return shifted * inverse, inverse


def mixer_kernel(block, ids_s, tok, win, gains, vblk, ids, n1_o, proj_o, x0_o, u_o, long_o, car_o, end_o, heads_o,
                 n1_s, proj_s, state_s):
    rows = BEFORE + block
    lane_blocks = BLOCK // LANES

    @pl.when(pl.program_id(0) == 0)
    def _():
        gain = gains[0:1, :]

        def normed(j, _):
            at = pl.ds(pl.multiple_of(j * 16, 16), 16)
            values = jnp.where(ids[at, 0:1] >= 0.0, tok[at, :].astype(F32), 0.0)
            n1_s[at, :] = (row_stats(values)[0] * gain).astype(BF16)
            return 0

        lax.fori_loop(0, rows // 16, normed, 0)
        n1_o[...] = n1_s[pl.ds(BEFORE, block), :]

    for s in range(3):
        part = jnp.dot(n1_s[...], win[s], preferred_element_type=F32).astype(BF16)
        for b in range(lane_blocks):
            proj_o[s, b] = part[:, b * LANES : (b + 1) * LANES]
            proj_s[s, b] = part[:, b * LANES : (b + 1) * LANES].astype(F32)

    def convolved(start, size):
        own = ids[pl.ds(start, size), :]
        same = [None] + [own == ids[pl.ds(start - j, size), :] for j in (1, 2)]
        results = []
        for b in range(lane_blocks):
            lanes = slice(b * LANES, (b + 1) * LANES)
            streams = []
            for s in range(3):
                value = vblk[6 + s : 7 + s, lanes] * proj_s[s, b, pl.ds(start, size), :]
                for j in (1, 2):
                    tap = vblk[6 + 3 * j + s : 7 + 3 * j + s, lanes]
                    value += jnp.where(same[j], tap * proj_s[s, b, pl.ds(start - j, size), :], 0.0)
                streams.append(value)
            u_o[b, pl.ds(start, size), :] = (streams[0] * streams[2]).astype(BF16).astype(F32)
            results.append(streams)
        return results

    convolved(16, 32)
    for b, streams in enumerate(convolved(BEFORE, 8)):
        heads_o[0:8, b * LANES : (b + 1) * LANES] = streams[2]
        heads_o[8:16, b * LANES : (b + 1) * LANES] = streams[0]
    for b in range(lane_blocks):
        u_o[b, 0:16, :] = jnp.zeros((16, LANES), F32)

    def conv_chunk(j, _):
        start = pl.multiple_of(BEFORE + j * 32, 16)
        for b, streams in enumerate(convolved(start, 32)):
            x0_o[b, pl.ds(pl.multiple_of(j * 32, 32), 32), :] = streams[1]
        return 0

    lax.fori_loop(0, block // 32, conv_chunk, 0)

    row_id = lax.broadcasted_iota(jnp.int32, (8, LANES), 0)
    rates = [vblk[4:5, b * LANES : (b + 1) * LANES] for b in range(lane_blocks)]
    powers = [jnp.exp(-rate * (row_id + 1).astype(F32)) for rate in rates]
    lams = [[jnp.exp(-rate * float(step)) for step in (1, 2, 4)] for rate in rates]
    for b in range(lane_blocks):
        state_s[b, 0:8, :] = jnp.zeros((8, LANES), F32)

    def scan_group(g, carry):
        start = pl.multiple_of(BEFORE + g * 8, 8)
        own = ids[pl.ds(start, 8), :]
        masks = [(own == ids[pl.ds(start - step, 8), :]) & (row_id >= step) for step in (1, 2, 4)]
        joined = own == jnp.broadcast_to(ids[pl.ds(start - 1, 1), :], (8, LANES))
        result = []
        for b in range(lane_blocks):
            value = u_o[b, pl.ds(start, 8), :]
            for mask, lam, step in zip(masks, lams[b], (1, 2, 4)):
                value += jnp.where(mask, lam * pltpu.roll(value, step, 0), 0.0)
            value += jnp.where(joined, powers[b] * carry[b], 0.0)
            state_s[b, pl.ds(pl.multiple_of(8 + g * 8, 8), 8), :] = value
            result.append(jnp.broadcast_to(value[7:8, :], (8, LANES)))
        return tuple(result)

    zero = jnp.zeros((8, LANES), F32)
    final = lax.fori_loop(0, block // 8, scan_group, (zero,) * lane_blocks, unroll=4)
    for b in range(lane_blocks):
        end_o[:, b * LANES : (b + 1) * LANES] = final[b][0:1, :]

    for b in range(lane_blocks):
        lanes = slice(b * LANES, (b + 1) * LANES)
        bias, gain, lam = vblk[2:3, lanes], vblk[3:4, lanes], lams[b][0]
        nu = vblk[5:6, lanes]

        def long_chunk(j, _):
            start = pl.multiple_of(BEFORE + j * CHUNK, 16)
            to = pl.ds(pl.multiple_of(j * CHUNK, CHUNK), CHUNK)
            own = ids[pl.ds(start, CHUNK), :]
            here = u_o[b, pl.ds(start, CHUNK), :]
            previous = state_s[b, pl.ds(7 + j * CHUNK, CHUNK), :]
            carried = jnp.where(own == ids[pl.ds(start - 1, CHUNK), :], lam * previous, 0.0)
            car_o[b, to, :] = carried
            base = bias * here + (gain * nu) * carried
            whole = ids_s[start + CHUNK - 1] == ids_s[start - FIR + 1]

            @pl.when(whole)
            def _():
                total = base
                for k in range(FIR):
                    total += vblk[16 + k : 17 + k, lanes] * u_o[b, pl.ds(start - k, CHUNK), :]
                long_o[b, to, :] = total

            @pl.when(jnp.logical_not(whole))
            def _():
                total = base
                for k in range(FIR):
                    term = vblk[16 + k : 17 + k, lanes] * u_o[b, pl.ds(start - k, CHUNK), :]
                    total += jnp.where(own == ids[pl.ds(start - k, CHUNK), :], term, 0.0)
                long_o[b, to, :] = total

            return 0

        lax.fori_loop(0, block // CHUNK, long_chunk, 0)


def mixer(ids_s, tok, win, gains, vec, ids):
    rows, full = tok.shape
    block = rows - BEFORE
    lane_blocks, lanes = BLOCK // LANES, full // LANES
    whole = lambda *shape: pl.BlockSpec(shape, lambda i: (0,) * len(shape))
    by_channel = lambda count: pl.BlockSpec((count, BLOCK), lambda i: (0, i))
    stacked = lambda count: pl.BlockSpec((lane_blocks, count, LANES), lambda i: (i, 0, 0))
    return pl.pallas_call(
        functools.partial(mixer_kernel, block),
        name="mixer",
        grid=(full // BLOCK,),
        out_shape=(
            jax.ShapeDtypeStruct((block, full), BF16),
            jax.ShapeDtypeStruct((3, lanes, rows, LANES), BF16),
            jax.ShapeDtypeStruct((lanes, block, LANES), F32),
            jax.ShapeDtypeStruct((lanes, rows, LANES), F32),
            jax.ShapeDtypeStruct((lanes, block, LANES), F32),
            jax.ShapeDtypeStruct((lanes, block, LANES), F32),
            jax.ShapeDtypeStruct((1, full), F32),
            jax.ShapeDtypeStruct((16, full), F32),
        ),
        in_specs=[
            pl.BlockSpec(memory_space=pltpu.SMEM),
            whole(rows, full),
            pl.BlockSpec((3, full, BLOCK), lambda i: (0, 0, i)),
            whole(*gains.shape),
            by_channel(vec.shape[0]),
            whole(*ids.shape),
        ],
        out_specs=(
            whole(block, full),
            pl.BlockSpec((3, lane_blocks, rows, LANES), lambda i: (0, i, 0, 0)),
            stacked(block),
            stacked(rows),
            stacked(block),
            stacked(block),
            by_channel(1),
            by_channel(16),
        ),
        scratch_shapes=[
            pltpu.VMEM((rows, full), BF16),
            pltpu.VMEM((3, lane_blocks, rows, LANES), F32),
            pltpu.VMEM((lane_blocks, 8 + block, LANES), F32),
        ],
        compiler_params=pltpu.CompilerParams(vmem_limit_bytes=VMEM_LIMIT),
    )(ids_s, tok, win, gains, vec, ids)


def device_of(index):
    return (index // 2, index % 2)


class Pushing:
    def __init__(self, n, reach, backward, source, slots, send_sem, recv_sem):
        self.total, self.reach = 2 * n, reach
        self.me = 2 * lax.axis_index("seq") + lax.axis_index("ch")
        self.ahead = -1 if backward else 1
        self.place = self.total - 1 - self.me if backward else self.me
        self.source, self.slots, self.send_sem, self.recv_sem = source, slots, send_sem, recv_sem

    def greet(self, barrier):
        for k in range(self.reach):

            @pl.when(self.place - 1 - k >= 0)
            def _():
                pl.semaphore_signal(
                    barrier, inc=1, device_id=device_of(self.me - self.ahead * (1 + k)), device_id_type=MESH)

    def await_greetings(self, barrier, others):
        following = self.total - 1 - self.place
        for count in range(0, self.reach + 1):
            if count + others:

                @pl.when((following >= count) if count == self.reach else (following == count))
                def _():
                    pl.semaphore_wait(barrier, count + others)

    def copy(self, k):
        return pltpu.make_async_remote_copy(
            src_ref=self.source, dst_ref=self.slots.at[k], send_sem=self.send_sem.at[k], recv_sem=self.recv_sem.at[k],
            device_id=device_of(self.me + self.ahead * (1 + k)), device_id_type=MESH)

    def start(self):
        for k in range(self.reach):

            @pl.when(self.place + 1 + k < self.total)
            def _():
                self.copy(k).start()

    def take(self, use):
        for k in range(self.reach):

            @pl.when(self.place - 1 - k >= 0)
            def _():
                self.copy(k).wait_recv()
                use(k, self.slots[k])

            @pl.when(self.place + 1 + k < self.total)
            def _():
                self.copy(k).wait_send()


def push_kernel(n, reach, block, marks, end, vec, enter_o, slots, send_sem, recv_sem):
    pushing = Pushing(n, reach, False, end, slots, send_sem, recv_sem)
    barrier = pltpu.get_barrier_semaphore()
    pushing.greet(barrier)
    pushing.await_greetings(barrier, 0)
    pushing.start()
    enter_o[...] = jnp.zeros_like(enter_o)
    rate = vec[4:5, :]
    last = marks[2 * n + jnp.maximum(pushing.me - 1, 0)]

    def use(k, state):
        same = jnp.where(marks[2 * n + pushing.me - 1 - k] == last, 1.0, 0.0)
        enter_o[...] += same * jnp.exp(-rate * float(block * k)) * state

    pushing.take(use)


def push(n, block, marks, end, vec):
    full = end.shape[1]
    reach = min(DOC_MOST // block, 2 * n - 1)
    vmem = pl.BlockSpec(memory_space=pltpu.VMEM)
    return pl.pallas_call(
        functools.partial(push_kernel, n, reach, block),
        name="push",
        out_shape=jax.ShapeDtypeStruct((1, full), F32),
        in_specs=[pl.BlockSpec(memory_space=pltpu.SMEM), vmem, vmem],
        out_specs=vmem,
        scratch_shapes=[
            pltpu.VMEM((reach, 1, full), F32), pltpu.SemaphoreType.DMA((reach,)), pltpu.SemaphoreType.DMA((reach,))],
        compiler_params=pltpu.CompilerParams(collective_id=1, has_side_effects=True),
    )(marks, end, vec)


TILE = 512
PART = TILE // 2
STAGES = 5


class Summing:
    def __init__(self, slots, rows, staged, first, second, third, fourth, fifth, send_sem, recv_sem):
        self.slots, self.rows, self.staged = slots, rows, staged
        self.first, self.second, self.third, self.fourth, self.fifth = first, second, third, fourth, fifth
        self.send_sem, self.recv_sem = send_sem, recv_sem
        self.s, self.c = lax.axis_index("seq"), lax.axis_index("ch")
        self.bits = [(self.s // (1 << b)) % 2 for b in range(4)]
        self.peers = [(self.s + (1 - 2 * bit) * (1 << b), self.c) for b, bit in enumerate(self.bits)]
        self.partner = (self.s, 1 - self.c)
        self.order = ((0, 1, 2, 3), (1, 0, 2, 3))

    @staticmethod
    def scratch(tiles, slots, rows):
        return [
            pltpu.VMEM((2, 2, 2, 2, 2, 2, rows, TILE), BF16),
            pltpu.VMEM((slots, 2, 2, 2, 2, rows, TILE), BF16),
            pltpu.VMEM((slots, 2, 2, 2, 2, rows, PART), BF16),
            pltpu.VMEM((slots, 2, 2, 2, rows, PART), BF16),
            pltpu.VMEM((slots, 2, 2, rows, PART), BF16),
            pltpu.VMEM((slots, 2, rows, PART), BF16),
            pltpu.SemaphoreType.DMA((tiles, 1 + 2 * 4)),
            pltpu.SemaphoreType.DMA((tiles, 1 + 2 * 4)),
        ]

    def greet(self, barrier):
        for peer in [self.partner] + self.peers:
            pl.semaphore_signal(barrier, inc=1, device_id=peer, device_id_type=MESH)

    def remote(self, src, dst, tile, k, target):
        return pltpu.make_async_remote_copy(
            src_ref=src, dst_ref=dst, send_sem=self.send_sem.at[tile, k], recv_sem=self.recv_sem.at[tile, k],
            device_id=target, device_id_type=MESH)

    def copies(self, tile, stage):
        slot = tile % self.slots
        if stage == 0:
            return [self.remote(self.staged.at[tile % 2, 1], self.first.at[slot], tile, 0, self.partner)]
        result = []
        for part in range(2):
            bit = self.order[part][stage - 1]
            away = 1 - self.bits[bit]
            at = pl.ds(part * PART, PART)
            if stage == 1:
                src = self.first.at[slot, :, :, :, away, :, at] if part == 0 else self.first.at[slot, :, :, away, :, :, at]
                dst = self.second.at[slot, part]
            elif stage == 2:
                src, dst = self.second.at[slot, part, :, :, away], self.third.at[slot, part]
            elif stage == 3:
                src, dst = self.third.at[slot, part, :, away], self.fourth.at[slot, part]
            else:
                src, dst = self.fourth.at[slot, part, away], self.fifth.at[slot, part]
            result.append(self.remote(src, dst, tile, 1 + 2 * (stage - 1) + part, self.peers[bit]))
        return result

    def start(self, tile, stage):
        for copy in self.copies(tile, stage):
            copy.start()

    def advance(self, tile, stage, total):
        for copy in self.copies(tile, stage):
            copy.wait()
        x, y, low, high = self.bits
        slot = tile % self.slots
        if stage == 0:
            def add(i, _):
                for h in range(2):
                    for j in range(2):
                        for k in range(2):
                            self.first[slot, h, i, j, k] += self.staged[tile % 2, 0, h, i, j, k]
                return 0
            lax.fori_loop(0, 2, add, 0)
        elif stage == 1:
            def add(i, _):
                for h in range(2):
                    for k in range(2):
                        self.second[slot, 0, h, i, k] += self.first[slot, h, i, k, x, :, 0:PART]
                        self.second[slot, 1, h, i, k] += self.first[slot, h, i, y, k, :, PART:TILE]
                return 0
            lax.fori_loop(0, 2, add, 0)
        elif stage == 2:
            for i in range(2):
                for k in range(2):
                    self.third[slot, 0, i, k] += self.second[slot, 0, i, k, y]
                    self.third[slot, 1, i, k] += self.second[slot, 1, i, k, x]
        elif stage == 3:
            for part in range(2):
                for i in range(2):
                    self.fourth[slot, part, i] += self.third[slot, part, i, low]
        else:
            for part in range(2):
                mine = self.fourth[slot, part, high].astype(F32)
                total(tile, part, mine + self.fifth[slot, part].astype(F32))
            return
        self.start(tile, stage + 1)


class Joining:
    def __init__(self, sums, held, arrived, send_sem, recv_sem):
        self.held, self.arrived, self.send_sem, self.recv_sem = held, arrived, send_sem, recv_sem
        self.targets = [sums.partner] + sums.peers

    @staticmethod
    def scratch(*shape):
        return [pltpu.VMEM((STAGES,) + shape, F32), pltpu.VMEM((STAGES,) + shape, F32),
                pltpu.SemaphoreType.DMA((STAGES,)), pltpu.SemaphoreType.DMA((STAGES,))]

    def copy(self, stage):
        return pltpu.make_async_remote_copy(
            src_ref=self.held.at[stage], dst_ref=self.arrived.at[stage], send_sem=self.send_sem.at[stage],
            recv_sem=self.recv_sem.at[stage], device_id=self.targets[stage], device_id_type=MESH)

    def start(self, stage):
        self.copy(stage).start()

    def advance(self, stage, result):
        self.copy(stage).wait()
        total = self.held[stage] + self.arrived[stage]
        if stage == STAGES - 1:
            result[...] = total
        else:
            self.held[stage + 1] = total
            self.start(stage + 1)


def contract(left, right, dims):
    return lax.dot_general(left, right, (dims, ((), ())), preferred_element_type=F32)


def contract(left, right, dims):
    return lax.dot_general(left, right, (dims, ((), ())), preferred_element_type=F32)


TILES = 6
EPILOGUE, GATE, TAPS, BACK = TILES, TILES + 1, TILES + 2, TILES + 3
HALO = 80


def backward_kernel(n, block, reach, summed, marks, tok, ids, enter, g, gains, vec, wout, x0, base, car, u, n1, heads,
                    wup_a, wup_b, wdn_a, wdn_b, win, proj, *refs):
    full = g.shape[1]
    width, lane_blocks = full // 2, full // LANES
    steps = full // BLOCK
    last_back = BACK + steps - 1
    outs, refs = refs[:6], refs[6:]
    if summed:
        part_a, part_b, small_a, small_b, out_full, gtok_full = outs
    else:
        grads_o, small_a, small_b, out_o, gtok_o, _ = outs
    (mixed_s, middle_s, n2_s, gn_s, gout_s, out_s, gmid_s, long_s, car_s, glong_s, q_s, gc_s, gp_s, proj_s,
     dist_s, rest_s, taps_s, first_s, slots_s, joined_s, halo_s, halo_r, head_s,
     push_send, push_recv, halo_sem, *buffers) = refs
    step = pl.program_id(0)
    groups = block // 32
    barrier = pltpu.get_barrier_semaphore()
    pushing = Pushing(n, reach, True, first_s, slots_s, push_send, push_recv)
    c = lax.axis_index("ch")
    lanes_of = lambda b: pl.ds(pl.multiple_of(b * LANES, LANES), LANES)
    if summed:
        sums = Summing(TILES, full // 16, *buffers[:8])
        joins = [(Joining(sums, *buffers[8:12]), small_a, TAPS), (Joining(sums, *buffers[12:16]), small_b, last_back)]
        local_sem, exchange_send, exchange_recv = buffers[16:]

        def shares(k, src, dst):
            at = pl.ds(pl.multiple_of(c * block, block), block)
            of_core = lambda which: src.at[:, pl.ds(pl.multiple_of(which * width, width), width)]
            return (
                pltpu.make_async_copy(of_core(c), dst.at[at, :], local_sem.at[k]),
                pltpu.make_async_remote_copy(
                    src_ref=of_core(1 - c), dst_ref=dst.at[at, :], send_sem=exchange_send.at[k],
                    recv_sem=exchange_recv.at[k], device_id=sums.partner, device_id_type=MESH),
            )

    halo_copy = pltpu.make_async_remote_copy(
        src_ref=halo_s, dst_ref=halo_r, send_sem=halo_sem.at[0], recv_sem=halo_sem.at[1],
        device_id=device_of(pushing.me - 1), device_id_type=MESH)

    @pl.when(step == 0)
    def _():
        pushing.greet(barrier)
        if summed:
            sums.greet(barrier)

        last = ids[pl.ds(BEFORE - 1, 1), :]
        for b in range(lane_blocks):
            lanes = slice(b * LANES, (b + 1) * LANES)
            rate, tail = vec[4:5, lanes], vec[3:4, lanes] * vec[5:6, lanes]
            state = enter[0:1, lanes]

            def mix(j, _):
                at = pl.ds(pl.multiple_of(j * 32, 32), 32)
                passed = (lax.broadcasted_iota(jnp.int32, (32, LANES), 0) + (j * 32 + 1)).astype(F32)
                same = ids[pl.ds(pl.multiple_of(BEFORE + j * 32, 16), 32), :] == last
                entered = jnp.where(same, jnp.exp(-rate * passed) * state, 0.0)
                car_s[b, at, :] = car[b, at, :] + entered
                long = base[b, at, :] + tail * entered
                long_s[b, at, :] = long
                mixed_s[at, lanes] = (long * x0[b, at, :]).astype(BF16)
                return 0

            lax.fori_loop(0, groups, mix, 0)
        middle_s[...] = jnp.dot(mixed_s[...], wout[...], preferred_element_type=F32)

        def norm(j, _):
            at = pl.ds(pl.multiple_of(j * 32, 32), 32)
            start = pl.multiple_of(BEFORE + j * 32, 16)
            values = middle_s[at, :] + tok[pl.ds(start, 32), :].astype(F32)
            middle_s[at, :] = values
            out_s[at, :] = values
            n2_s[at, :] = (row_stats(values)[0] * gains[1:2, :]).astype(BF16)
            gn_s[at, :] = jnp.zeros_like(values)
            own = ids[pl.ds(start, 32), :]
            before = after = jnp.zeros((32, LANES), F32)
            for k in range(1, FIR):
                before += jnp.where(own == ids[pl.ds(start - k, 32), :], 1.0, 0.0)
                after += jnp.where(own == ids[pl.ds(start + k, 32), :], 1.0, 0.0)
            dist_s[at, :] = before
            rest_s[at, :] = after
            return 0

        lax.fori_loop(0, groups, norm, 0)
        pushing.await_greetings(barrier, 5 if summed else 0)

    if summed:

        def total(tile, part, value):
            (part_a, part_b)[part][:, pl.ds(pl.multiple_of(tile * PART, PART), PART)] = value

        for stage in range(STAGES - 1, -1, -1):
            since = step - 1 - stage

            @pl.when(((since >= 0) & (since < TILES)) | ((since >= BACK) & (since <= last_back)))
            def _():
                sums.advance(since - (BACK - TILES) * (since // BACK), stage, total)

            for join, result, begun in joins:

                @pl.when(since == begun)
                def _():
                    join.advance(stage, result)

    def put(tile, start, grad):
        size = grad[0].shape[1]
        at = pl.ds(start, size)
        for half in range(2):
            if summed:
                whose = (half + c) % 2
                for q in range(16):
                    sums.staged[tile % 2, whose, q // 8, q // 4 % 2, q // 2 % 2, q % 2, :, at] = (
                        grad[half][q * sums.rows : (q + 1) * sums.rows])
            else:
                grads_o[0, half, :, at] = grad[half]

    @pl.when(step < TILES)
    def _():
        for half, (wup, wdn) in enumerate(((wup_a, wdn_a), (wup_b, wdn_b))):
            n2, rows = n2_s[...], g[...]
            up = jnp.dot(n2, wup[...], preferred_element_type=F32)
            pulled = contract(rows, wdn[...], ((1,), (1,)))
            square = up * up
            inner = ROOT_TWO_OVER_PI * up * (1.0 + 0.044715 * square)
            bent = jnp.tanh(inner)
            part = 0.5 * (1.0 + bent)
            active = (up * part).astype(BF16)
            slope = part + (0.5 * ROOT_TWO_OVER_PI) * up * (1.0 - bent * bent) * (1.0 + 0.134145 * square)
            g_up = (pulled * slope).astype(BF16)
            out_s[...] += jnp.dot(active, wdn[...], preferred_element_type=F32)
            gn_s[...] += contract(g_up, wup[...], ((1,), (1,)))
            pair = (contract(n2, g_up, ((0,), (0,))).astype(BF16), contract(rows, active, ((0,), (0,))).astype(BF16))
            for k in range(2):
                at = pl.ds(k * PART, PART)
                if summed:
                    whose = (half + c) % 2
                    for q in range(16):
                        sums.staged[step % 2, whose, q // 8, q // 4 % 2, q // 2 % 2, q % 2, :, at] = (
                            pair[k][q * sums.rows : (q + 1) * sums.rows])
                else:
                    grads_o[0, half, :, at] = pair[k]
        if summed:
            sums.start(step, 0)

    @pl.when(step == EPILOGUE)
    def _():
        if summed:
            for copy in shares(0, out_s, out_full):
                copy.start()
        else:
            out_o[...] = out_s[...]

        def back(j, total):
            at = pl.ds(pl.multiple_of(j * 32, 32), 32)
            normal, inverse = row_stats(middle_s[at, :])
            grad = gn_s[at, :]
            total += jnp.sum(grad * normal, axis=0, keepdims=True)
            scaled = grad * gains[1:2, :]
            cross = jnp.mean(scaled * normal, axis=1, keepdims=True)
            result = g[at, :].astype(F32) + inverse * (
                scaled - jnp.mean(scaled, axis=1, keepdims=True) - normal * cross)
            gmid_s[at, :] = result
            gout_s[at, :] = result.astype(BF16)
            gn_s[at, :] = jnp.zeros_like(grad)
            return total

        gain_two = lax.fori_loop(0, groups, back, jnp.zeros((1, full), F32))
        head_s[...] = jnp.zeros_like(head_s)
        head_s[0:1, :] = gain_two
        for i in range(steps):
            gmix = contract(gout_s[...], wout[i * BLOCK : (i + 1) * BLOCK, :], ((1,), (1,)))
            for k in range(BLOCK // LANES):
                b = i * (BLOCK // LANES) + k
                part = gmix[:, k * LANES : (k + 1) * LANES]
                glong_s[b, 0:block, :] = part * x0[b]
                long_s[b] = part * long_s[b]

    row_id = lax.broadcasted_iota(jnp.int32, (8, LANES), 0)
    zero = jnp.zeros((8, LANES), F32)

    @pl.when(step == GATE)
    def _():
        rates = [vec[4:5, b * LANES : (b + 1) * LANES] for b in range(lane_blocks)]
        tails = [vec[3:4, b * LANES : (b + 1) * LANES] * vec[5:6, b * LANES : (b + 1) * LANES] for b in range(lane_blocks)]
        lams = [[jnp.exp(-rate * float(k)) for k in (1, 2, 4)] for rate in rates]
        powers = [jnp.exp(-rate * (8 - row_id).astype(F32)) for rate in rates]

        def scan_group(i, carry):
            at = block // 8 - 1 - i
            to = pl.ds(pl.multiple_of(at * 8, 8), 8)
            start = pl.multiple_of(BEFORE + at * 8, 8)
            own = ids[pl.ds(start, 8), :]
            masks = [(own == ids[pl.ds(start + k, 8), :]) & (row_id < 8 - k) for k in (1, 2, 4)]
            joined = own == jnp.broadcast_to(ids[pl.ds(start + 8, 1), :], (8, LANES))
            states, biases, carries = [], [], []
            for b in range(lane_blocks):
                grad = glong_s[b, to, :]
                value = grad * tails[b]
                for mask, lam, k in zip(masks, lams[b], (1, 2, 4)):
                    value += jnp.where(mask, lam * pltpu.roll(value, 8 - k, 0), 0.0)
                value += jnp.where(joined, powers[b] * carry[0][b], 0.0)
                q_s[b, to, :] = value
                states.append(jnp.broadcast_to(value[0:1, :], (8, LANES)))
                biases.append(carry[1][b] + grad * u[b, pl.ds(start, 8), :])
                carries.append(carry[2][b] + grad * car_s[b, to, :])
            return tuple(states), tuple(biases), tuple(carries)

        many = (zero,) * lane_blocks
        states, biases, carries = lax.fori_loop(0, block // 8, scan_group, (many, many, many), unroll=2)
        for b in range(lane_blocks):
            lanes = slice(b * LANES, (b + 1) * LANES)
            first_s[:, lanes] = states[b][0:1, :]
            head_s[1:2, lanes] = jnp.sum(biases[b], axis=0, keepdims=True)
            head_s[2:3, lanes] = jnp.sum(carries[b], axis=0, keepdims=True)
            halo_s[0:48, lanes] = glong_s[b, 0:48, :]
            halo_s[48:56, lanes] = q_s[b, 0:8, :]
            halo_s[72:80, lanes] = long_s[b, 0:8, :]
        halo_s[56:72, :] = heads[...]
        pushing.start()

        @pl.when(pushing.me > 0)
        def _():
            halo_copy.start()

    @pl.when(step == TAPS)
    def _():
        taps_s[...] = jnp.zeros_like(taps_s)

        def pairs(p, _):
            def chunk(j, _):
                at = pl.ds(pl.multiple_of(j * 32, 32), 32)
                start = BEFORE + j * 32
                near = dist_s[at, :]
                here = [glong_s[2 * p + k, at, :] for k in range(2)]
                for tap in range(FIR):
                    same = near >= float(tap)
                    for k in range(2):
                        term = jnp.where(same, here[k] * u[2 * p + k, pl.ds(start - tap, 32), :], 0.0)
                        taps_s[2 * p + k, tap] += jnp.sum(term.reshape(4, 8, LANES), axis=0)
                return 0

            lax.fori_loop(0, groups, chunk, 0)
            return 0

        lax.fori_loop(0, lane_blocks // 2, pairs, 0)
        result = joins[0][0].held.at[0] if summed else small_a
        for b in range(lane_blocks):
            lanes = slice(b * LANES, (b + 1) * LANES)
            result[0:FIR, lanes] = jnp.sum(taps_s[b], axis=1)
        result[FIR : FIR + 8, :] = head_s[...]
        if summed:
            joins[0][0].start(0)

    @pl.when(step == BACK)
    def _():
        joined_s[...] = jnp.zeros_like(joined_s)
        rate = vec[4:5, :]
        following = 2 * n + jnp.minimum(pushing.me + 1, 2 * n - 1)
        lasts = (marks[2 * n + pushing.me], marks[following])

        def use(k, state):
            first = marks[pushing.me + 1 + k]
            for row in range(2):
                if k >= row:
                    same = jnp.where(first == lasts[row], 1.0, 0.0)
                    joined_s[row : row + 1, :] += same * jnp.exp(-rate * float(block * (k - row) + 1)) * state

        pushing.take(use)

        @pl.when(pushing.me > 0)
        def _():
            halo_copy.wait_send()

        @pl.when(pushing.me < 2 * n - 1)
        def _():
            halo_copy.wait_recv()

        for b in range(lane_blocks):
            glong_s[b, block : block + 48, :] = halo_r[0:48, b * LANES : (b + 1) * LANES]

    @pl.when((step >= BACK) & (step <= last_back))
    def _():
        i = step - BACK
        two = range(2)
        lanes = [lanes_of(2 * i + k) for k in two]
        rates = [vec[4:5, lanes[k]] for k in two]
        scales = [vec[2:3, lanes[k]] - vec[3:4, lanes[k]] * vec[5:6, lanes[k]] for k in two]
        mine = [joined_s[0:1, lanes[k]] for k in two]
        for k in two:
            for s in range(3):
                proj_s[s, k] = proj[s, k].astype(F32)
        last = ids[pl.ds(BEFORE + block - 1, 1), :]

        def conv_at(s, k, start, size, same):
            value = vec[6 + s : 7 + s, lanes[k]] * proj_s[s, k, pl.ds(start, size), :]
            for j in (1, 2):
                tap = vec[6 + 3 * j + s : 7 + 3 * j + s, lanes[k]]
                value += jnp.where(same[j - 1], tap * proj_s[s, k, pl.ds(start - j, size), :], 0.0)
            return value

        def chunk(j, totals):
            at = pl.ds(pl.multiple_of(j * 32, 32), 32)
            start = pl.multiple_of(BEFORE + j * 32, 16)
            own = ids[pl.ds(start, 32), :]
            left = (block - 1 - j * 32 - lax.broadcasted_iota(jnp.int32, (32, LANES), 0)).astype(F32)
            after = rest_s[at, :]
            near = dist_s[at, :]
            grads, result = [], []
            for k in two:
                b = 2 * i + k
                state = q_s[b, at, :] + jnp.where(own == last, jnp.exp(-rates[k] * left) * mine[k], 0.0)
                result.append(totals[k] + jnp.sum((car_s[b, at, :] * state).reshape(4, 8, LANES), axis=0))
                grads.append(scales[k] * glong_s[b, at, :] + state)
            for tap in range(FIR):
                same = after >= float(tap)
                for k in two:
                    term = vec[16 + tap : 17 + tap, lanes[k]] * glong_s[2 * i + k, pl.ds(j * 32 + tap, 32), :]
                    grads[k] += jnp.where(same, term, 0.0)
            same = [near >= 1.0, near >= 2.0]
            for k in two:
                gc_s[0, k, at, :] = grads[k] * conv_at(2, k, start, 32, same)
                gc_s[1, k, at, :] = long_s[2 * i + k, at, :]
                gc_s[2, k, at, :] = grads[k] * conv_at(0, k, start, 32, same)
            return tuple(result)

        crossed = lax.fori_loop(0, groups, chunk, (zero, zero))

        start = BEFORE + block
        own = ids[pl.ds(start, 8), :]
        end_id = marks[2 * n + jnp.minimum(pushing.me + 1, 2 * n - 1)].astype(F32)
        left = (block - 1 - row_id).astype(F32)
        for k in two:
            b = 2 * i + k
            entered = jnp.exp(-rates[k] * left) * joined_s[1:2, lanes[k]]
            grad = halo_r[48:56, lanes[k]] + jnp.where(own == end_id, entered, 0.0)
            grad += scales[k] * glong_s[b, block : block + 8, :]
            for tap in range(FIR):
                term = vec[16 + tap : 17 + tap, lanes[k]] * glong_s[b, block + tap : block + tap + 8, :]
                grad += jnp.where(own == ids[pl.ds(start + tap, 8), :], term, 0.0)
            gc_s[0, k, block : block + 8, :] = grad * halo_r[56:64, lanes[k]]
            gc_s[1, k, block : block + 8, :] = halo_r[72:80, lanes[k]]
            gc_s[2, k, block : block + 8, :] = grad * halo_r[64:72, lanes[k]]

        small = joins[1][0].held.at[0] if summed else small_b
        for k in two:

            def short(j, totals):
                at = pl.ds(pl.multiple_of(j * 32, 32), 32)
                start = pl.multiple_of(BEFORE + j * 32, 16)
                same = [dist_s[at, :] >= float(d) for d in (1, 2)]
                later = [rest_s[at, :] >= float(d) for d in (1, 2)]
                result = []
                for s in range(3):
                    here = gc_s[s, k, at, :]
                    value = vec[6 + s : 7 + s, lanes[k]] * here
                    for d in (1, 2):
                        tap = vec[6 + 3 * d + s : 7 + 3 * d + s, lanes[k]]
                        value += jnp.where(later[d - 1], tap * gc_s[s, k, pl.ds(j * 32 + d, 32), :], 0.0)
                    gp_s[s, at, k * LANES : (k + 1) * LANES] = value.astype(BF16)
                    for d in range(3):
                        term = here * proj_s[s, k, pl.ds(start - d, 32), :]
                        if d:
                            term = jnp.where(same[d - 1], term, 0.0)
                        result.append(totals[3 * s + d] + jnp.sum(term.reshape(4, 8, LANES), axis=0))
                return tuple(result)

            totals = lax.fori_loop(0, groups, short, (zero,) * 9)
            rows = [None] * 9
            for s in range(3):
                for d in range(3):
                    rows[3 * d + s] = jnp.sum(totals[3 * s + d], axis=0, keepdims=True)
            rows.append(jnp.sum(crossed[k], axis=0, keepdims=True))
            for row, value in enumerate(rows):
                small[row : row + 1, lanes[k]] = value

        tile = TILES + i
        pieces = []
        for s in range(3):
            part = gp_s[s]
            pieces.append(contract(n1[...], part, ((0,), (0,))).astype(BF16))
            gn_s[...] += contract(part, win[s], ((1,), (1,)))
        at = pl.ds(pl.multiple_of(i * BLOCK, BLOCK), BLOCK)
        pieces.append(contract(gout_s[...], mixed_s[:, at], ((0,), (0,))).astype(BF16))
        for s, piece in enumerate(pieces):
            put(tile, s * LANES, [piece[:, half * LANES : (half + 1) * LANES] for half in range(2)])
        if summed:
            sums.start(tile, 0)

    @pl.when(step == last_back)
    def _():
        def back(j, total):
            at = pl.ds(pl.multiple_of(j * 32, 32), 32)
            normal, inverse = row_stats(tok[pl.ds(pl.multiple_of(BEFORE + j * 32, 16), 32), :].astype(F32))
            grad = gn_s[at, :]
            total += jnp.sum(grad * normal, axis=0, keepdims=True)
            scaled = grad * gains[0:1, :]
            cross = jnp.mean(scaled * normal, axis=1, keepdims=True)
            middle_s[at, :] = gmid_s[at, :] + inverse * (
                scaled - jnp.mean(scaled, axis=1, keepdims=True) - normal * cross)
            return total

        gain_one = lax.fori_loop(0, groups, back, jnp.zeros((1, full), F32))
        small = joins[1][0].held.at[0] if summed else small_b
        small[10:11, :] = gain_one
        small[11:16, :] = jnp.zeros((5, full), F32)
        if summed:
            joins[1][0].start(0)
            for copy in shares(1, middle_s, gtok_full):
                copy.start()
        else:
            gtok_o[...] = middle_s[...]

    if summed:

        @pl.when(step == last_back + STAGES)
        def _():
            for k, (src, dst) in enumerate(((out_s, out_full), (middle_s, gtok_full))):
                for copy in shares(k, src, dst):
                    copy.wait()


def backward(n, summed, marks, tok, ids, enter, g, gains, vec, wout, x0, base, car, u, n1, heads, wup, wdn, win, proj):
    block, full = g.shape
    rows, lane_blocks = BEFORE + block, full // LANES
    steps = full // BLOCK
    tiles = TILES + steps
    reach = min(DOC_MOST // block + 1, 2 * n - 1)
    whole = lambda *shape: pl.BlockSpec(shape, lambda i: (0,) * len(shape), pipeline_mode=pl.Buffered(1))
    tile = lambda i, half: jnp.minimum(i, TILES - 1) + half * TILES
    back = lambda i: jnp.clip(i - BACK, 0, steps - 1)
    wide = lambda dtype: pltpu.VMEM((block, full), dtype)
    stacked = lambda count, dtype=F32: pltpu.VMEM((lane_blocks, count, LANES), dtype)
    shape = jax.ShapeDtypeStruct
    if summed:
        out_shape = [shape((full // 16, tiles * PART), F32)] * 2 + [shape((FIR + 8, full), F32), shape((16, full), F32)]
        out_shape += [shape((2 * block, full // 2), F32)] * 2
        out_specs = [whole(full // 16, tiles * PART)] * 2 + [whole(FIR + 8, full), whole(16, full)]
        out_specs += [pl.BlockSpec(memory_space=pl.ANY)] * 2
        extra = Summing.scratch(tiles, TILES, full // 16) + Joining.scratch(FIR + 8, full) + Joining.scratch(16, full)
        extra += [pltpu.SemaphoreType.DMA((2,))] * 3
    else:
        out_shape = [shape((tiles, 2, full, TILE), BF16), shape((FIR + 8, full), F32), shape((16, full), F32)]
        out_shape += [shape((block, full), F32)] * 2 + [shape((8, LANES), F32)]
        place = lambda i: jnp.minimum(i, TILES - 1) + jnp.clip(i - BACK + 1, 0, steps)
        out_specs = [pl.BlockSpec((1, 2, full, TILE), lambda i: (place(i), 0, 0, 0)), whole(FIR + 8, full), whole(16, full)]
        out_specs += [whole(block, full)] * 2 + [whole(8, LANES)]
        extra = []
    return pl.pallas_call(
        functools.partial(backward_kernel, n, block, reach, summed),
        name="backward",
        grid=(BACK + steps + (STAGES if summed else 0),),
        out_shape=out_shape,
        in_specs=[
            pl.BlockSpec(memory_space=pltpu.SMEM),
            whole(*tok.shape), whole(*ids.shape), whole(*enter.shape), whole(*g.shape), whole(*gains.shape),
            whole(*vec.shape), whole(*wout.shape), whole(*x0.shape), whole(*base.shape), whole(*car.shape),
            whole(*u.shape), whole(*n1.shape), whole(*heads.shape),
            pl.BlockSpec((full, PART), lambda i: (0, tile(i, 0))),
            pl.BlockSpec((full, PART), lambda i: (0, tile(i, 1))),
            pl.BlockSpec((PART, full), lambda i: (tile(i, 0), 0)),
            pl.BlockSpec((PART, full), lambda i: (tile(i, 1), 0)),
            pl.BlockSpec((3, full, BLOCK), lambda i: (0, 0, back(i))),
            pl.BlockSpec((3, BLOCK // LANES, rows, LANES), lambda i: (0, back(i), 0, 0)),
        ],
        out_specs=out_specs,
        scratch_shapes=[
            wide(BF16), wide(F32), wide(BF16), wide(F32), wide(BF16), wide(F32), wide(F32),
            stacked(block), stacked(block), stacked(block + 48), stacked(block),
            pltpu.VMEM((3, BLOCK // LANES, block + 8, LANES), F32),
            pltpu.VMEM((3, block, BLOCK), BF16),
            pltpu.VMEM((3, BLOCK // LANES, rows, LANES), F32),
            pltpu.VMEM((block, LANES), F32),
            pltpu.VMEM((block, LANES), F32),
            pltpu.VMEM((lane_blocks, FIR, 8, LANES), F32),
            pltpu.VMEM((1, full), F32),
            pltpu.VMEM((reach, 1, full), F32),
            pltpu.VMEM((2, full), F32),
            pltpu.VMEM((HALO, full), F32),
            pltpu.VMEM((HALO, full), F32),
            pltpu.VMEM((8, full), F32),
            pltpu.SemaphoreType.DMA((reach,)),
            pltpu.SemaphoreType.DMA((reach,)),
            pltpu.SemaphoreType.DMA((2,)),
            *extra,
        ],
        compiler_params=pltpu.CompilerParams(collective_id=2, has_side_effects=True, vmem_limit_bytes=60 << 20),
    )(marks, tok, ids, enter, g, gains, vec, wout, x0, base, car, u, n1, heads, wup, wup, wdn, wdn, win, proj)


def reduce_plain(n, grads, small_a, small_b, out, gtok):
    both = lax.psum_scatter(grads.astype(F32), "ch", scatter_dimension=1, tiled=False)
    total = lax.psum_scatter(both, "seq", scatter_dimension=1, tiled=True)
    total = jnp.transpose(total, (1, 0, 2))
    parts = [total[:, :, k * PART : (k + 1) * PART].reshape(total.shape[0], -1) for k in range(2)]
    swap = lambda whole: lax.all_to_all(whole, "ch", split_axis=1, concat_axis=0, tiled=True)
    small_a, small_b = lax.psum((small_a, small_b), ("seq", "ch"))
    return *parts, small_a, small_b, swap(out), swap(gtok)


def on_device(tokens, seg_ids, norm1_gain, in_weight, short_weight, filt_w1, filt_b1, filt_w2, filt_w3,
              long_bias, tail_gain, tail_rate, out_weight, norm2_gain, up_weight, down_weight, grad_out):
    rows, width = tokens.shape
    full, block = 2 * width, rows // 2
    n = lax.axis_size("seq")
    devices = 2 * n
    me = 2 * lax.axis_index("seq") + lax.axis_index("ch")
    row_start = me * block
    total_rows = seg_ids.shape[0]
    length = min(SEQ_LEN, total_rows)

    keys = seg_ids + (jnp.arange(total_rows, dtype=jnp.int32) // length) * 65536
    padded = jnp.concatenate([jnp.full((BEFORE,), -1, jnp.int32), keys, jnp.full((block + AFTER,), -2, jnp.int32)])
    near = lax.dynamic_slice_in_dim(padded, row_start, BEFORE + block + AFTER)
    window, ids_s = near, near
    ids = jnp.broadcast_to(window.astype(F32)[:, None], (window.shape[0], LANES))

    channel_start = lax.axis_index("ch") * width
    pos_table = position_table(FIR, (filt_w1.shape[0] - 1) // 2)
    pre_one = jnp.dot(pos_table, filt_w1, precision=HIGHEST) + filt_b1
    hidden_one = jnp.sin(pre_one)
    pre_two = jnp.dot(hidden_one, filt_w2, precision=HIGHEST)
    hidden_two = jnp.sin(pre_two)
    channel = channel_start.astype(F32) + jnp.arange(width, dtype=F32)
    window_of = lambda channels: jnp.exp(
        -(0.5 + 3.0 * channels / full)[None, :] * jnp.arange(FIR, dtype=F32)[:, None] / FIR)
    taps = jnp.dot(hidden_two, filt_w3, precision=HIGHEST) * window_of(channel)
    norm_tail = jnp.sqrt(-jnp.expm1(-2.0 * tail_rate))
    def rows_in(count, parts):
        index = jnp.arange(count)[:, None]
        rows = jnp.zeros((count, width), F32)
        for k, part in enumerate(parts):
            rows = jnp.where(index == k, part[None, :], rows)
        return rows

    gains = jnp.concatenate([rows_in(8, [norm1_gain, norm2_gain]), filt_w3])
    zeros = jnp.zeros((width,), F32)
    head = rows_in(HEAD, [zeros, zeros, long_bias, tail_gain, tail_rate, norm_tail] + [
        short_weight[j, s] for j in range(3) for s in range(3)])

    tok, g, win, wout, wup, wdn, gains, vec = exchange(
        n, tokens, grad_out, jnp.transpose(in_weight, (1, 0, 2)), out_weight, up_weight, down_weight, gains, head, taps)

    n1, proj, x0, u, base, car, end, heads = mixer(ids_s, tok, win, gains, vec, ids)
    marks = jnp.concatenate([keys[::block], keys[block - 1 :: block]])
    enter = push(n, block, marks, end, vec)

    summed = n == 16
    results = backward(n, summed, marks, tok, ids, enter, g, gains[:8], vec, wout, x0, base, car, u, n1, heads, wup, wdn, win, proj)
    if not summed:
        results = reduce_plain(n, *results[:5])
    part_a, part_b, small_a, small_b, out, gtok = results

    def natural(paired):
        count = paired.shape[0]
        return jnp.transpose(paired.reshape(count, -1, 2, LANES), (0, 2, 1, 3)).reshape(count, full)

    small_a, gain_two = natural(small_a), small_a[FIR]
    small_b, gain_one = natural(small_b), small_b[10]
    taps_grad, bias_grad, long_car = small_a[:FIR], small_a[FIR + 1], small_a[FIR + 2]
    short_grad, carried_q = small_b[:9].reshape(3, 3, full), small_b[9]
    vec = natural(vec[:HEAD])
    gain, rate, nu = vec[3], vec[4], vec[5]
    factor = jnp.exp(-rate)
    rate_grad = gain * long_car * factor * factor / nu - carried_q
    raw_grad = taps_grad * window_of(jnp.arange(full, dtype=F32))
    w3_grad = jnp.dot(hidden_two.T, raw_grad, precision=HIGHEST)
    pre_two_grad = jnp.dot(raw_grad, gains[8:].T, precision=HIGHEST) * jnp.cos(pre_two)
    w2_grad = jnp.dot(hidden_one.T, pre_two_grad, precision=HIGHEST)
    pre_one_grad = jnp.dot(pre_two_grad, filt_w2.T, precision=HIGHEST) * jnp.cos(pre_one)
    w1_grad = jnp.dot(pos_table.T, pre_one_grad, precision=HIGHEST)
    hidden = up_weight.shape[1]
    rows_out = part_a.shape[0]
    mixer_grads = jnp.stack([part[:, hidden:].reshape(rows_out, -1, 2, LANES) for part in (part_a, part_b)], axis=2)
    mixer_grads = mixer_grads.reshape(rows_out, -1, 4, LANES)
    mixer_grads = jnp.transpose(mixer_grads, (0, 2, 1, 3)).reshape(rows_out, 4, width)
    return (
        out,
        gtok,
        gain_one,
        mixer_grads[:, :3],
        short_grad,
        w1_grad,
        jnp.sum(pre_one_grad, axis=0),
        w2_grad,
        w3_grad,
        bias_grad,
        nu * long_car,
        rate_grad,
        mixer_grads[:, 3].T,
        gain_two,
        part_a[:, :hidden],
        part_b[:, :hidden].T,
    )


def solution(mesh):
    placed = (
        P("seq", "ch"),
        P(),
        P("ch"),
        P(None, None, "ch"),
        P(None, None, "ch"),
        P(),
        P(),
        P(),
        P(None, "ch"),
        P("ch"),
        P("ch"),
        P("ch"),
        P("ch", None),
        P("ch"),
        P(None, "ch"),
        P("ch", None),
        P("seq", "ch"),
    )
    return jax.shard_map(
        on_device,
        mesh=mesh,
        in_specs=placed,
        out_specs=(
            P("seq", "ch"),
            P("seq", "ch"),
            P(),
            P("seq", None, "ch"),
            P(),
            P(),
            P(),
            P(),
            P(),
            P(),
            P(),
            P(),
            P("ch", "seq"),
            P(),
            P("seq", "ch"),
            P("ch", "seq"),
        ),
        check_vma=False,
    )
```

time: 273 us -> 213 us (0.78)
  Pallas kernels: 236 us -> 183 us
  other arithmetic: 9.51 us -> 6.59 us
    pallas_call x6 -> x2, Pallas kernels: 189 us -> 136 us  [the longest x1 129 us: backward(): pl.pallas_call(functools.partial(backward_kernel, n, block, reach, summed...]
    concatenate x1 -> x0, local copies, waits for them, and re-layouts: 2.95 us -> none  [on_device(): jnp.concatenate([sums_two[:42], sums, gain_one, gain_two, jnp.zeros((2, f...]
    slice x6 -> x16, local copies, waits for them, and re-layouts: 4.08 us -> 6.77 us  [the longest x1 1.34 us: on_device(): small_b, gain_one = (natural(small_b), small_b[10])]
where the time goes in v1:
time: 213 us; the launch traced here: 212 us
  Pallas kernels  183 us (86%)
  local copies, waits for them, and re-layouts  14.9 us (7%)
  matrix products  6.72 us (3%)
  other arithmetic  6.59 us (3%)
    pallas_call x1, Pallas kernels, backward(): pl.pallas_call(functools.partial(backward_kernel, n, block, reach, summed...  129 us
    pallas_call x1, Pallas kernels, mixer(): pl.pallas_call(functools.partial(mixer_kernel, block), name='mixer', grid...  26 us
    pallas_call x1, Pallas kernels, exchange(): pl.pallas_call(functools.partial(exchange_kernel, (n, rows, width, hidden...  21.6 us
    pallas_call x1, Pallas kernels, push(): pl.pallas_call(functools.partial(push_kernel, n, reach, block), name='pus...  6.52 us

profile of v1, /device:TPU:0, one launch (start us, length us, event | category | flops | bytes accessed | tf_op | source)
XLA Modules:
  0.0 212.4 jit_solution(11095726796030497234)
XLA Ops:
  0.6 0.0 copy-start
  0.7 0.9 slice_reduce_fusion.10
  1.6 0.7 negate_sqrt_fusion
  2.3 1.4 select_select_fusion.head
  3.8 0.1 multiply_cosine_fusion
  3.9 1.0 fusion.20
  5.0 0.0 copy-done
  5.0 0.2 fusion.21
  5.2 1.7 convolution_multiply_fusion.taps
  6.9 0.8 select_select_fusion.1
  7.7 1.5 pad_maximum_fusion.1.gains
  9.2 0.0 copy-start.6
  9.2 21.6 %exchange.1 = (bf16[560,768]{1,0:T(8,128)(2,1)}, bf16[512,768]{1,0:T(8,128)(2,1)}, bf16[3,768,768]{2,1,0:T(8,128)(2,1)}, bf16[768,768]{1,0:T(8,128)(2,1)}, bf16[...) custom-call(bf16[1024,384]{1,0:T(8,128)(2,1)} %tokens.1, ...), custom_call_target="tpu_custom_call" | custom-call | tf_op jit(solution)/shard_map/exchange/pallas_call | solution.py:158
  30.9 0.0 copy-done.6
  30.9 0.1 concatenate.15
  31.0 0.7 fusion.17
  31.7 0.9 broadcast_in_dim.269.ids
  32.6 0.0 copy-start.3
  32.6 26.0 %mixer.1 = (bf16[512,768]{1,0:T(8,128)(2,1)}, bf16[3,6,560,128]{3,2,1,0:T(8,128)(2,1)}, f32[6,512,128]{2,1,0:T(8,128)}, f32[6,560,128]{2,1,0:T(8,128)}, f32[6,51...) custom-call(s32[640]{0:T(1024)} %get-tuple-element.70.ids_s, ...), custom_call_target="tpu_custom_call" | custom-call | tf_op jit(solution)/shard_map/mixer/pallas_call | solution.py:311
  58.5 0.1 slice.100
  58.6 0.1 slice.101
  58.8 0.6 pad_add_fusion.marks
  59.4 6.5 %push.1.enter = f32[1,768]{1,0:T(1,128)} custom-call(s32[64]{0:T(128)} %pad_add_fusion.marks, f32[1,768]{1,0:T(1,128)} %get-tuple-element.42.end, f32[48,768]{1,0:T(8,128)} %get-tuple-element.41.vblk.vec), custom_call_target="tpu_custom_call" | custom-call | tf_op jit(solution)/shard_map/push/pallas_call | solution.py:427
  65.9 0.0 copy-done.3
  65.9 0.6 slice.111.gains
  66.5 129.1 %backward.1 = (f32[48,2304]{1,0:T(8,128)}, f32[48,2304]{1,0:T(8,128)}, f32[40,768]{1,0:T(8,128)}, f32[16,768]{1,0:T(8,128)}, f32[1024,384]{1,0:T(8,128)}, /*index=5*/f32[1024,384]{1,0:T(8,128)}) custom-call(s32[64]{0:T(128)} %pad_add_fusion.marks, bf16[560,768]{1,0:T(8,128)(2,1)} %get-tuple-element.38.tok, f32[640,128]{1,0:T(8,128)} %broadcast_in_dim.269.ids, ...), custom_call_target="tpu_custom_call" | custom-call | tf_op jit(solution)/shard_map/backward/pallas_call | solution.py:1027
  195.6 0.0 copy-start.5
  195.6 0.0 copy-start.4
  195.6 1.0 reshape.205
  196.7 0.8 reshape.203
  197.6 0.8 slice.121
  198.5 0.6 fusion.12
  199.2 0.1 slice.118
  199.2 0.3 convolution_multiply_fusion.2
  199.5 0.9 fusion.23
  200.4 0.7 fusion.22
  201.1 0.9 fusion.16
  202.0 0.0 copy-done.5
  202.0 0.1 stack_reshape.6
  202.1 0.0 copy-done.4
  202.1 0.1 stack_reshape.7
  202.2 0.0 copy-start.2
  202.3 0.7 slice.131
  203.0 0.6 slice_bitcast_fusion.1
  203.6 1.0 fusion.1
  204.7 0.6 squeeze.26
  205.3 0.7 slice.129
  206.0 0.7 slice_bitcast_fusion
  206.8 0.0 copy-start.1
  206.8 0.6 reshape.204
  207.4 1.3 slice_reduce_fusion
  208.8 1.3 slice_reduce_fusion.1
  210.1 0.0 copy-done.2
  210.1 1.1 copy.51
  211.2 0.0 copy-done.1
  211.2 1.1 copy.52
  (36 shorter events, 0.4 us)
Async XLA Ops:
  0.6 4.3 %copy-start = (f32[64,64]{1,0:T(8,128)S(1)}, f32[64,64]{1,0:T(8,128)}, u32[]{:S(2)}) copy-start(f32[64,64]{1,0:T(8,128)} %param.24) | copy-start | bytes 49156
  9.2 21.6 %copy-start.6 = (s32[16384]{0:T(1024)S(1)}, s32[16384]{0:T(1024)}, u32[]{:S(2)}) copy-start(s32[16384]{0:T(1024)} %param.18) | copy-start | bytes 196612
  32.6 33.3 %copy-start.3 = (f32[72,768]{1,0:T(8,128)S(1)}, f32[72,768]{1,0:T(8,128)}, u32[]{:S(2)}) copy-start(f32[72,768]{1,0:T(8,128)} %get-tuple-element.40.gains) | copy-start | bytes 663556
  195.6 6.4 %copy-start.5 = (f32[48,2304]{1,0:T(8,128)S(1)}, f32[48,2304]{1,0:T(8,128)}, u32[]{:S(2)}) copy-start(f32[48,2304]{1,0:T(8,128)} %get-tuple-element.57) | copy-start | bytes 1327108
  195.6 6.5 %copy-start.4 = (f32[48,2304]{1,0:T(8,128)S(1)}, f32[48,2304]{1,0:T(8,128)}, u32[]{:S(2)}) copy-start(f32[48,2304]{1,0:T(8,128)} %get-tuple-element.58) | copy-start | bytes 1327108
  202.2 7.9 %copy-start.2 = (f32[1024,384]{1,0:T(8,128)S(1)}, f32[1024,384]{1,0:T(8,128)}, u32[]{:S(2)}) copy-start(f32[1024,384]{1,0:T(8,128)} %get-tuple-element.116) | copy-start | bytes 4718596
  206.8 4.5 %copy-start.1 = (f32[1024,384]{1,0:T(8,128)S(1)}, f32[1024,384]{1,0:T(8,128)}, u32[]{:S(2)}) copy-start(f32[1024,384]{1,0:T(8,128)} %get-tuple-element.117) | copy-start | bytes 4718596

commit v2 on v1

--- a/solution.py
+++ b/solution.py
@@ -38,317 +38,6 @@
     return pl.ds(pl.multiple_of(start, size), size)
 
 
-def exchange_kernel(sizes, tokens, gout, w_in, w_out, w_up, w_down, gains, head, taps,
-                    tok_o, g_o, in_o, out_o, up_o, down_o, gains_o, vec_o, local_sem, send_sem, recv_sem):
-    n, rows, width, hidden = sizes
-    block = rows // 2
-    s, c = lax.axis_index("seq"), lax.axis_index("ch")
-    barrier = pltpu.get_barrier_semaphore()
-    pl.semaphore_signal(barrier, inc=1, device_id=(s, 1 - c), device_id_type=MESH)
-
-    @pl.when((c == 0) & (s > 0))
-    def _():
-        for k in range(2):
-            pl.semaphore_signal(barrier, inc=1, device_id=(s - 1, k), device_id_type=MESH)
-
-    @pl.when(s < n - 1)
-    def _():
-        pl.semaphore_wait(barrier, 2)
-
-    @pl.when(s == n - 1)
-    def _():
-        pl.semaphore_wait(barrier, 1)
-
-    cols = pl.ds(pl.multiple_of(c * width, width), width)
-    hid = pl.ds(pl.multiple_of(c * hidden, hidden), hidden)
-    pairs = [
-        (gains, gains_o.at[:, cols]),
-        (w_up, up_o.at[:, hid]),
-        (w_down, down_o.at[hid, :]),
-    ]
-    for i in range(width // LANES):
-        source = pl.ds(i * LANES, LANES)
-        paired = pl.ds(pl.multiple_of((2 * i + c) * LANES, LANES), LANES)
-        pairs += [
-            (w_in.at[:, :, source], in_o.at[:, :, paired]),
-            (w_out.at[source, :], out_o.at[paired, :]),
-            (head.at[:, source], vec_o.at[pl.ds(0, HEAD), paired]),
-            (taps.at[:, source], vec_o.at[pl.ds(HEAD, FIR), paired]),
-        ]
-
-    def remote(src, dst, k, target):
-        return pltpu.make_async_remote_copy(
-            src_ref=src, dst_ref=dst, send_sem=send_sem.at[k], recv_sem=recv_sem.at[k],
-            device_id=target, device_id_type=MESH)
-
-    partner = (s, 1 - c)
-    left, right = pl.ds(0, width), pl.ds(width, width)
-    first, second = pl.ds(0, block), pl.ds(block, block)
-    early = pl.ds(block - BEFORE, block + BEFORE)
-    tail = pl.ds(rows - BEFORE, BEFORE)
-
-    @pl.when(c == 0)
-    def _():
-        remote(tokens.at[early, :], tok_o.at[:, left], 0, partner).start()
-        remote(gout.at[second, :], g_o.at[:, left], 1, partner).start()
-        pltpu.make_async_copy(tokens.at[first, :], tok_o.at[pl.ds(BEFORE, block), left], local_sem.at[0]).start()
-        pltpu.make_async_copy(gout.at[first, :], g_o.at[:, left], local_sem.at[1]).start()
-
-        @pl.when(s < n - 1)
-        def _():
-            remote(tokens.at[tail, :], tok_o.at[pl.ds(0, BEFORE), left], 2, (s + 1, 0)).start()
-
-    @pl.when(c == 1)
-    def _():
-        remote(tokens.at[first, :], tok_o.at[pl.ds(BEFORE, block), right], 0, partner).start()
-        remote(gout.at[first, :], g_o.at[:, right], 1, partner).start()
-        pltpu.make_async_copy(tokens.at[early, :], tok_o.at[:, right], local_sem.at[0]).start()
-        pltpu.make_async_copy(gout.at[second, :], g_o.at[:, right], local_sem.at[1]).start()
-
-        @pl.when(s < n - 1)
-        def _():
-            remote(tokens.at[tail, :], tok_o.at[pl.ds(0, BEFORE), right], 3, (s + 1, 0)).start()
-
-    for k, (src, dst) in enumerate(pairs):
-        remote(src, dst, 4 + k, partner).start()
-        pltpu.make_async_copy(src, dst, local_sem.at[2 + k]).start()
-
-    for k, (src, dst) in enumerate(pairs):
-        pltpu.make_async_copy(src, dst, local_sem.at[2 + k]).wait()
-        remote(src, dst, 4 + k, partner).wait()
-
-    @pl.when(c == 0)
-    def _():
-        remote(tokens.at[early, :], tok_o.at[:, left], 0, partner).wait_send()
-        remote(gout.at[second, :], g_o.at[:, left], 1, partner).wait_send()
-        remote(tokens.at[first, :], tok_o.at[pl.ds(BEFORE, block), right], 0, partner).wait_recv()
-        remote(gout.at[first, :], g_o.at[:, right], 1, partner).wait_recv()
-        pltpu.make_async_copy(tokens.at[first, :], tok_o.at[pl.ds(BEFORE, block), left], local_sem.at[0]).wait()
-        pltpu.make_async_copy(gout.at[first, :], g_o.at[:, left], local_sem.at[1]).wait()
-
-        @pl.when(s < n - 1)
-        def _():
-            remote(tokens.at[tail, :], tok_o.at[pl.ds(0, BEFORE), left], 2, (s + 1, 0)).wait_send()
-
-        @pl.when(s > 0)
-        def _():
-            remote(tokens.at[tail, :], tok_o.at[pl.ds(0, BEFORE), left], 2, partner).wait_recv()
-            remote(tokens.at[tail, :], tok_o.at[pl.ds(0, BEFORE), right], 3, partner).wait_recv()
-
-    @pl.when(c == 1)
-    def _():
-        remote(tokens.at[first, :], tok_o.at[pl.ds(BEFORE, block), right], 0, partner).wait_send()
-        remote(gout.at[first, :], g_o.at[:, right], 1, partner).wait_send()
-        remote(tokens.at[early, :], tok_o.at[:, left], 0, partner).wait_recv()
-        remote(gout.at[second, :], g_o.at[:, left], 1, partner).wait_recv()
-        pltpu.make_async_copy(tokens.at[early, :], tok_o.at[:, right], local_sem.at[0]).wait()
-        pltpu.make_async_copy(gout.at[second, :], g_o.at[:, right], local_sem.at[1]).wait()
-
-        @pl.when(s < n - 1)
-        def _():
-            remote(tokens.at[tail, :], tok_o.at[pl.ds(0, BEFORE), right], 3, (s + 1, 0)).wait_send()
-
-
-def exchange(n, tokens, gout, w_in, w_out, w_up, w_down, *vec):
-    rows, width = tokens.shape
-    hidden = w_up.shape[1]
-    full, block = 2 * width, rows // 2
-    pieces = 3 + 4 * (width // LANES)
-    anywhere = pl.BlockSpec(memory_space=pl.ANY)
-    return pl.pallas_call(
-        functools.partial(exchange_kernel, (n, rows, width, hidden)),
-        name="exchange",
-        out_shape=(
-            jax.ShapeDtypeStruct((BEFORE + block, full), BF16),
-            jax.ShapeDtypeStruct((block, full), BF16),
-            jax.ShapeDtypeStruct((3, full, full), BF16),
-            jax.ShapeDtypeStruct((full, full), BF16),
-            jax.ShapeDtypeStruct((full, 2 * hidden), BF16),
-            jax.ShapeDtypeStruct((2 * hidden, full), BF16),
-            jax.ShapeDtypeStruct((vec[0].shape[0], full), F32),
-            jax.ShapeDtypeStruct((HEAD + FIR, full), F32),
-        ),
-        in_specs=[anywhere] * 9,
-        out_specs=[pl.BlockSpec(memory_space=pltpu.VMEM)] * 8,
-        scratch_shapes=[pltpu.SemaphoreType.DMA((2 + pieces,))] + [pltpu.SemaphoreType.DMA((4 + pieces,))] * 2,
-        compiler_params=pltpu.CompilerParams(collective_id=0, has_side_effects=True, vmem_limit_bytes=VMEM_LIMIT),
-    )(tokens, gout, w_in, w_out, w_up, w_down, *vec)
-
-
-def row_stats(values):
-    center = jnp.mean(values, axis=1, keepdims=True)
-    shifted = values - center
-    inverse = lax.rsqrt(jnp.mean(shifted * shifted, axis=1, keepdims=True) + EPSILON)
-    return shifted * inverse, inverse
-
-
-def mixer_kernel(block, ids_s, tok, win, gains, vblk, ids, n1_o, proj_o, x0_o, u_o, long_o, car_o, end_o, heads_o,
-                 n1_s, proj_s, state_s):
-    rows = BEFORE + block
-    lane_blocks = BLOCK // LANES
-
-    @pl.when(pl.program_id(0) == 0)
-    def _():
-        gain = gains[0:1, :]
-
-        def normed(j, _):
-            at = pl.ds(pl.multiple_of(j * 16, 16), 16)
-            values = jnp.where(ids[at, 0:1] >= 0.0, tok[at, :].astype(F32), 0.0)
-            n1_s[at, :] = (row_stats(values)[0] * gain).astype(BF16)
-            return 0
-
-        lax.fori_loop(0, rows // 16, normed, 0)
-        n1_o[...] = n1_s[pl.ds(BEFORE, block), :]
-
-    for s in range(3):
-        part = jnp.dot(n1_s[...], win[s], preferred_element_type=F32).astype(BF16)
-        for b in range(lane_blocks):
-            proj_o[s, b] = part[:, b * LANES : (b + 1) * LANES]
-            proj_s[s, b] = part[:, b * LANES : (b + 1) * LANES].astype(F32)
-
-    def convolved(start, size):
-        own = ids[pl.ds(start, size), :]
-        same = [None] + [own == ids[pl.ds(start - j, size), :] for j in (1, 2)]
-        results = []
-        for b in range(lane_blocks):
-            lanes = slice(b * LANES, (b + 1) * LANES)
-            streams = []
-            for s in range(3):
-                value = vblk[6 + s : 7 + s, lanes] * proj_s[s, b, pl.ds(start, size), :]
-                for j in (1, 2):
-                    tap = vblk[6 + 3 * j + s : 7 + 3 * j + s, lanes]
-                    value += jnp.where(same[j], tap * proj_s[s, b, pl.ds(start - j, size), :], 0.0)
-                streams.append(value)
-            u_o[b, pl.ds(start, size), :] = (streams[0] * streams[2]).astype(BF16).astype(F32)
-            results.append(streams)
-        return results
-
-    convolved(16, 32)
-    for b, streams in enumerate(convolved(BEFORE, 8)):
-        heads_o[0:8, b * LANES : (b + 1) * LANES] = streams[2]
-        heads_o[8:16, b * LANES : (b + 1) * LANES] = streams[0]
-    for b in range(lane_blocks):
-        u_o[b, 0:16, :] = jnp.zeros((16, LANES), F32)
-
-    def conv_chunk(j, _):
-        start = pl.multiple_of(BEFORE + j * 32, 16)
-        for b, streams in enumerate(convolved(start, 32)):
-            x0_o[b, pl.ds(pl.multiple_of(j * 32, 32), 32), :] = streams[1]
-        return 0
-
-    lax.fori_loop(0, block // 32, conv_chunk, 0)
-
-    row_id = lax.broadcasted_iota(jnp.int32, (8, LANES), 0)
-    rates = [vblk[4:5, b * LANES : (b + 1) * LANES] for b in range(lane_blocks)]
-    powers = [jnp.exp(-rate * (row_id + 1).astype(F32)) for rate in rates]
-    lams = [[jnp.exp(-rate * float(step)) for step in (1, 2, 4)] for rate in rates]
-    for b in range(lane_blocks):
-        state_s[b, 0:8, :] = jnp.zeros((8, LANES), F32)
-
-    def scan_group(g, carry):
-        start = pl.multiple_of(BEFORE + g * 8, 8)
-        own = ids[pl.ds(start, 8), :]
-        masks = [(own == ids[pl.ds(start - step, 8), :]) & (row_id >= step) for step in (1, 2, 4)]
-        joined = own == jnp.broadcast_to(ids[pl.ds(start - 1, 1), :], (8, LANES))
-        result = []
-        for b in range(lane_blocks):
-            value = u_o[b, pl.ds(start, 8), :]
-            for mask, lam, step in zip(masks, lams[b], (1, 2, 4)):
-                value += jnp.where(mask, lam * pltpu.roll(value, step, 0), 0.0)
-            value += jnp.where(joined, powers[b] * carry[b], 0.0)
-            state_s[b, pl.ds(pl.multiple_of(8 + g * 8, 8), 8), :] = value
-            result.append(jnp.broadcast_to(value[7:8, :], (8, LANES)))
-        return tuple(result)
-
-    zero = jnp.zeros((8, LANES), F32)
-    final = lax.fori_loop(0, block // 8, scan_group, (zero,) * lane_blocks, unroll=4)
-    for b in range(lane_blocks):
-        end_o[:, b * LANES : (b + 1) * LANES] = final[b][0:1, :]
-
-    for b in range(lane_blocks):
-        lanes = slice(b * LANES, (b + 1) * LANES)
-        bias, gain, lam = vblk[2:3, lanes], vblk[3:4, lanes], lams[b][0]
-        nu = vblk[5:6, lanes]
-
-        def long_chunk(j, _):
-            start = pl.multiple_of(BEFORE + j * CHUNK, 16)
-            to = pl.ds(pl.multiple_of(j * CHUNK, CHUNK), CHUNK)
-            own = ids[pl.ds(start, CHUNK), :]
-            here = u_o[b, pl.ds(start, CHUNK), :]
-            previous = state_s[b, pl.ds(7 + j * CHUNK, CHUNK), :]
-            carried = jnp.where(own == ids[pl.ds(start - 1, CHUNK), :], lam * previous, 0.0)
-            car_o[b, to, :] = carried
-            base = bias * here + (gain * nu) * carried
-            whole = ids_s[start + CHUNK - 1] == ids_s[start - FIR + 1]
-
-            @pl.when(whole)
-            def _():
-                total = base
-                for k in range(FIR):
-                    total += vblk[16 + k : 17 + k, lanes] * u_o[b, pl.ds(start - k, CHUNK), :]
-                long_o[b, to, :] = total
-
-            @pl.when(jnp.logical_not(whole))
-            def _():
-                total = base
-                for k in range(FIR):
-                    term = vblk[16 + k : 17 + k, lanes] * u_o[b, pl.ds(start - k, CHUNK), :]
-                    total += jnp.where(own == ids[pl.ds(start - k, CHUNK), :], term, 0.0)
-                long_o[b, to, :] = total
-
-            return 0
-
-        lax.fori_loop(0, block // CHUNK, long_chunk, 0)
-
-
-def mixer(ids_s, tok, win, gains, vec, ids):
-    rows, full = tok.shape
-    block = rows - BEFORE
-    lane_blocks, lanes = BLOCK // LANES, full // LANES
-    whole = lambda *shape: pl.BlockSpec(shape, lambda i: (0,) * len(shape))
-    by_channel = lambda count: pl.BlockSpec((count, BLOCK), lambda i: (0, i))
-    stacked = lambda count: pl.BlockSpec((lane_blocks, count, LANES), lambda i: (i, 0, 0))
-    return pl.pallas_call(
-        functools.partial(mixer_kernel, block),
-        name="mixer",
-        grid=(full // BLOCK,),
-        out_shape=(
-            jax.ShapeDtypeStruct((block, full), BF16),
-            jax.ShapeDtypeStruct((3, lanes, rows, LANES), BF16),
-            jax.ShapeDtypeStruct((lanes, block, LANES), F32),
-            jax.ShapeDtypeStruct((lanes, rows, LANES), F32),
-            jax.ShapeDtypeStruct((lanes, block, LANES), F32),
-            jax.ShapeDtypeStruct((lanes, block, LANES), F32),
-            jax.ShapeDtypeStruct((1, full), F32),
-            jax.ShapeDtypeStruct((16, full), F32),
-        ),
-        in_specs=[
-            pl.BlockSpec(memory_space=pltpu.SMEM),
-            whole(rows, full),
-            pl.BlockSpec((3, full, BLOCK), lambda i: (0, 0, i)),
-            whole(*gains.shape),
-            by_channel(vec.shape[0]),
-            whole(*ids.shape),
-        ],
-        out_specs=(
-            whole(block, full),
-            pl.BlockSpec((3, lane_blocks, rows, LANES), lambda i: (0, i, 0, 0)),
-            stacked(block),
-            stacked(rows),
-            stacked(block),
-            stacked(block),
-            by_channel(1),
-            by_channel(16),
-        ),
-        scratch_shapes=[
-            pltpu.VMEM((rows, full), BF16),
-            pltpu.VMEM((3, lane_blocks, rows, LANES), F32),
-            pltpu.VMEM((lane_blocks, 8 + block, LANES), F32),
-        ],
-        compiler_params=pltpu.CompilerParams(vmem_limit_bytes=VMEM_LIMIT),
-    )(ids_s, tok, win, gains, vec, ids)
-
-
 def device_of(index):
     return (index // 2, index % 2)
 
@@ -403,37 +92,371 @@
                 self.copy(k).wait_send()
 
 
-def push_kernel(n, reach, block, marks, end, vec, enter_o, slots, send_sem, recv_sem):
-    pushing = Pushing(n, reach, False, end, slots, send_sem, recv_sem)
+def row_stats(values):
+    center = jnp.mean(values, axis=1, keepdims=True)
+    shifted = values - center
+    inverse = lax.rsqrt(jnp.mean(shifted * shifted, axis=1, keepdims=True) + EPSILON)
+    return shifted * inverse, inverse
+
+
+def forward_kernel(n, rows, reach, marks, tokens, gout, w_in, w_out, w_up, w_down, gains, head, taps, ids,
+                   tok_o, g_o, in_o, out_o, up_o, down_o, gains_o, vec_o,
+                   n1_o, proj_o, x0_o, u_o, heads_o, long_o, car_o, dist_o, rest_o, enter_o,
+                   tok_v, g_v, in_v, out_v, gains_v, vec_v, n1_s, proj_s, u_s, state_s, end_s, slots_s,
+                   local_sem, store_sem, send_sem, recv_sem, push_send, push_recv):
+    block, full = rows // 2, in_v.shape[1]
+    width = full // 2
+    steps = full // BLOCK
+    two = range(BLOCK // LANES)
+    step = pl.program_id(0)
+    s, c = lax.axis_index("seq"), lax.axis_index("ch")
     barrier = pltpu.get_barrier_semaphore()
-    pushing.greet(barrier)
-    pushing.await_greetings(barrier, 0)
-    pushing.start()
-    enter_o[...] = jnp.zeros_like(enter_o)
-    rate = vec[4:5, :]
-    last = marks[2 * n + jnp.maximum(pushing.me - 1, 0)]
-
-    def use(k, state):
-        same = jnp.where(marks[2 * n + pushing.me - 1 - k] == last, 1.0, 0.0)
-        enter_o[...] += same * jnp.exp(-rate * float(block * k)) * state
-
-    pushing.take(use)
-
-
-def push(n, block, marks, end, vec):
-    full = end.shape[1]
+    pushing = Pushing(n, reach, False, end_s, slots_s, push_send, push_recv)
+    partner = (s, 1 - c)
+    cols = pl.ds(pl.multiple_of(c * width, width), width)
+    early = [(gains, gains_v.at[:, cols])]
+    late = []
+    for i in range(width // LANES):
+        source = pl.ds(i * LANES, LANES)
+        paired = pl.ds(pl.multiple_of((2 * i + c) * LANES, LANES), LANES)
+        early += [
+            (head.at[:, source], vec_v.at[pl.ds(0, HEAD), paired]),
+            (taps.at[:, source], vec_v.at[pl.ds(HEAD, FIR), paired]),
+            (w_in.at[:, :, source], in_v.at[:, :, paired]),
+        ]
+        late.append((w_out.at[source, :], out_v.at[paired, :]))
+
+    def remote(src, dst, k, target=partner):
+        return pltpu.make_async_remote_copy(
+            src_ref=src, dst_ref=dst, send_sem=send_sem.at[k], recv_sem=recv_sem.at[k],
+            device_id=target, device_id_type=MESH)
+
+    halves = [(early[k], k) for k in range(len(early))] + [(late[k], len(early) + k) for k in range(len(late))]
+    count = len(halves)
+    far = [remote(w_up, up_o, count), remote(w_down, down_o, count + 1)]
+    at_tokens = count + 2
+
+    left, right = pl.ds(0, width), pl.ds(width, width)
+    first, second = pl.ds(0, block), pl.ds(block, block)
+    ahead, tail = pl.ds(block - BEFORE, block + BEFORE), pl.ds(rows - BEFORE, BEFORE)
+    main = pl.ds(BEFORE, block)
+    keeps = [
+        [(tokens.at[first, :], tok_v.at[main, left]), (gout.at[first, :], g_v.at[:, left])],
+        [(tokens.at[ahead, :], tok_v.at[:, right]), (gout.at[second, :], g_v.at[:, right])],
+    ]
+    sends = [
+        [(tokens.at[ahead, :], tok_v.at[:, left]), (gout.at[second, :], g_v.at[:, left])],
+        [(tokens.at[first, :], tok_v.at[main, right]), (gout.at[first, :], g_v.at[:, right])],
+    ]
+
+    def edge(which, target):
+        return remote(
+            tokens.at[tail, :], tok_v.at[pl.ds(0, BEFORE), (left, right)[which]], at_tokens + 2 + which, target)
+
+    def for_core(action):
+        for which in range(2):
+
+            @pl.when(c == which)
+            def _():
+                action(which)
+
+    stores = [(tok_v, tok_o), (gains_v, gains_o), (vec_v, vec_o), (in_v, in_o), (g_v, g_o), (out_v, out_o)]
+
+    def store(k):
+        return pltpu.make_async_copy(*stores[k], store_sem.at[k])
+
+    @pl.when(step == 0)
+    def _():
+        pushing.greet(barrier)
+        pl.semaphore_signal(barrier, inc=1, device_id=partner, device_id_type=MESH)
+
+        @pl.when((c == 0) & (s > 0))
+        def _():
+            for k in range(2):
+                pl.semaphore_signal(barrier, inc=1, device_id=(s - 1, k), device_id_type=MESH)
+
+        def begin_own(which):
+            for k, (src, dst) in enumerate(keeps[which]):
+                pltpu.make_async_copy(src, dst, local_sem.at[at_tokens + k]).start()
+
+        for_core(begin_own)
+        for (src, dst), k in halves:
+            pltpu.make_async_copy(src, dst, local_sem.at[k]).start()
+
+        @pl.when(s < n - 1)
+        def _():
+            pushing.await_greetings(barrier, 2)
+
+        @pl.when(s == n - 1)
+        def _():
+            pushing.await_greetings(barrier, 1)
+
+        def begin(which):
+            remote(*sends[which][0], at_tokens).start()
+
+            @pl.when(s < n - 1)
+            def _():
+                edge(which, (s + 1, 0)).start()
+
+        for_core(begin)
+        for (src, dst), k in halves[: len(early)]:
+            remote(src, dst, k).start()
+        for_core(lambda which: remote(*sends[which][1], at_tokens + 1).start())
+        for (src, dst), k in halves[len(early) :]:
+            remote(src, dst, k).start()
+        for copy in far:
+            copy.start()
+
+        def distances(j, _):
+            at = pl.ds(pl.multiple_of(j * 32, 32), 32)
+            start = pl.multiple_of(BEFORE + j * 32, 16)
+            own = ids[pl.ds(start, 32), :]
+            before = after = jnp.zeros((32, LANES), F32)
+            for k in range(1, FIR):
+                before += jnp.where(own == ids[pl.ds(start - k, 32), :], 1.0, 0.0)
+                after += jnp.where(own == ids[pl.ds(start + k, 32), :], 1.0, 0.0)
+            dist_o[at, :] = before
+            rest_o[at, :] = after
+            return 0
+
+        lax.fori_loop(0, block // 32, distances, 0)
+
+        def take_tokens(which):
+            remote(*sends[which][0], at_tokens).wait_send()
+            remote(*sends[1 - which][0], at_tokens).wait_recv()
+            pltpu.make_async_copy(*keeps[which][0], local_sem.at[at_tokens]).wait()
+
+            @pl.when(s < n - 1)
+            def _():
+                edge(which, (s + 1, 0)).wait_send()
+
+            if which == 0:
+
+                @pl.when(s > 0)
+                def _():
+                    for k in range(2):
+                        edge(k, partner).wait_recv()
+
+        for_core(take_tokens)
+        for (src, dst), k in halves[:1]:
+            pltpu.make_async_copy(src, dst, local_sem.at[k]).wait()
+            remote(src, dst, k).wait()
+        store(0).start()
+        store(1).start()
+
+        def normed(j, _):
+            at = pl.ds(pl.multiple_of(j * 80, 16), 80)
+            values = jnp.where(ids[at, 0:1] >= 0.0, tok_v[at, :].astype(F32), 0.0)
+            n1_s[at, :] = (row_stats(values)[0] * gains_v[0:1, :]).astype(BF16)
+            return 0
+
+        lax.fori_loop(0, (BEFORE + block) // 80, normed, 0)
+        n1_o[...] = n1_s[pl.ds(BEFORE, block), :]
+        for (src, dst), k in halves[1 : len(early)]:
+            pltpu.make_async_copy(src, dst, local_sem.at[k]).wait()
+            remote(src, dst, k).wait()
+        store(2).start()
+        store(3).start()
+
+    @pl.when(step < steps)
+    def _():
+        lanes = [pl.ds(pl.multiple_of((2 * step + b) * LANES, LANES), LANES) for b in two]
+        wide = pl.ds(pl.multiple_of(step * BLOCK, BLOCK), BLOCK)
+        for t in range(3):
+            part = jnp.dot(n1_s[...], in_v[t, :, wide], preferred_element_type=F32).astype(BF16)
+            for b in two:
+                proj_o[t, b] = part[:, b * LANES : (b + 1) * LANES]
+                proj_s[t, b] = part[:, b * LANES : (b + 1) * LANES].astype(F32)
+
+        def convolved(start, size):
+            own = ids[pl.ds(start, size), :]
+            same = [None] + [own == ids[pl.ds(start - j, size), :] for j in (1, 2)]
+            results = []
+            for b in two:
+                streams = []
+                for t in range(3):
+                    value = vec_v[6 + t : 7 + t, lanes[b]] * proj_s[t, b, pl.ds(start, size), :]
+                    for j in (1, 2):
+                        tap = vec_v[6 + 3 * j + t : 7 + 3 * j + t, lanes[b]]
+                        value += jnp.where(same[j], tap * proj_s[t, b, pl.ds(start - j, size), :], 0.0)
+                    streams.append(value)
+                gated = (streams[0] * streams[2]).astype(BF16).astype(F32)
+                u_s[2 * step + b, pl.ds(start, size), :] = gated
+                u_o[b, pl.ds(start, size), :] = gated
+                results.append(streams)
+            return results
+
+        convolved(16, 32)
+        for b, streams in enumerate(convolved(BEFORE, 8)):
+            heads_o[0:8, b * LANES : (b + 1) * LANES] = streams[2]
+            heads_o[8:16, b * LANES : (b + 1) * LANES] = streams[0]
+            u_o[b, 0:16, :] = jnp.zeros((16, LANES), F32)
+            u_s[2 * step + b, 0:16, :] = jnp.zeros((16, LANES), F32)
+
+        def conv_chunk(j, _):
+            start = pl.multiple_of(BEFORE + j * 32, 16)
+            for b, streams in enumerate(convolved(start, 32)):
+                x0_o[b, pl.ds(pl.multiple_of(j * 32, 32), 32), :] = streams[1]
+            return 0
+
+        lax.fori_loop(0, block // 32, conv_chunk, 0)
+
+        row_id = lax.broadcasted_iota(jnp.int32, (8, LANES), 0)
+        rates = [vec_v[4:5, lanes[b]] for b in two]
+        powers = [jnp.exp(-rate * (row_id + 1).astype(F32)) for rate in rates]
+        lams = [[jnp.exp(-rate * float(k)) for k in (1, 2, 4)] for rate in rates]
+        for b in two:
+            state_s[2 * step + b, 0:8, :] = jnp.zeros((8, LANES), F32)
+
+        def scan_group(g, carry):
+            start = pl.multiple_of(BEFORE + g * 8, 8)
+            own = ids[pl.ds(start, 8), :]
+            masks = [(own == ids[pl.ds(start - k, 8), :]) & (row_id >= k) for k in (1, 2, 4)]
+            joined = own == jnp.broadcast_to(ids[pl.ds(start - 1, 1), :], (8, LANES))
+            result = []
+            for b in two:
+                value = u_s[2 * step + b, pl.ds(start, 8), :]
+                for mask, lam, k in zip(masks, lams[b], (1, 2, 4)):
+                    value += jnp.where(mask, lam * pltpu.roll(value, k, 0), 0.0)
+                value += jnp.where(joined, powers[b] * carry[b], 0.0)
+                state_s[2 * step + b, pl.ds(pl.multiple_of(8 + g * 8, 8), 8), :] = value
+                result.append(jnp.broadcast_to(value[7:8, :], (8, LANES)))
+            return tuple(result)
+
+        zero = jnp.zeros((8, LANES), F32)
+        final = lax.fori_loop(0, block // 8, scan_group, (zero,) * len(two), unroll=4)
+        for b in two:
+            end_s[:, lanes[b]] = final[b][0:1, :]
+
+    @pl.when(step == steps - 1)
+    def _():
+        pushing.start()
+
+    @pl.when(step >= steps)
+    def _():
+        i = step - steps
+        lanes = [pl.ds(pl.multiple_of((2 * i + b) * LANES, LANES), LANES) for b in two]
+        lam = [jnp.exp(-vec_v[4:5, lanes[b]]) for b in two]
+        tails = [vec_v[3:4, lanes[b]] * vec_v[5:6, lanes[b]] for b in two]
+
+        def long_chunk(j, _):
+            at = pl.ds(pl.multiple_of(j * 32, 32), 32)
+            start = pl.multiple_of(BEFORE + j * 32, 16)
+            near = dist_o[at, :]
+            totals = []
+            for b in two:
+                previous = state_s[2 * i + b, pl.ds(7 + j * 32, 32), :]
+                carried = jnp.where(near >= 1.0, lam[b] * previous, 0.0)
+                car_o[b, at, :] = carried
+                here = u_s[2 * i + b, pl.ds(start, 32), :]
+                totals.append((vec_v[2:3, lanes[b]] + vec_v[16:17, lanes[b]]) * here + tails[b] * carried)
+            for k in range(1, FIR):
+                same = near >= float(k)
+                for b in two:
+                    term = vec_v[16 + k : 17 + k, lanes[b]] * u_s[2 * i + b, pl.ds(start - k, 32), :]
+                    totals[b] += jnp.where(same, term, 0.0)
+            for b in two:
+                long_o[b, at, :] = totals[b]
+            return 0
+
+        lax.fori_loop(0, block // 32, long_chunk, 0)
+
+    @pl.when(step == steps)
+    def _():
+        def take_rows(which):
+            remote(*sends[which][1], at_tokens + 1).wait_send()
+            remote(*sends[1 - which][1], at_tokens + 1).wait_recv()
+            pltpu.make_async_copy(*keeps[which][1], local_sem.at[at_tokens + 1]).wait()
+
+        for_core(take_rows)
+        for (src, dst), k in halves[len(early) :]:
+            pltpu.make_async_copy(src, dst, local_sem.at[k]).wait()
+            remote(src, dst, k).wait()
+        store(4).start()
+        store(5).start()
+
+    @pl.when(step == 2 * steps - 1)
+    def _():
+        enter_o[...] = jnp.zeros_like(enter_o)
+        rate = vec_v[4:5, :]
+        last = marks[2 * n + jnp.maximum(pushing.me - 1, 0)]
+
+        def use(k, state):
+            same = jnp.where(marks[2 * n + pushing.me - 1 - k] == last, 1.0, 0.0)
+            enter_o[...] += same * jnp.exp(-rate * float(block * k)) * state
+
+        pushing.take(use)
+        for copy in far:
+            copy.wait()
+        for k in range(len(stores)):
+            store(k).wait()
+
+
+def forward(n, marks, tokens, gout, w_in, w_out, w_up, w_down, gains, head, taps, ids):
+    rows, width = tokens.shape
+    hidden = w_up.shape[1]
+    full, block = 2 * width, rows // 2
+    window = BEFORE + block
+    steps, lane_blocks = full // BLOCK, full // LANES
     reach = min(DOC_MOST // block, 2 * n - 1)
-    vmem = pl.BlockSpec(memory_space=pltpu.VMEM)
+    anywhere = pl.BlockSpec(memory_space=pl.ANY)
+    whole = lambda *shape: pl.BlockSpec(shape, lambda i: (0,) * len(shape), pipeline_mode=pl.Buffered(1))
+    soon, later = lambda i: jnp.minimum(i, steps - 1), lambda i: jnp.maximum(i - steps, 0)
+    stacked = lambda count, place: pl.BlockSpec((BLOCK // LANES, count, LANES), lambda i: (place(i), 0, 0))
+    shape = jax.ShapeDtypeStruct
+    vmem = pltpu.VMEM
+    far = 1 + 4 * (width // LANES) + 2 + 4
+    dma = pltpu.SemaphoreType.DMA
+    landing = [
+        ((window, full), BF16), ((block, full), BF16), ((3, full, full), BF16), ((full, full), BF16),
+        ((gains.shape[0], full), F32), ((HEAD + FIR, full), F32),
+    ]
     return pl.pallas_call(
-        functools.partial(push_kernel, n, reach, block),
-        name="push",
-        out_shape=jax.ShapeDtypeStruct((1, full), F32),
-        in_specs=[pl.BlockSpec(memory_space=pltpu.SMEM), vmem, vmem],
-        out_specs=vmem,
+        functools.partial(forward_kernel, n, rows, reach),
+        name="forward",
+        grid=(2 * steps,),
+        out_shape=(
+            *[shape(*part) for part in landing[:4]],
+            shape((full, hidden), BF16),
+            shape((hidden, full), BF16),
+            *[shape(*part) for part in landing[4:]],
+            shape((block, full), BF16),
+            shape((3, lane_blocks, window, LANES), BF16),
+            shape((lane_blocks, block, LANES), F32),
+            shape((lane_blocks, window, LANES), F32),
+            shape((16, full), F32),
+            shape((lane_blocks, block, LANES), F32),
+            shape((lane_blocks, block, LANES), F32),
+            shape((block, LANES), F32),
+            shape((block, LANES), F32),
+            shape((1, full), F32),
+        ),
+        in_specs=[pl.BlockSpec(memory_space=pltpu.SMEM)] + [anywhere] * 9 + [whole(*ids.shape)],
+        out_specs=(
+            *[anywhere] * 8,
+            whole(block, full),
+            pl.BlockSpec((3, BLOCK // LANES, window, LANES), lambda i: (0, soon(i), 0, 0)),
+            stacked(block, soon),
+            stacked(window, soon),
+            pl.BlockSpec((16, BLOCK), lambda i: (0, soon(i))),
+            stacked(block, later),
+            stacked(block, later),
+            whole(block, LANES),
+            whole(block, LANES),
+            whole(1, full),
+        ),
         scratch_shapes=[
-            pltpu.VMEM((reach, 1, full), F32), pltpu.SemaphoreType.DMA((reach,)), pltpu.SemaphoreType.DMA((reach,))],
-        compiler_params=pltpu.CompilerParams(collective_id=1, has_side_effects=True),
-    )(marks, end, vec)
+            *[vmem(*part) for part in landing],
+            vmem((window, full), BF16),
+            vmem((3, BLOCK // LANES, window, LANES), F32),
+            vmem((lane_blocks, window, LANES), F32),
+            vmem((lane_blocks, 8 + block, LANES), F32),
+            vmem((1, full), F32),
+            vmem((reach, 1, full), F32),
+            dma((far,)), dma((6,)), dma((far,)), dma((far,)), dma((reach,)), dma((reach,)),
+        ],
+        compiler_params=pltpu.CompilerParams(collective_id=0, has_side_effects=True, vmem_limit_bytes=VMEM_LIMIT),
+    )(marks, tokens, gout, w_in, w_out, w_up, w_down, gains, head, taps, ids)
 
 
 TILE = 512
@@ -575,10 +598,11 @@
 
 TILES = 6
 EPILOGUE, GATE, TAPS, BACK = TILES, TILES + 1, TILES + 2, TILES + 3
+LAGS = (1, 3, 5, 6, 7)
 HALO = 80
 
 
-def backward_kernel(n, block, reach, summed, marks, tok, ids, enter, g, gains, vec, wout, x0, base, car, u, n1, heads,
+def backward_kernel(n, block, reach, summed, marks, tok, ids, dist_s, rest_s, enter, g, gains, vec, wout, x0, base, car, u, n1, heads,
                     wup_a, wup_b, wdn_a, wdn_b, win, proj, *refs):
     full = g.shape[1]
     width, lane_blocks = full // 2, full // LANES
@@ -590,7 +614,7 @@
     else:
         grads_o, small_a, small_b, out_o, gtok_o, _ = outs
     (mixed_s, middle_s, n2_s, gn_s, gout_s, out_s, gmid_s, long_s, car_s, glong_s, q_s, gc_s, gp_s, proj_s,
-     dist_s, rest_s, taps_s, first_s, slots_s, joined_s, halo_s, halo_r, head_s,
+     taps_s, first_s, slots_s, joined_s, halo_s, halo_r, head_s,
      push_send, push_recv, halo_sem, *buffers) = refs
     step = pl.program_id(0)
     groups = block // 32
@@ -651,13 +675,6 @@
             out_s[at, :] = values
             n2_s[at, :] = (row_stats(values)[0] * gains[1:2, :]).astype(BF16)
             gn_s[at, :] = jnp.zeros_like(values)
-            own = ids[pl.ds(start, 32), :]
-            before = after = jnp.zeros((32, LANES), F32)
-            for k in range(1, FIR):
-                before += jnp.where(own == ids[pl.ds(start - k, 32), :], 1.0, 0.0)
-                after += jnp.where(own == ids[pl.ds(start + k, 32), :], 1.0, 0.0)
-            dist_s[at, :] = before
-            rest_s[at, :] = after
             return 0
 
         lax.fori_loop(0, groups, norm, 0)
@@ -669,11 +686,12 @@
             (part_a, part_b)[part][:, pl.ds(pl.multiple_of(tile * PART, PART), PART)] = value
 
         for stage in range(STAGES - 1, -1, -1):
-            since = step - 1 - stage
-
-            @pl.when(((since >= 0) & (since < TILES)) | ((since >= BACK) & (since <= last_back)))
+            since, early = step - 1 - stage, step - LAGS[stage]
+            is_late = step // (BACK + 1 + stage)
+
+            @pl.when(((early >= 0) & (early < TILES)) | ((since >= BACK) & (since <= last_back)))
             def _():
-                sums.advance(since - (BACK - TILES) * (since // BACK), stage, total)
+                sums.advance(early + (since - (BACK - TILES) - early) * is_late, stage, total)
 
             for join, result, begun in joins:
 
@@ -712,12 +730,11 @@
             for k in range(2):
                 at = pl.ds(k * PART, PART)
                 if summed:
-                    whose = (half + c) % 2
                     for q in range(16):
-                        sums.staged[step % 2, whose, q // 8, q // 4 % 2, q // 2 % 2, q % 2, :, at] = (
+                        sums.staged[step % 2, half, q // 8, q // 4 % 2, q // 2 % 2, q % 2, :, at] = (
                             pair[k][q * sums.rows : (q + 1) * sums.rows])
                 else:
-                    grads_o[0, half, :, at] = pair[k]
+                    grads_o[0, (half + c) % 2, :, at] = pair[k]
         if summed:
             sums.start(step, 0)
 
@@ -953,17 +970,15 @@
                 small[row : row + 1, lanes[k]] = value
 
         tile = TILES + i
-        pieces = []
-        for s in range(3):
-            part = gp_s[s]
-            pieces.append(contract(n1[...], part, ((0,), (0,))).astype(BF16))
-            gn_s[...] += contract(part, win[s], ((1,), (1,)))
+        pieces = [contract(n1[...], gp_s[s], ((0,), (0,))).astype(BF16) for s in range(3)]
         at = pl.ds(pl.multiple_of(i * BLOCK, BLOCK), BLOCK)
         pieces.append(contract(gout_s[...], mixed_s[:, at], ((0,), (0,))).astype(BF16))
         for s, piece in enumerate(pieces):
             put(tile, s * LANES, [piece[:, half * LANES : (half + 1) * LANES] for half in range(2)])
         if summed:
             sums.start(tile, 0)
+        for s in range(3):
+            gn_s[...] += contract(gp_s[s], win[s], ((1,), (1,)))
 
     @pl.when(step == last_back)
     def _():
@@ -998,14 +1013,15 @@
                     copy.wait()
 
 
-def backward(n, summed, marks, tok, ids, enter, g, gains, vec, wout, x0, base, car, u, n1, heads, wup, wdn, win, proj):
+def backward(n, summed, marks, tok, ids, dist, rest, enter, g, gains, vec, wout, x0, base, car, u, n1, heads, ups, downs,
+             win, proj):
     block, full = g.shape
     rows, lane_blocks = BEFORE + block, full // LANES
     steps = full // BLOCK
     tiles = TILES + steps
     reach = min(DOC_MOST // block + 1, 2 * n - 1)
     whole = lambda *shape: pl.BlockSpec(shape, lambda i: (0,) * len(shape), pipeline_mode=pl.Buffered(1))
-    tile = lambda i, half: jnp.minimum(i, TILES - 1) + half * TILES
+    tile = lambda i: jnp.minimum(i, TILES - 1)
     back = lambda i: jnp.clip(i - BACK, 0, steps - 1)
     wide = lambda dtype: pltpu.VMEM((block, full), dtype)
     stacked = lambda count, dtype=F32: pltpu.VMEM((lane_blocks, count, LANES), dtype)
@@ -1031,13 +1047,11 @@
         out_shape=out_shape,
         in_specs=[
             pl.BlockSpec(memory_space=pltpu.SMEM),
-            whole(*tok.shape), whole(*ids.shape), whole(*enter.shape), whole(*g.shape), whole(*gains.shape),
+            whole(*tok.shape), whole(*ids.shape), whole(*dist.shape), whole(*rest.shape), whole(*enter.shape), whole(*g.shape), whole(*gains.shape),
             whole(*vec.shape), whole(*wout.shape), whole(*x0.shape), whole(*base.shape), whole(*car.shape),
             whole(*u.shape), whole(*n1.shape), whole(*heads.shape),
-            pl.BlockSpec((full, PART), lambda i: (0, tile(i, 0))),
-            pl.BlockSpec((full, PART), lambda i: (0, tile(i, 1))),
-            pl.BlockSpec((PART, full), lambda i: (tile(i, 0), 0)),
-            pl.BlockSpec((PART, full), lambda i: (tile(i, 1), 0)),
+            *[pl.BlockSpec((full, PART), lambda i: (0, tile(i)))] * 2,
+            *[pl.BlockSpec((PART, full), lambda i: (tile(i), 0))] * 2,
             pl.BlockSpec((3, full, BLOCK), lambda i: (0, 0, back(i))),
             pl.BlockSpec((3, BLOCK // LANES, rows, LANES), lambda i: (0, back(i), 0, 0)),
         ],
@@ -1048,8 +1062,6 @@
             pltpu.VMEM((3, BLOCK // LANES, block + 8, LANES), F32),
             pltpu.VMEM((3, block, BLOCK), BF16),
             pltpu.VMEM((3, BLOCK // LANES, rows, LANES), F32),
-            pltpu.VMEM((block, LANES), F32),
-            pltpu.VMEM((block, LANES), F32),
             pltpu.VMEM((lane_blocks, FIR, 8, LANES), F32),
             pltpu.VMEM((1, full), F32),
             pltpu.VMEM((reach, 1, full), F32),
@@ -1063,7 +1075,7 @@
             *extra,
         ],
         compiler_params=pltpu.CompilerParams(collective_id=2, has_side_effects=True, vmem_limit_bytes=60 << 20),
-    )(marks, tok, ids, enter, g, gains, vec, wout, x0, base, car, u, n1, heads, wup, wup, wdn, wdn, win, proj)
+    )(marks, tok, ids, dist, rest, enter, g, gains, vec, wout, x0, base, car, u, n1, heads, *ups, *downs, win, proj)
 
 
 def reduce_plain(n, grads, small_a, small_b, out, gtok):
@@ -1090,7 +1102,7 @@
     keys = seg_ids + (jnp.arange(total_rows, dtype=jnp.int32) // length) * 65536
     padded = jnp.concatenate([jnp.full((BEFORE,), -1, jnp.int32), keys, jnp.full((block + AFTER,), -2, jnp.int32)])
     near = lax.dynamic_slice_in_dim(padded, row_start, BEFORE + block + AFTER)
-    window, ids_s = near, near
+    window = near
     ids = jnp.broadcast_to(window.astype(F32)[:, None], (window.shape[0], LANES))
 
     channel_start = lax.axis_index("ch") * width
@@ -1116,15 +1128,15 @@
     head = rows_in(HEAD, [zeros, zeros, long_bias, tail_gain, tail_rate, norm_tail] + [
         short_weight[j, s] for j in range(3) for s in range(3)])
 
-    tok, g, win, wout, wup, wdn, gains, vec = exchange(
-        n, tokens, grad_out, jnp.transpose(in_weight, (1, 0, 2)), out_weight, up_weight, down_weight, gains, head, taps)
-
-    n1, proj, x0, u, base, car, end, heads = mixer(ids_s, tok, win, gains, vec, ids)
     marks = jnp.concatenate([keys[::block], keys[block - 1 :: block]])
-    enter = push(n, block, marks, end, vec)
+    (tok, g, win, wout, up_other, down_other, gains, vec, n1, proj, x0, u, heads, base, car, dist, rest, enter) = forward(
+        n, marks, tokens, grad_out, jnp.transpose(in_weight, (1, 0, 2)), out_weight, up_weight, down_weight,
+        gains, head, taps, ids)
 
     summed = n == 16
-    results = backward(n, summed, marks, tok, ids, enter, g, gains[:8], vec, wout, x0, base, car, u, n1, heads, wup, wdn, win, proj)
+    results = backward(
+        n, summed, marks, tok, ids, dist, rest, enter, g, gains[:8], vec, wout, x0, base, car, u, n1, heads,
+        (up_weight, up_other), (down_weight, down_other), win, proj)
     if not summed:
         results = reduce_plain(n, *results[:5])
     part_a, part_b, small_a, small_b, out, gtok = results

time: 213 us -> 179 us (0.84)
  Pallas kernels: 183 us -> 148 us
    pallas_call x3 -> x1, Pallas kernels: 54.1 us -> 31.3 us  [forward(): pl.pallas_call(functools.partial(forward_kernel, n, rows, reach), name='f...]
    pallas_call x1, Pallas kernels: 129 us -> 116 us  [backward(): pl.pallas_call(functools.partial(backward_kernel, n, block, reach, summed...]
where the time goes in v2:
time: 179 us; the launch traced here: 178 us
  Pallas kernels  148 us (83%)
  local copies, waits for them, and re-layouts  15.6 us (9%)
  other arithmetic  6.83 us (4%)
  matrix products  6.72 us (4%)
    pallas_call x1, Pallas kernels, backward(): pl.pallas_call(functools.partial(backward_kernel, n, block, reach, summed...  116 us
    pallas_call x1, Pallas kernels, forward(): pl.pallas_call(functools.partial(forward_kernel, n, rows, reach), name='f...  31.3 us

profile of v2, /device:TPU:0, one launch (start us, length us, event | category | flops | bytes accessed | tf_op | source)
XLA Modules:
  0.0 177.9 jit_solution(7597750436659048225)
XLA Ops:
  0.6 0.0 copy-start
  0.7 0.9 slice_reduce_fusion.10
  1.6 0.7 negate_sqrt_fusion
  2.3 1.4 select_select_fusion.head
  3.8 0.9 fusion.3
  4.6 0.1 concatenate.15
  4.7 0.1 dynamic-slice_convert_fusion
  4.8 0.9 broadcast_in_dim.269.ids
  5.7 0.1 multiply_cosine_fusion
  5.9 1.0 fusion.19
  6.9 0.0 copy-done
  6.9 0.2 fusion.20
  7.2 1.7 convolution_multiply_fusion.taps
  8.9 0.1 slice.100
  9.0 0.1 slice.101
  9.1 0.6 pad_add_fusion.marks
  9.7 0.8 select_select_fusion.1
  10.5 1.5 pad_maximum_fusion.1.gains
  12.0 31.3 %forward.1 = (bf16[560,768]{1,0:T(8,128)(2,1)}, bf16[512,768]{1,0:T(8,128)(2,1)}, bf16[3,768,768]{2,1,0:T(8,128)(2,1)}, bf16[768,768]{1,0:T(8,128)(2,1)}, bf16[7...) custom-call(s32[64]{0:T(128)} %pad_add_fusion.marks, ...), custom_call_target="tpu_custom_call" | custom-call | tf_op jit(solution)/shard_map/forward/pallas_call | solution.py:414
  43.3 1.3 slice.111.gains
  44.6 116.4 %backward.1 = (f32[48,2304]{1,0:T(8,128)}, f32[48,2304]{1,0:T(8,128)}, f32[40,768]{1,0:T(8,128)}, f32[16,768]{1,0:T(8,128)}, f32[1024,384]{1,0:T(8,128)}, /*index=5*/f32[1024,384]{1,0:T(8,128)}) custom-call(s32[64]{0:T(128)} %pad_add_fusion.marks, bf16[560,768]{1,0:T(8,128)(2,1)} %get-tuple-element.40.tok, f32[640,128]{1,0:T(8,128)} %broadcast_in_dim.269.ids, ...), custom_call_target="tpu_custom_call" | custom-call | tf_op jit(solution)/shard_map/backward/pallas_call | solution.py:1043
  161.0 0.0 copy-start.5
  161.0 0.0 copy-start.4
  161.1 0.0 copy-start.3
  161.1 1.1 reshape.205
  162.2 0.8 reshape.203
  163.1 0.8 slice.121
  164.0 0.6 fusion.12
  164.6 0.1 slice.118
  164.7 0.0 copy-done.5
  164.7 0.3 convolution_multiply_fusion.2
  165.0 0.9 fusion.22
  165.8 0.7 fusion.21
  166.5 0.9 fusion.16
  167.5 0.0 copy-done.4
  167.5 0.1 stack_reshape.6
  167.6 0.0 copy-done.3
  167.6 0.1 stack_reshape.7
  167.7 0.0 copy-start.2
  167.8 0.7 slice.131
  168.5 0.6 slice_bitcast_fusion.1
  169.1 1.0 fusion.1
  170.2 0.6 squeeze.26
  170.8 0.7 slice.129
  171.5 0.7 slice_bitcast_fusion
  172.2 0.0 copy-start.1
  172.2 0.6 reshape.204
  172.9 1.3 slice_reduce_fusion
  174.2 1.3 slice_reduce_fusion.1
  175.6 0.0 copy-done.2
  175.6 1.1 copy.51
  176.7 0.0 copy-done.1
  176.7 1.1 copy.52
  (35 shorter events, 0.4 us)
Async XLA Ops:
  0.6 6.3 %copy-start = (f32[64,64]{1,0:T(8,128)S(1)}, f32[64,64]{1,0:T(8,128)}, u32[]{:S(2)}) copy-start(f32[64,64]{1,0:T(8,128)} %param.24) | copy-start | bytes 49156
  161.0 3.7 %copy-start.5 = (f32[72,768]{1,0:T(8,128)S(1)}, f32[72,768]{1,0:T(8,128)}, u32[]{:S(2)}) copy-start(f32[72,768]{1,0:T(8,128)} %get-tuple-element.45) | copy-start | bytes 663556
  161.0 6.4 %copy-start.4 = (f32[48,2304]{1,0:T(8,128)S(1)}, f32[48,2304]{1,0:T(8,128)}, u32[]{:S(2)}) copy-start(f32[48,2304]{1,0:T(8,128)} %get-tuple-element.61) | copy-start | bytes 1327108
  161.1 6.5 %copy-start.3 = (f32[48,2304]{1,0:T(8,128)S(1)}, f32[48,2304]{1,0:T(8,128)}, u32[]{:S(2)}) copy-start(f32[48,2304]{1,0:T(8,128)} %get-tuple-element.62) | copy-start | bytes 1327108
  167.7 7.9 %copy-start.2 = (f32[1024,384]{1,0:T(8,128)S(1)}, f32[1024,384]{1,0:T(8,128)}, u32[]{:S(2)}) copy-start(f32[1024,384]{1,0:T(8,128)} %get-tuple-element.118) | copy-start | bytes 4718596
  172.2 4.5 %copy-start.1 = (f32[1024,384]{1,0:T(8,128)S(1)}, f32[1024,384]{1,0:T(8,128)}, u32[]{:S(2)}) copy-start(f32[1024,384]{1,0:T(8,128)} %get-tuple-element.119) | copy-start | bytes 4718596

commit v3 on v2

--- a/solution.py
+++ b/solution.py
@@ -38,6 +38,19 @@
     return pl.ds(pl.multiple_of(start, size), size)
 
 
+def filter_layers(table, w1, b1, w2):
+    pre_one = jnp.dot(table, w1, precision=HIGHEST, preferred_element_type=F32) + b1
+    hidden_one = jnp.sin(pre_one)
+    pre_two = jnp.dot(hidden_one, w2, precision=HIGHEST, preferred_element_type=F32)
+    return pre_one, hidden_one, pre_two, jnp.sin(pre_two)
+
+
+def filter_window(start, count, full):
+    channel = (start + lax.broadcasted_iota(jnp.int32, (FIR, count), 1)).astype(F32)
+    place = lax.broadcasted_iota(jnp.int32, (FIR, count), 0).astype(F32)
+    return jnp.exp(-(0.5 + 3.0 * channel / full) * place / FIR)
+
+
 def device_of(index):
     return (index // 2, index % 2)
 
@@ -99,10 +112,11 @@
     return shifted * inverse, inverse
 
 
-def forward_kernel(n, rows, reach, marks, tokens, gout, w_in, w_out, w_up, w_down, gains, head, taps, ids,
+def forward_kernel(n, rows, reach, marks, tokens, gout, w_in, w_out, w_up, w_down, filt_w3, table, filt_w1, filt_b1, filt_w2,
+                   norms_a, norms_b, biases, tails, decays, nus, shorts, ids,
                    tok_o, g_o, in_o, out_o, up_o, down_o, gains_o, vec_o,
                    n1_o, proj_o, x0_o, u_o, heads_o, long_o, car_o, dist_o, rest_o, enter_o,
-                   tok_v, g_v, in_v, out_v, gains_v, vec_v, n1_s, proj_s, u_s, state_s, end_s, slots_s,
+                   tok_v, g_v, in_v, out_v, gains_v, vec_v, gains, head, n1_s, proj_s, u_s, state_s, end_s, slots_s,
                    local_sem, store_sem, send_sem, recv_sem, push_send, push_recv):
     block, full = rows // 2, in_v.shape[1]
     width = full // 2
@@ -114,14 +128,13 @@
     pushing = Pushing(n, reach, False, end_s, slots_s, push_send, push_recv)
     partner = (s, 1 - c)
     cols = pl.ds(pl.multiple_of(c * width, width), width)
-    early = [(gains, gains_v.at[:, cols])]
+    early = [(gains, gains_v.at[pl.ds(0, 8), cols]), (filt_w3, gains_v.at[pl.ds(8, filt_w3.shape[0]), cols])]
     late = []
     for i in range(width // LANES):
         source = pl.ds(i * LANES, LANES)
         paired = pl.ds(pl.multiple_of((2 * i + c) * LANES, LANES), LANES)
         early += [
             (head.at[:, source], vec_v.at[pl.ds(0, HEAD), paired]),
-            (taps.at[:, source], vec_v.at[pl.ds(HEAD, FIR), paired]),
             (w_in.at[:, :, source], in_v.at[:, :, paired]),
         ]
         late.append((w_out.at[source, :], out_v.at[paired, :]))
@@ -175,6 +188,15 @@
             for k in range(2):
                 pl.semaphore_signal(barrier, inc=1, device_id=(s - 1, k), device_id_type=MESH)
 
+        gains[...] = jnp.zeros_like(gains)
+        head[...] = jnp.zeros_like(head)
+        for ref, row, value in ((gains, 0, norms_a), (gains, 1, norms_b), (head, 2, biases), (head, 3, tails),
+                                (head, 4, decays), (head, 5, nus)):
+            ref[row : row + 1, :] = value[...].reshape(1, width)
+        for j in range(3):
+            for t in range(3):
+                head[6 + 3 * j + t : 7 + 3 * j + t, :] = shorts[j, t : t + 1, :]
+
         def begin_own(which):
             for k, (src, dst) in enumerate(keeps[which]):
                 pltpu.make_async_copy(src, dst, local_sem.at[at_tokens + k]).start()
@@ -238,7 +260,8 @@
                         edge(k, partner).wait_recv()
 
         for_core(take_tokens)
-        for (src, dst), k in halves[:1]:
+        hidden_two = filter_layers(table[...], filt_w1[...], filt_b1[...], filt_w2[...])[3]
+        for (src, dst), k in halves[:2]:
             pltpu.make_async_copy(src, dst, local_sem.at[k]).wait()
             remote(src, dst, k).wait()
         store(0).start()
@@ -252,9 +275,16 @@
 
         lax.fori_loop(0, (BEFORE + block) // 80, normed, 0)
         n1_o[...] = n1_s[pl.ds(BEFORE, block), :]
-        for (src, dst), k in halves[1 : len(early)]:
+        for (src, dst), k in halves[2 : len(early)]:
             pltpu.make_async_copy(src, dst, local_sem.at[k]).wait()
             remote(src, dst, k).wait()
+        taps = jnp.dot(hidden_two, gains_v[8:, :], precision=HIGHEST, preferred_element_type=F32)
+        taps *= filter_window(0, full, full)
+        for i in range(width // LANES):
+            for half in range(2):
+                source = half * width + i * LANES
+                vec_v[HEAD : HEAD + FIR, (2 * i + half) * LANES : (2 * i + half + 1) * LANES] = (
+                    taps[:, source : source + LANES])
         store(2).start()
         store(3).start()
 
@@ -392,7 +422,7 @@
             store(k).wait()
 
 
-def forward(n, marks, tokens, gout, w_in, w_out, w_up, w_down, gains, head, taps, ids):
+def forward(n, marks, tokens, gout, w_in, w_out, w_up, w_down, filt_w3, table, filt_w1, filt_b1, filt_w2, vectors, ids):
     rows, width = tokens.shape
     hidden = w_up.shape[1]
     full, block = 2 * width, rows // 2
@@ -405,11 +435,11 @@
     stacked = lambda count, place: pl.BlockSpec((BLOCK // LANES, count, LANES), lambda i: (place(i), 0, 0))
     shape = jax.ShapeDtypeStruct
     vmem = pltpu.VMEM
-    far = 1 + 4 * (width // LANES) + 2 + 4
+    far = 2 + 3 * (width // LANES) + 2 + 4
     dma = pltpu.SemaphoreType.DMA
     landing = [
         ((window, full), BF16), ((block, full), BF16), ((3, full, full), BF16), ((full, full), BF16),
-        ((gains.shape[0], full), F32), ((HEAD + FIR, full), F32),
+        ((8 + filt_w3.shape[0], full), F32), ((HEAD + FIR, full), F32),
     ]
     return pl.pallas_call(
         functools.partial(forward_kernel, n, rows, reach),
@@ -431,7 +461,8 @@
             shape((block, LANES), F32),
             shape((1, full), F32),
         ),
-        in_specs=[pl.BlockSpec(memory_space=pltpu.SMEM)] + [anywhere] * 9 + [whole(*ids.shape)],
+        in_specs=[pl.BlockSpec(memory_space=pltpu.SMEM)] + [anywhere] * 7 + [
+            whole(*part.shape) for part in (table, filt_w1, filt_b1, filt_w2, *vectors, ids)],
         out_specs=(
             *[anywhere] * 8,
             whole(block, full),
@@ -447,6 +478,8 @@
         ),
         scratch_shapes=[
             *[vmem(*part) for part in landing],
+            vmem((8, width), F32),
+            vmem((HEAD, width), F32),
             vmem((window, full), BF16),
             vmem((3, BLOCK // LANES, window, LANES), F32),
             vmem((lane_blocks, window, LANES), F32),
@@ -456,7 +489,7 @@
             dma((far,)), dma((6,)), dma((far,)), dma((far,)), dma((reach,)), dma((reach,)),
         ],
         compiler_params=pltpu.CompilerParams(collective_id=0, has_side_effects=True, vmem_limit_bytes=VMEM_LIMIT),
-    )(marks, tokens, gout, w_in, w_out, w_up, w_down, gains, head, taps, ids)
+    )(marks, tokens, gout, w_in, w_out, w_up, w_down, filt_w3, table, filt_w1, filt_b1, filt_w2, *vectors, ids)
 
 
 TILE = 512
@@ -1088,6 +1121,80 @@
     return *parts, small_a, small_b, swap(out), swap(gtok)
 
 
+def finish_kernel(part_a, part_b, small_a, small_b, gains, vec, table, w1, b1, w2, out, gtok,
+                  out_o, gtok_o, gain_one_o, in_o, short_o, w1_o, b1_o, w2_o, w3_o, bias_o, tgain_o, trate_o,
+                  outw_o, gain_two_o, up_o, down_o, out_v, gtok_v, sem):
+    full = gains.shape[1]
+    width, hidden = full // 2, up_o.shape[1]
+    loads = [pltpu.make_async_copy(src, dst, sem.at[k]) for k, (src, dst) in enumerate(((out, out_v), (gtok, gtok_v)))]
+    saves = [pltpu.make_async_copy(src, dst, sem.at[2 + k]) for k, (src, dst) in enumerate(((out_v, out_o), (gtok_v, gtok_o)))]
+    for copy in loads:
+        copy.start()
+
+    def natural(rows):
+        blocks = [rows[:, b * LANES : (b + 1) * LANES] for b in range(full // LANES)]
+        return jnp.concatenate(blocks[0::2] + blocks[1::2], axis=1)
+
+    raw = natural(small_a[0:FIR, :]) * filter_window(0, full, full)
+    pre_one, hidden_one, pre_two, hidden_two = filter_layers(table[...], w1[...], b1[...], w2[...])
+
+    def exact(left, right, dims):
+        return lax.dot_general(left, right, (dims, ((), ())), precision=HIGHEST, preferred_element_type=F32)
+
+    w3_o[...] = exact(hidden_two, raw, ((0,), (0,)))
+    pre_two_grad = exact(raw, gains[8:, :], ((1,), (1,))) * jnp.cos(pre_two)
+    w2_o[...] = exact(hidden_one, pre_two_grad, ((0,), (0,)))
+    pre_one_grad = exact(pre_two_grad, w2[...], ((1,), (1,))) * jnp.cos(pre_one)
+    w1_o[...] = exact(table[...], pre_one_grad, ((0,), (0,)))
+    b1_o[...] = jnp.sum(pre_one_grad, axis=0, keepdims=True).reshape(b1_o.shape)
+
+    for copy, following in zip(loads, saves):
+        copy.wait()
+        following.start()
+
+    gain_one_o[...] = small_b[10:11, :].reshape(full)
+    gain_two_o[...] = small_a[FIR : FIR + 1, :].reshape(full)
+    bias_o[...] = natural(small_a[FIR + 1 : FIR + 2, :]).reshape(full)
+    long_car, rate, nu = small_a[FIR + 2 : FIR + 3, :], vec[4:5, :], vec[5:6, :]
+    factor = jnp.exp(-rate)
+    tgain_o[...] = natural(nu * long_car).reshape(full)
+    trate_o[...] = natural(vec[3:4, :] * long_car * factor * factor / nu - small_b[9:10, :]).reshape(full)
+    short = natural(small_b[0:9, :])
+    for j in range(3):
+        for s in range(3):
+            short_o[j, s : s + 1, :] = short[3 * j + s : 3 * j + s + 1, :]
+    up_o[...] = part_a[:, 0:hidden]
+    down_o[...] = part_b[:, 0:hidden]
+    for i in range(width // LANES):
+        at, lanes = hidden + i * PART, slice(i * LANES, (i + 1) * LANES)
+        for s, (ref, start) in enumerate(((part_a, at), (part_a, at + LANES), (part_b, at))):
+            in_o[s, :, lanes] = ref[:, start : start + LANES]
+        outw_o[:, lanes] = part_b[:, at + LANES : at + 2 * LANES]
+    for copy in saves:
+        copy.wait()
+
+
+def finish(part_a, part_b, small_a, small_b, gains, vec, table, w1, b1, w2, out, gtok):
+    full, rows = gains.shape[1], part_a.shape[0]
+    width, hidden = full // 2, part_a.shape[1] - full // 2 // LANES * PART
+    shape = jax.ShapeDtypeStruct
+    vmem, anywhere = pl.BlockSpec(memory_space=pltpu.VMEM), pl.BlockSpec(memory_space=pl.ANY)
+    vector = shape((full,), F32)
+    return pl.pallas_call(
+        finish_kernel,
+        name="finish",
+        out_shape=(
+            shape(out.shape, F32), shape(gtok.shape, F32), vector, shape((3, rows, width), F32), shape((3, 3, full), F32),
+            shape(w1.shape, F32), shape((b1.shape[1],), F32), shape(w2.shape, F32), shape((w2.shape[0], full), F32),
+            vector, vector, vector, shape((rows, width), F32), vector, shape((rows, hidden), F32), shape((rows, hidden), F32),
+        ),
+        in_specs=[vmem] * 10 + [anywhere] * 2,
+        out_specs=(anywhere, anywhere) + (vmem,) * 14,
+        scratch_shapes=[pltpu.VMEM(out.shape, F32), pltpu.VMEM(gtok.shape, F32), pltpu.SemaphoreType.DMA((4,))],
+        compiler_params=pltpu.CompilerParams(vmem_limit_bytes=VMEM_LIMIT),
+    )(part_a, part_b, small_a, small_b, gains, vec, table, w1, b1, w2, out, gtok)
+
+
 def on_device(tokens, seg_ids, norm1_gain, in_weight, short_weight, filt_w1, filt_b1, filt_w2, filt_w3,
               long_bias, tail_gain, tail_rate, out_weight, norm2_gain, up_weight, down_weight, grad_out):
     rows, width = tokens.shape
@@ -1105,82 +1212,29 @@
     window = near
     ids = jnp.broadcast_to(window.astype(F32)[:, None], (window.shape[0], LANES))
 
-    channel_start = lax.axis_index("ch") * width
-    pos_table = position_table(FIR, (filt_w1.shape[0] - 1) // 2)
-    pre_one = jnp.dot(pos_table, filt_w1, precision=HIGHEST) + filt_b1
-    hidden_one = jnp.sin(pre_one)
-    pre_two = jnp.dot(hidden_one, filt_w2, precision=HIGHEST)
-    hidden_two = jnp.sin(pre_two)
-    channel = channel_start.astype(F32) + jnp.arange(width, dtype=F32)
-    window_of = lambda channels: jnp.exp(
-        -(0.5 + 3.0 * channels / full)[None, :] * jnp.arange(FIR, dtype=F32)[:, None] / FIR)
-    taps = jnp.dot(hidden_two, filt_w3, precision=HIGHEST) * window_of(channel)
+    table = position_table(FIR, (filt_w1.shape[0] - 1) // 2)
     norm_tail = jnp.sqrt(-jnp.expm1(-2.0 * tail_rate))
-    def rows_in(count, parts):
-        index = jnp.arange(count)[:, None]
-        rows = jnp.zeros((count, width), F32)
-        for k, part in enumerate(parts):
-            rows = jnp.where(index == k, part[None, :], rows)
-        return rows
-
-    gains = jnp.concatenate([rows_in(8, [norm1_gain, norm2_gain]), filt_w3])
-    zeros = jnp.zeros((width,), F32)
-    head = rows_in(HEAD, [zeros, zeros, long_bias, tail_gain, tail_rate, norm_tail] + [
-        short_weight[j, s] for j in range(3) for s in range(3)])
-
+    vectors = (norm1_gain, norm2_gain, long_bias, tail_gain, tail_rate, norm_tail, short_weight)
+    filt_b1 = filt_b1[None, :]
     marks = jnp.concatenate([keys[::block], keys[block - 1 :: block]])
     (tok, g, win, wout, up_other, down_other, gains, vec, n1, proj, x0, u, heads, base, car, dist, rest, enter) = forward(
         n, marks, tokens, grad_out, jnp.transpose(in_weight, (1, 0, 2)), out_weight, up_weight, down_weight,
-        gains, head, taps, ids)
+        filt_w3, table, filt_w1, filt_b1, filt_w2, vectors, ids)
 
     summed = n == 16
     results = backward(
-        n, summed, marks, tok, ids, dist, rest, enter, g, gains[:8], vec, wout, x0, base, car, u, n1, heads,
+        n, summed, marks, tok, ids, dist, rest, enter, g, gains, vec, wout, x0, base, car, u, n1, heads,
         (up_weight, up_other), (down_weight, down_other), win, proj)
     if not summed:
         results = reduce_plain(n, *results[:5])
     part_a, part_b, small_a, small_b, out, gtok = results
 
-    def natural(paired):
-        count = paired.shape[0]
-        return jnp.transpose(paired.reshape(count, -1, 2, LANES), (0, 2, 1, 3)).reshape(count, full)
-
-    small_a, gain_two = natural(small_a), small_a[FIR]
-    small_b, gain_one = natural(small_b), small_b[10]
-    taps_grad, bias_grad, long_car = small_a[:FIR], small_a[FIR + 1], small_a[FIR + 2]
-    short_grad, carried_q = small_b[:9].reshape(3, 3, full), small_b[9]
-    vec = natural(vec[:HEAD])
-    gain, rate, nu = vec[3], vec[4], vec[5]
-    factor = jnp.exp(-rate)
-    rate_grad = gain * long_car * factor * factor / nu - carried_q
-    raw_grad = taps_grad * window_of(jnp.arange(full, dtype=F32))
-    w3_grad = jnp.dot(hidden_two.T, raw_grad, precision=HIGHEST)
-    pre_two_grad = jnp.dot(raw_grad, gains[8:].T, precision=HIGHEST) * jnp.cos(pre_two)
-    w2_grad = jnp.dot(hidden_one.T, pre_two_grad, precision=HIGHEST)
-    pre_one_grad = jnp.dot(pre_two_grad, filt_w2.T, precision=HIGHEST) * jnp.cos(pre_one)
-    w1_grad = jnp.dot(pos_table.T, pre_one_grad, precision=HIGHEST)
-    hidden = up_weight.shape[1]
-    rows_out = part_a.shape[0]
-    mixer_grads = jnp.stack([part[:, hidden:].reshape(rows_out, -1, 2, LANES) for part in (part_a, part_b)], axis=2)
-    mixer_grads = mixer_grads.reshape(rows_out, -1, 4, LANES)
-    mixer_grads = jnp.transpose(mixer_grads, (0, 2, 1, 3)).reshape(rows_out, 4, width)
+    (out, gtok, gain_one, in_grad, short_grad, w1_grad, b1_grad, w2_grad, w3_grad, bias_grad, tail_gain_grad, rate_grad,
+     out_grad, gain_two, up_grad, down_grad) = finish(
+        part_a, part_b, small_a, small_b, gains, vec, table, filt_w1, filt_b1, filt_w2, out, gtok)
     return (
-        out,
-        gtok,
-        gain_one,
-        mixer_grads[:, :3],
-        short_grad,
-        w1_grad,
-        jnp.sum(pre_one_grad, axis=0),
-        w2_grad,
-        w3_grad,
-        bias_grad,
-        nu * long_car,
-        rate_grad,
-        mixer_grads[:, 3].T,
-        gain_two,
-        part_a[:, :hidden],
-        part_b[:, :hidden].T,
+        out, gtok, gain_one, jnp.transpose(in_grad, (1, 0, 2)), short_grad, w1_grad, b1_grad, w2_grad, w3_grad, bias_grad,
+        tail_gain_grad, rate_grad, out_grad.T, gain_two, up_grad, down_grad.T,
     )
 
 

time: 179 us -> 160 us (0.89)
  local copies, waits for them, and re-layouts: 15.6 us -> 1.21 us
  matrix products: 6.72 us -> 0 us
  Pallas kernels: 148 us -> 154 us
  other arithmetic: 6.83 us -> 3.66 us
    slice x14 -> x0, local copies, waits for them, and re-layouts: 7.28 us -> none  [the longest x1 1.35 us: on_device(): gains[:8]]
    dot_general x8 -> x0, matrix products: 6.72 us -> none  [the longest x1 1.7 us: on_device(): taps = jnp.dot(hidden_two, filt_w3, precision=HIGHEST) * window_of(channel)]
    pallas_call x0 -> x1, Pallas kernels: none -> 5.61 us  [finish(): pl.pallas_call(finish_kernel, name='finish', out_shape=(shape(out.shape,...]
    reshape x8 -> x0, local copies, waits for them, and re-layouts: 2.65 us -> none  [the longest x6 1.99 us: natural(): paired.reshape(count, -1, 2, LANES)]
    unnamed x14 -> x0, local copies, waits for them, and re-layouts: 2.32 us -> none
    select_n x2 -> x0, other arithmetic: 2.2 us -> none  [rows_in(): rows = jnp.where(index == k, part[None, :], rows)]
where the time goes in v3:
time: 160 us; the launch traced here: 159 us
  Pallas kernels  154 us (96%)
  other arithmetic  3.66 us (2%)
    pallas_call x1, Pallas kernels, backward(): pl.pallas_call(functools.partial(backward_kernel, n, block, reach, summed...  117 us
    pallas_call x1, Pallas kernels, forward(): pl.pallas_call(functools.partial(forward_kernel, n, rows, reach), name='f...  31.3 us
    pallas_call x1, Pallas kernels, finish(): pl.pallas_call(finish_kernel, name='finish', out_shape=(shape(out.shape,...  5.61 us

profile of v3, /device:TPU:0, one launch (start us, length us, event | category | flops | bytes accessed | tf_op | source)
XLA Modules:
  0.0 159.4 jit_solution(13924604146594183071)
XLA Ops:
  0.7 1.3 negate_sqrt_fusion.nus
  2.0 0.1 multiply_cosine_fusion
  2.1 0.7 pad_maximum_fusion.table
  2.8 0.9 fusion.1
  3.7 0.1 slice.7
  3.8 0.1 slice.6
  3.9 0.6 pad_add_fusion.marks
  4.5 0.1 concatenate.11
  4.6 0.1 dynamic-slice_convert_fusion
  4.7 0.9 broadcast_in_dim.21.ids
  5.6 31.3 %forward.1 = (bf16[560,768]{1,0:T(8,128)(2,1)}, bf16[512,768]{1,0:T(8,128)(2,1)}, bf16[3,768,768]{2,1,0:T(8,128)(2,1)}, bf16[768,768]{1,0:T(8,128)(2,1)}, bf16[7...) custom-call(s32[64]{0:T(128)} %pad_add_fusion.marks, ...), custom_call_target="tpu_custom_call" | custom-call | tf_op jit(solution)/shard_map/forward/pallas_call | solution.py:444
  36.9 116.9 %backward.1 = (f32[48,2304]{1,0:T(8,128)}, f32[48,2304]{1,0:T(8,128)}, f32[40,768]{1,0:T(8,128)}, f32[16,768]{1,0:T(8,128)}, f32[1024,384]{1,0:T(8,128)}, /*index=5*/f32[1024,384]{1,0:T(8,128)}) custom-call(s32[64]{0:T(128)} %pad_add_fusion.marks, bf16[560,768]{1,0:T(8,128)(2,1)} %get-tuple-element.56.tok, f32[640,128]{1,0:T(8,128)} %broadcast_in_dim.21.ids, ...), custom_call_target="tpu_custom_call" | custom-call | tf_op jit(solution)/shard_map/backward/pallas_call | solution.py:1076
  153.8 5.6 %finish.1 = (f32[1024,384]{1,0:T(8,128)}, f32[1024,384]{1,0:T(8,128)}, f32[768]{0:T(1024)}, f32[3,48,384]{2,1,0:T(8,128)}, f32[3,3,768]{2,1,0:T(4,128)}, /*index...) custom-call(f32[48,2304]{1,0:T(8,128)} %get-tuple-element.74.part_a,, ...), custom_call_target="tpu_custom_call" | custom-call | tf_op jit(solution)/shard_map/finish/pallas_call | solution.py:1183
  (5 shorter events, 0.0 us)

commit v4 on v3

--- a/solution.py
+++ b/solution.py
@@ -495,30 +495,32 @@
 TILE = 512
 PART = TILE // 2
 STAGES = 5
+FEED_ORDERS = ((0, 1, 2, 3), (0, 2, 3, 1), (1, 0, 2, 3), (1, 2, 3, 0))
+MIX_ORDERS = ((0, 1, 2, 3), (1, 0, 2, 3), (2, 0, 1, 3))
 
 
 class Summing:
     def __init__(self, slots, rows, staged, first, second, third, fourth, fifth, send_sem, recv_sem):
         self.slots, self.rows, self.staged = slots, rows, staged
-        self.first, self.second, self.third, self.fourth, self.fifth = first, second, third, fourth, fifth
+        self.held = (first, second, third, fourth, fifth)
         self.send_sem, self.recv_sem = send_sem, recv_sem
         self.s, self.c = lax.axis_index("seq"), lax.axis_index("ch")
         self.bits = [(self.s // (1 << b)) % 2 for b in range(4)]
         self.peers = [(self.s + (1 - 2 * bit) * (1 << b), self.c) for b, bit in enumerate(self.bits)]
         self.partner = (self.s, 1 - self.c)
-        self.order = ((0, 1, 2, 3), (1, 0, 2, 3))
 
     @staticmethod
     def scratch(tiles, slots, rows):
+        parts = len(FEED_ORDERS)
         return [
-            pltpu.VMEM((2, 2, 2, 2, 2, 2, rows, TILE), BF16),
-            pltpu.VMEM((slots, 2, 2, 2, 2, rows, TILE), BF16),
-            pltpu.VMEM((slots, 2, 2, 2, 2, rows, PART), BF16),
-            pltpu.VMEM((slots, 2, 2, 2, rows, PART), BF16),
-            pltpu.VMEM((slots, 2, 2, rows, PART), BF16),
-            pltpu.VMEM((slots, 2, rows, PART), BF16),
-            pltpu.SemaphoreType.DMA((tiles, 1 + 2 * 4)),
-            pltpu.SemaphoreType.DMA((tiles, 1 + 2 * 4)),
+            pltpu.VMEM((2, 2, parts, 2, 2, 2, 2, rows, LANES), BF16),
+            pltpu.VMEM((slots, parts, 2, 2, 2, 2, rows, LANES), BF16),
+            pltpu.VMEM((slots, parts, 2, 2, 2, rows, LANES), BF16),
+            pltpu.VMEM((slots, parts, 2, 2, rows, LANES), BF16),
+            pltpu.VMEM((slots, parts, 2, rows, LANES), BF16),
+            pltpu.VMEM((slots, parts, rows, LANES), BF16),
+            pltpu.SemaphoreType.DMA((tiles, 1 + 4 * parts)),
+            pltpu.SemaphoreType.DMA((tiles, 1 + 4 * parts)),
         ]
 
     def greet(self, barrier):
@@ -530,67 +532,52 @@
             src_ref=src, dst_ref=dst, send_sem=self.send_sem.at[tile, k], recv_sem=self.recv_sem.at[tile, k],
             device_id=target, device_id_type=MESH)
 
-    def copies(self, tile, stage):
+    def stage_in(self, tile, whose, part, order, grad):
+        for q in range(16):
+            at = [(q >> bit) & 1 for bit in order]
+            self.staged[(tile % 2, whose, part, *at)] = grad[q * self.rows : (q + 1) * self.rows]
+
+    def copies(self, tile, stage, orders):
         slot = tile % self.slots
         if stage == 0:
-            return [self.remote(self.staged.at[tile % 2, 1], self.first.at[slot], tile, 0, self.partner)]
+            parts = pl.ds(0, len(orders))
+            return [self.remote(self.staged.at[tile % 2, 1, parts], self.held[0].at[slot, parts], tile, 0, self.partner)]
         result = []
-        for part in range(2):
-            bit = self.order[part][stage - 1]
-            away = 1 - self.bits[bit]
-            at = pl.ds(part * PART, PART)
-            if stage == 1:
-                src = self.first.at[slot, :, :, :, away, :, at] if part == 0 else self.first.at[slot, :, :, away, :, :, at]
-                dst = self.second.at[slot, part]
-            elif stage == 2:
-                src, dst = self.second.at[slot, part, :, :, away], self.third.at[slot, part]
-            elif stage == 3:
-                src, dst = self.third.at[slot, part, :, away], self.fourth.at[slot, part]
-            else:
-                src, dst = self.fourth.at[slot, part, away], self.fifth.at[slot, part]
-            result.append(self.remote(src, dst, tile, 1 + 2 * (stage - 1) + part, self.peers[bit]))
+        for part, order in enumerate(orders):
+            bit = order[stage - 1]
+            src, dst = self.held[stage - 1].at[slot, part, 1 - self.bits[bit]], self.held[stage].at[slot, part]
+            result.append(self.remote(src, dst, tile, 1 + 4 * (stage - 1) + part, self.peers[bit]))
         return result
 
-    def start(self, tile, stage):
-        for copy in self.copies(tile, stage):
+    def start(self, tile, stage, orders):
+        for copy in self.copies(tile, stage, orders):
             copy.start()
 
-    def advance(self, tile, stage, total):
-        for copy in self.copies(tile, stage):
+    def advance(self, tile, stage, orders, total):
+        for copy in self.copies(tile, stage, orders):
             copy.wait()
-        x, y, low, high = self.bits
         slot = tile % self.slots
         if stage == 0:
-            def add(i, _):
-                for h in range(2):
-                    for j in range(2):
-                        for k in range(2):
-                            self.first[slot, h, i, j, k] += self.staged[tile % 2, 0, h, i, j, k]
+
+            def add(part, _):
+                for q in range(16):
+                    at = (q >> 3, q >> 2 & 1, q >> 1 & 1, q & 1)
+                    self.held[0][(slot, part, *at)] += self.staged[(tile % 2, 0, part, *at)]
                 return 0
-            lax.fori_loop(0, 2, add, 0)
-        elif stage == 1:
-            def add(i, _):
-                for h in range(2):
-                    for k in range(2):
-                        self.second[slot, 0, h, i, k] += self.first[slot, h, i, k, x, :, 0:PART]
-                        self.second[slot, 1, h, i, k] += self.first[slot, h, i, y, k, :, PART:TILE]
-                return 0
-            lax.fori_loop(0, 2, add, 0)
-        elif stage == 2:
-            for i in range(2):
-                for k in range(2):
-                    self.third[slot, 0, i, k] += self.second[slot, 0, i, k, y]
-                    self.third[slot, 1, i, k] += self.second[slot, 1, i, k, x]
-        elif stage == 3:
-            for part in range(2):
-                for i in range(2):
-                    self.fourth[slot, part, i] += self.third[slot, part, i, low]
+
+            lax.fori_loop(0, len(orders), add, 0)
         else:
-            for part in range(2):
-                mine = self.fourth[slot, part, high].astype(F32)
-                total(tile, part, mine + self.fifth[slot, part].astype(F32))
-            return
-        self.start(tile, stage + 1)
+            for part, order in enumerate(orders):
+                mine = self.bits[order[stage - 1]]
+                for e in range(1 << (4 - stage)):
+                    inner = [(e >> (3 - stage - k)) & 1 for k in range(4 - stage)]
+                    source = self.held[stage - 1][(slot, part, mine, *inner)]
+                    if stage == STAGES - 1:
+                        total(tile, part, source.astype(F32) + self.held[stage][slot, part].astype(F32))
+                    else:
+                        self.held[stage][(slot, part, *inner)] += source
+        if stage < STAGES - 1:
+            self.start(tile, stage + 1, orders)
 
 
 class Joining:
@@ -615,7 +602,7 @@
         self.copy(stage).wait()
         total = self.held[stage] + self.arrived[stage]
         if stage == STAGES - 1:
-            result[...] = total
+            result(total)
         else:
             self.held[stage + 1] = total
             self.start(stage + 1)
@@ -641,11 +628,7 @@
     width, lane_blocks = full // 2, full // LANES
     steps = full // BLOCK
     last_back = BACK + steps - 1
-    outs, refs = refs[:6], refs[6:]
-    if summed:
-        part_a, part_b, small_a, small_b, out_full, gtok_full = outs
-    else:
-        grads_o, small_a, small_b, out_o, gtok_o, _ = outs
+    (grads_o, small_a, small_b, out_o, gtok_o), refs = refs[:5], refs[5:]
     (mixed_s, middle_s, n2_s, gn_s, gout_s, out_s, gmid_s, long_s, car_s, glong_s, q_s, gc_s, gp_s, proj_s,
      taps_s, first_s, slots_s, joined_s, halo_s, halo_r, head_s,
      push_send, push_recv, halo_sem, *buffers) = refs
@@ -657,7 +640,12 @@
     lanes_of = lambda b: pl.ds(pl.multiple_of(b * LANES, LANES), LANES)
     if summed:
         sums = Summing(TILES, full // 16, *buffers[:8])
-        joins = [(Joining(sums, *buffers[8:12]), small_a, TAPS), (Joining(sums, *buffers[12:16]), small_b, last_back)]
+        held_b = buffers[12]
+        joins = [(Joining(sums, *buffers[8:12]), lambda value: small_a.__setitem__(Ellipsis, value), TAPS)]
+        for k in range(steps):
+            at = slice(k * BLOCK, (k + 1) * BLOCK)
+            joins.append((Joining(sums, *[ref.at[k] for ref in buffers[12:16]]),
+                          lambda value, at=at: small_b.__setitem__((slice(None), at), value), BACK + k))
         local_sem, exchange_send, exchange_recv = buffers[16:]
 
         def shares(k, src, dst):
@@ -713,68 +701,53 @@
         lax.fori_loop(0, groups, norm, 0)
         pushing.await_greetings(barrier, 5 if summed else 0)
 
-    if summed:
-
-        def total(tile, part, value):
-            (part_a, part_b)[part][:, pl.ds(pl.multiple_of(tile * PART, PART), PART)] = value
-
-        for stage in range(STAGES - 1, -1, -1):
-            since, early = step - 1 - stage, step - LAGS[stage]
-            is_late = step // (BACK + 1 + stage)
-
-            @pl.when(((early >= 0) & (early < TILES)) | ((since >= BACK) & (since <= last_back)))
-            def _():
-                sums.advance(early + (since - (BACK - TILES) - early) * is_late, stage, total)
-
-            for join, result, begun in joins:
-
-                @pl.when(since == begun)
-                def _():
-                    join.advance(stage, result)
-
-    def put(tile, start, grad):
-        size = grad[0].shape[1]
-        at = pl.ds(start, size)
+    def put(tile, part, grad):
         for half in range(2):
             if summed:
-                whose = (half + c) % 2
-                for q in range(16):
-                    sums.staged[tile % 2, whose, q // 8, q // 4 % 2, q // 2 % 2, q % 2, :, at] = (
-                        grad[half][q * sums.rows : (q + 1) * sums.rows])
+                sums.stage_in(tile, (half + c) % 2, part, MIX_ORDERS[part], grad[half])
             else:
-                grads_o[0, half, :, at] = grad[half]
+                grads_o[0, half, :, part * LANES : (part + 1) * LANES] = grad[half]
+
+    def note(row, i, lanes, value):
+        if summed:
+            held_b[i, 0, row : row + 1, lanes] = value
+        else:
+            at = pl.ds(pl.multiple_of(i * BLOCK + lanes.start, LANES), lanes.stop - lanes.start)
+            small_b[row : row + 1, at] = value
+
+    def feed(half, wup, wdn):
+        n2, rows = n2_s[...], g[...]
+        up = jnp.dot(n2, wup[...], preferred_element_type=F32)
+        pulled = contract(rows, wdn[...], ((1,), (1,)))
+        square = up * up
+        inner = ROOT_TWO_OVER_PI * up * (1.0 + 0.044715 * square)
+        bent = jnp.tanh(inner)
+        part = 0.5 * (1.0 + bent)
+        active = (up * part).astype(BF16)
+        slope = part + (0.5 * ROOT_TWO_OVER_PI) * up * (1.0 - bent * bent) * (1.0 + 0.134145 * square)
+        g_up = (pulled * slope).astype(BF16)
+        out_s[...] += jnp.dot(active, wdn[...], preferred_element_type=F32)
+        gn_s[...] += contract(g_up, wup[...], ((1,), (1,)))
+        pair = (contract(n2, g_up, ((0,), (0,))).astype(BF16), contract(rows, active, ((0,), (0,))).astype(BF16))
+        for k in range(2):
+            if summed:
+                for j in range(2):
+                    columns = pair[k][:, j * LANES : (j + 1) * LANES]
+                    sums.stage_in(step, half, 2 * k + j, FEED_ORDERS[2 * k + j], columns)
+            else:
+                grads_o[0, (half + c) % 2, :, k * PART : (k + 1) * PART] = pair[k]
+
+    row_id = lax.broadcasted_iota(jnp.int32, (8, LANES), 0)
+    zero = jnp.zeros((8, LANES), F32)
 
     @pl.when(step < TILES)
     def _():
-        for half, (wup, wdn) in enumerate(((wup_a, wdn_a), (wup_b, wdn_b))):
-            n2, rows = n2_s[...], g[...]
-            up = jnp.dot(n2, wup[...], preferred_element_type=F32)
-            pulled = contract(rows, wdn[...], ((1,), (1,)))
-            square = up * up
-            inner = ROOT_TWO_OVER_PI * up * (1.0 + 0.044715 * square)
-            bent = jnp.tanh(inner)
-            part = 0.5 * (1.0 + bent)
-            active = (up * part).astype(BF16)
-            slope = part + (0.5 * ROOT_TWO_OVER_PI) * up * (1.0 - bent * bent) * (1.0 + 0.134145 * square)
-            g_up = (pulled * slope).astype(BF16)
-            out_s[...] += jnp.dot(active, wdn[...], preferred_element_type=F32)
-            gn_s[...] += contract(g_up, wup[...], ((1,), (1,)))
-            pair = (contract(n2, g_up, ((0,), (0,))).astype(BF16), contract(rows, active, ((0,), (0,))).astype(BF16))
-            for k in range(2):
-                at = pl.ds(k * PART, PART)
-                if summed:
-                    for q in range(16):
-                        sums.staged[step % 2, half, q // 8, q // 4 % 2, q // 2 % 2, q % 2, :, at] = (
-                            pair[k][q * sums.rows : (q + 1) * sums.rows])
-                else:
-                    grads_o[0, (half + c) % 2, :, at] = pair[k]
+        feed(0, wup_a, wdn_a)
+
+    @pl.when(step == EPILOGUE)
+    def _():
         if summed:
-            sums.start(step, 0)
-
-    @pl.when(step == EPILOGUE)
-    def _():
-        if summed:
-            for copy in shares(0, out_s, out_full):
+            for copy in shares(0, out_s, out_o):
                 copy.start()
         else:
             out_o[...] = out_s[...]
@@ -804,84 +777,11 @@
                 glong_s[b, 0:block, :] = part * x0[b]
                 long_s[b] = part * long_s[b]
 
-    row_id = lax.broadcasted_iota(jnp.int32, (8, LANES), 0)
-    zero = jnp.zeros((8, LANES), F32)
-
-    @pl.when(step == GATE)
-    def _():
-        rates = [vec[4:5, b * LANES : (b + 1) * LANES] for b in range(lane_blocks)]
-        tails = [vec[3:4, b * LANES : (b + 1) * LANES] * vec[5:6, b * LANES : (b + 1) * LANES] for b in range(lane_blocks)]
-        lams = [[jnp.exp(-rate * float(k)) for k in (1, 2, 4)] for rate in rates]
-        powers = [jnp.exp(-rate * (8 - row_id).astype(F32)) for rate in rates]
-
-        def scan_group(i, carry):
-            at = block // 8 - 1 - i
-            to = pl.ds(pl.multiple_of(at * 8, 8), 8)
-            start = pl.multiple_of(BEFORE + at * 8, 8)
-            own = ids[pl.ds(start, 8), :]
-            masks = [(own == ids[pl.ds(start + k, 8), :]) & (row_id < 8 - k) for k in (1, 2, 4)]
-            joined = own == jnp.broadcast_to(ids[pl.ds(start + 8, 1), :], (8, LANES))
-            states, biases, carries = [], [], []
-            for b in range(lane_blocks):
-                grad = glong_s[b, to, :]
-                value = grad * tails[b]
-                for mask, lam, k in zip(masks, lams[b], (1, 2, 4)):
-                    value += jnp.where(mask, lam * pltpu.roll(value, 8 - k, 0), 0.0)
-                value += jnp.where(joined, powers[b] * carry[0][b], 0.0)
-                q_s[b, to, :] = value
-                states.append(jnp.broadcast_to(value[0:1, :], (8, LANES)))
-                biases.append(carry[1][b] + grad * u[b, pl.ds(start, 8), :])
-                carries.append(carry[2][b] + grad * car_s[b, to, :])
-            return tuple(states), tuple(biases), tuple(carries)
-
-        many = (zero,) * lane_blocks
-        states, biases, carries = lax.fori_loop(0, block // 8, scan_group, (many, many, many), unroll=2)
-        for b in range(lane_blocks):
-            lanes = slice(b * LANES, (b + 1) * LANES)
-            first_s[:, lanes] = states[b][0:1, :]
-            head_s[1:2, lanes] = jnp.sum(biases[b], axis=0, keepdims=True)
-            head_s[2:3, lanes] = jnp.sum(carries[b], axis=0, keepdims=True)
-            halo_s[0:48, lanes] = glong_s[b, 0:48, :]
-            halo_s[48:56, lanes] = q_s[b, 0:8, :]
-            halo_s[72:80, lanes] = long_s[b, 0:8, :]
-        halo_s[56:72, :] = heads[...]
-        pushing.start()
-
-        @pl.when(pushing.me > 0)
-        def _():
-            halo_copy.start()
-
-    @pl.when(step == TAPS)
-    def _():
-        taps_s[...] = jnp.zeros_like(taps_s)
-
-        def pairs(p, _):
-            def chunk(j, _):
-                at = pl.ds(pl.multiple_of(j * 32, 32), 32)
-                start = BEFORE + j * 32
-                near = dist_s[at, :]
-                here = [glong_s[2 * p + k, at, :] for k in range(2)]
-                for tap in range(FIR):
-                    same = near >= float(tap)
-                    for k in range(2):
-                        term = jnp.where(same, here[k] * u[2 * p + k, pl.ds(start - tap, 32), :], 0.0)
-                        taps_s[2 * p + k, tap] += jnp.sum(term.reshape(4, 8, LANES), axis=0)
-                return 0
-
-            lax.fori_loop(0, groups, chunk, 0)
-            return 0
-
-        lax.fori_loop(0, lane_blocks // 2, pairs, 0)
-        result = joins[0][0].held.at[0] if summed else small_a
-        for b in range(lane_blocks):
-            lanes = slice(b * LANES, (b + 1) * LANES)
-            result[0:FIR, lanes] = jnp.sum(taps_s[b], axis=1)
-        result[FIR : FIR + 8, :] = head_s[...]
-        if summed:
-            joins[0][0].start(0)
-
     @pl.when(step == BACK)
     def _():
+        for i in range(steps):
+            for row in range(10, 16):
+                note(row, i, slice(0, BLOCK), jnp.zeros((1, BLOCK), F32))
         joined_s[...] = jnp.zeros_like(joined_s)
         rate = vec[4:5, :]
         following = 2 * n + jnp.minimum(pushing.me + 1, 2 * n - 1)
@@ -953,7 +853,129 @@
             return tuple(result)
 
         crossed = lax.fori_loop(0, groups, chunk, (zero, zero))
-
+        for k in two:
+            note(9, i, slice(k * LANES, (k + 1) * LANES), jnp.sum(crossed[k], axis=0, keepdims=True))
+
+    if summed:
+
+        def fed(tile, part, value):
+            grads_o[:, pl.ds(pl.multiple_of(tile * TILE + part * LANES, LANES), LANES)] = value
+
+        def mixed(tile, part, value):
+            at = TILES * TILE + (tile - TILES) * len(MIX_ORDERS) * LANES + part * LANES
+            grads_o[:, pl.ds(pl.multiple_of(at, LANES), LANES)] = value
+
+        for stage in range(STAGES - 1, -1, -1):
+            since, early = step - 1 - stage, step - LAGS[stage]
+
+            @pl.when((early >= 0) & (early < TILES))
+            def _():
+                sums.advance(early, stage, FEED_ORDERS, fed)
+
+            @pl.when((since == GATE) | ((since >= BACK) & (since <= last_back)))
+            def _():
+                sums.advance(since - 1 - since // BACK, stage, MIX_ORDERS, mixed)
+
+            for join, result, begun in joins:
+
+                @pl.when(since == begun)
+                def _():
+                    join.advance(stage, result)
+
+    @pl.when(step < TILES)
+    def _():
+        feed(1, wup_b, wdn_b)
+        if summed:
+            sums.start(step, 0, FEED_ORDERS)
+
+    @pl.when(step == GATE)
+    def _():
+        for i in range(steps):
+            piece = contract(gout_s[...], mixed_s[:, i * BLOCK : (i + 1) * BLOCK], ((0,), (0,))).astype(BF16)
+            put(TILES, i, [piece[:, half * LANES : (half + 1) * LANES] for half in range(2)])
+        if summed:
+            sums.start(TILES, 0, MIX_ORDERS)
+
+    @pl.when(step == GATE)
+    def _():
+        rates = [vec[4:5, b * LANES : (b + 1) * LANES] for b in range(lane_blocks)]
+        tails = [vec[3:4, b * LANES : (b + 1) * LANES] * vec[5:6, b * LANES : (b + 1) * LANES] for b in range(lane_blocks)]
+        lams = [[jnp.exp(-rate * float(k)) for k in (1, 2, 4)] for rate in rates]
+        powers = [jnp.exp(-rate * (8 - row_id).astype(F32)) for rate in rates]
+
+        def scan_group(i, carry):
+            at = block // 8 - 1 - i
+            to = pl.ds(pl.multiple_of(at * 8, 8), 8)
+            start = pl.multiple_of(BEFORE + at * 8, 8)
+            own = ids[pl.ds(start, 8), :]
+            masks = [(own == ids[pl.ds(start + k, 8), :]) & (row_id < 8 - k) for k in (1, 2, 4)]
+            joined = own == jnp.broadcast_to(ids[pl.ds(start + 8, 1), :], (8, LANES))
+            states, biases, carries = [], [], []
+            for b in range(lane_blocks):
+                grad = glong_s[b, to, :]
+                value = grad * tails[b]
+                for mask, lam, k in zip(masks, lams[b], (1, 2, 4)):
+                    value += jnp.where(mask, lam * pltpu.roll(value, 8 - k, 0), 0.0)
+                value += jnp.where(joined, powers[b] * carry[0][b], 0.0)
+                q_s[b, to, :] = value
+                states.append(jnp.broadcast_to(value[0:1, :], (8, LANES)))
+                biases.append(carry[1][b] + grad * u[b, pl.ds(start, 8), :])
+                carries.append(carry[2][b] + grad * car_s[b, to, :])
+            return tuple(states), tuple(biases), tuple(carries)
+
+        many = (zero,) * lane_blocks
+        states, biases, carries = lax.fori_loop(0, block // 8, scan_group, (many, many, many), unroll=2)
+        for b in range(lane_blocks):
+            lanes = slice(b * LANES, (b + 1) * LANES)
+            first_s[:, lanes] = states[b][0:1, :]
+            head_s[1:2, lanes] = jnp.sum(biases[b], axis=0, keepdims=True)
+            head_s[2:3, lanes] = jnp.sum(carries[b], axis=0, keepdims=True)
+            halo_s[0:48, lanes] = glong_s[b, 0:48, :]
+            halo_s[48:56, lanes] = q_s[b, 0:8, :]
+            halo_s[72:80, lanes] = long_s[b, 0:8, :]
+        halo_s[56:72, :] = heads[...]
+        pushing.start()
+
+        @pl.when(pushing.me > 0)
+        def _():
+            halo_copy.start()
+
+    @pl.when(step == TAPS)
+    def _():
+        taps_s[...] = jnp.zeros_like(taps_s)
+
+        def pairs(p, _):
+            def chunk(j, _):
+                at = pl.ds(pl.multiple_of(j * 32, 32), 32)
+                start = BEFORE + j * 32
+                near = dist_s[at, :]
+                here = [glong_s[2 * p + k, at, :] for k in range(2)]
+                for tap in range(FIR):
+                    same = near >= float(tap)
+                    for k in range(2):
+                        term = jnp.where(same, here[k] * u[2 * p + k, pl.ds(start - tap, 32), :], 0.0)
+                        taps_s[2 * p + k, tap] += jnp.sum(term.reshape(4, 8, LANES), axis=0)
+                return 0
+
+            lax.fori_loop(0, groups, chunk, 0)
+            return 0
+
+        lax.fori_loop(0, lane_blocks // 2, pairs, 0)
+        result = joins[0][0].held.at[0] if summed else small_a
+        for b in range(lane_blocks):
+            lanes = slice(b * LANES, (b + 1) * LANES)
+            result[0:FIR, lanes] = jnp.sum(taps_s[b], axis=1)
+        result[FIR : FIR + 8, :] = head_s[...]
+        if summed:
+            joins[0][0].start(0)
+
+    @pl.when((step >= BACK) & (step <= last_back))
+    def _():
+        i = step - BACK
+        two = range(2)
+        lanes = [lanes_of(2 * i + k) for k in two]
+        rates = [vec[4:5, lanes[k]] for k in two]
+        scales = [vec[2:3, lanes[k]] - vec[3:4, lanes[k]] * vec[5:6, lanes[k]] for k in two]
         start = BEFORE + block
         own = ids[pl.ds(start, 8), :]
         end_id = marks[2 * n + jnp.minimum(pushing.me + 1, 2 * n - 1)].astype(F32)
@@ -970,7 +992,6 @@
             gc_s[1, k, block : block + 8, :] = halo_r[72:80, lanes[k]]
             gc_s[2, k, block : block + 8, :] = grad * halo_r[64:72, lanes[k]]
 
-        small = joins[1][0].held.at[0] if summed else small_b
         for k in two:
 
             def short(j, totals):
@@ -998,18 +1019,15 @@
             for s in range(3):
                 for d in range(3):
                     rows[3 * d + s] = jnp.sum(totals[3 * s + d], axis=0, keepdims=True)
-            rows.append(jnp.sum(crossed[k], axis=0, keepdims=True))
             for row, value in enumerate(rows):
-                small[row : row + 1, lanes[k]] = value
-
-        tile = TILES + i
+                note(row, i, slice(k * LANES, (k + 1) * LANES), value)
+
+        tile = TILES + 1 + i
         pieces = [contract(n1[...], gp_s[s], ((0,), (0,))).astype(BF16) for s in range(3)]
-        at = pl.ds(pl.multiple_of(i * BLOCK, BLOCK), BLOCK)
-        pieces.append(contract(gout_s[...], mixed_s[:, at], ((0,), (0,))).astype(BF16))
         for s, piece in enumerate(pieces):
-            put(tile, s * LANES, [piece[:, half * LANES : (half + 1) * LANES] for half in range(2)])
+            put(tile, s, [piece[:, half * LANES : (half + 1) * LANES] for half in range(2)])
         if summed:
-            sums.start(tile, 0)
+            sums.start(tile, 0, MIX_ORDERS)
         for s in range(3):
             gn_s[...] += contract(gp_s[s], win[s], ((1,), (1,)))
 
@@ -1027,21 +1045,24 @@
             return total
 
         gain_one = lax.fori_loop(0, groups, back, jnp.zeros((1, full), F32))
-        small = joins[1][0].held.at[0] if summed else small_b
-        small[10:11, :] = gain_one
-        small[11:16, :] = jnp.zeros((5, full), F32)
+        for k in range(steps):
+            note(10 + k, steps - 1, slice(0, BLOCK), gain_one[:, k * BLOCK : (k + 1) * BLOCK])
         if summed:
-            joins[1][0].start(0)
-            for copy in shares(1, middle_s, gtok_full):
+            for copy in shares(1, middle_s, gtok_o):
                 copy.start()
         else:
             gtok_o[...] = middle_s[...]
 
     if summed:
+        for join, _, begun in joins[1:]:
+
+            @pl.when(step == begun)
+            def _():
+                join.start(0)
 
         @pl.when(step == last_back + STAGES)
         def _():
-            for k, (src, dst) in enumerate(((out_s, out_full), (middle_s, gtok_full))):
+            for k, (src, dst) in enumerate(((out_s, out_o), (middle_s, gtok_o))):
                 for copy in shares(k, src, dst):
                     copy.wait()
 
@@ -1051,7 +1072,7 @@
     block, full = g.shape
     rows, lane_blocks = BEFORE + block, full // LANES
     steps = full // BLOCK
-    tiles = TILES + steps
+    tiles = TILES + 1 + steps
     reach = min(DOC_MOST // block + 1, 2 * n - 1)
     whole = lambda *shape: pl.BlockSpec(shape, lambda i: (0,) * len(shape), pipeline_mode=pl.Buffered(1))
     tile = lambda i: jnp.minimum(i, TILES - 1)
@@ -1060,18 +1081,20 @@
     stacked = lambda count, dtype=F32: pltpu.VMEM((lane_blocks, count, LANES), dtype)
     shape = jax.ShapeDtypeStruct
     if summed:
-        out_shape = [shape((full // 16, tiles * PART), F32)] * 2 + [shape((FIR + 8, full), F32), shape((16, full), F32)]
+        columns = TILES * TILE + (1 + steps) * len(MIX_ORDERS) * LANES
+        out_shape = [shape((full // 16, columns), F32), shape((FIR + 8, full), F32), shape((16, full), F32)]
         out_shape += [shape((2 * block, full // 2), F32)] * 2
-        out_specs = [whole(full // 16, tiles * PART)] * 2 + [whole(FIR + 8, full), whole(16, full)]
+        out_specs = [whole(full // 16, columns), whole(FIR + 8, full), whole(16, full)]
         out_specs += [pl.BlockSpec(memory_space=pl.ANY)] * 2
-        extra = Summing.scratch(tiles, TILES, full // 16) + Joining.scratch(FIR + 8, full) + Joining.scratch(16, full)
+        extra = Summing.scratch(tiles, TILES, full // 16) + Joining.scratch(FIR + 8, full)
+        extra += [pltpu.VMEM((steps, STAGES, 16, BLOCK), F32)] * 2 + [pltpu.SemaphoreType.DMA((steps, STAGES))] * 2
         extra += [pltpu.SemaphoreType.DMA((2,))] * 3
     else:
         out_shape = [shape((tiles, 2, full, TILE), BF16), shape((FIR + 8, full), F32), shape((16, full), F32)]
-        out_shape += [shape((block, full), F32)] * 2 + [shape((8, LANES), F32)]
-        place = lambda i: jnp.minimum(i, TILES - 1) + jnp.clip(i - BACK + 1, 0, steps)
+        out_shape += [shape((block, full), F32)] * 2
+        place = lambda i: jnp.minimum(i, TILES - 1) + jnp.clip(i - GATE + 1, 0, 1) + jnp.clip(i - BACK + 1, 0, steps)
         out_specs = [pl.BlockSpec((1, 2, full, TILE), lambda i: (place(i), 0, 0, 0)), whole(FIR + 8, full), whole(16, full)]
-        out_specs += [whole(block, full)] * 2 + [whole(8, LANES)]
+        out_specs += [whole(block, full)] * 2
         extra = []
     return pl.pallas_call(
         functools.partial(backward_kernel, n, block, reach, summed),
@@ -1115,13 +1138,14 @@
     both = lax.psum_scatter(grads.astype(F32), "ch", scatter_dimension=1, tiled=False)
     total = lax.psum_scatter(both, "seq", scatter_dimension=1, tiled=True)
     total = jnp.transpose(total, (1, 0, 2))
-    parts = [total[:, :, k * PART : (k + 1) * PART].reshape(total.shape[0], -1) for k in range(2)]
+    used = len(MIX_ORDERS) * LANES
+    total = jnp.concatenate([total[:, :TILES].reshape(total.shape[0], -1), total[:, TILES:, :used].reshape(total.shape[0], -1)], axis=1)
     swap = lambda whole: lax.all_to_all(whole, "ch", split_axis=1, concat_axis=0, tiled=True)
     small_a, small_b = lax.psum((small_a, small_b), ("seq", "ch"))
-    return *parts, small_a, small_b, swap(out), swap(gtok)
-
-
-def finish_kernel(part_a, part_b, small_a, small_b, gains, vec, table, w1, b1, w2, out, gtok,
+    return total, small_a, small_b, swap(out), swap(gtok)
+
+
+def finish_kernel(total, small_a, small_b, gains, vec, table, w1, b1, w2, out, gtok,
                   out_o, gtok_o, gain_one_o, in_o, short_o, w1_o, b1_o, w2_o, w3_o, bias_o, tgain_o, trate_o,
                   outw_o, gain_two_o, up_o, down_o, out_v, gtok_v, sem):
     full = gains.shape[1]
@@ -1152,7 +1176,8 @@
         copy.wait()
         following.start()
 
-    gain_one_o[...] = small_b[10:11, :].reshape(full)
+    last = [small_b[10 + k : 11 + k, full - BLOCK : full] for k in range(full // BLOCK)]
+    gain_one_o[...] = jnp.concatenate(last, axis=1).reshape(full)
     gain_two_o[...] = small_a[FIR : FIR + 1, :].reshape(full)
     bias_o[...] = natural(small_a[FIR + 1 : FIR + 2, :]).reshape(full)
     long_car, rate, nu = small_a[FIR + 2 : FIR + 3, :], vec[4:5, :], vec[5:6, :]
@@ -1163,20 +1188,21 @@
     for j in range(3):
         for s in range(3):
             short_o[j, s : s + 1, :] = short[3 * j + s : 3 * j + s + 1, :]
-    up_o[...] = part_a[:, 0:hidden]
-    down_o[...] = part_b[:, 0:hidden]
+    for k in range(TILES):
+        up_o[:, k * PART : (k + 1) * PART] = total[:, k * TILE : k * TILE + PART]
+        down_o[:, k * PART : (k + 1) * PART] = total[:, k * TILE + PART : (k + 1) * TILE]
+    outw_o[...] = total[:, TILES * TILE : TILES * TILE + width]
     for i in range(width // LANES):
-        at, lanes = hidden + i * PART, slice(i * LANES, (i + 1) * LANES)
-        for s, (ref, start) in enumerate(((part_a, at), (part_a, at + LANES), (part_b, at))):
-            in_o[s, :, lanes] = ref[:, start : start + LANES]
-        outw_o[:, lanes] = part_b[:, at + LANES : at + 2 * LANES]
+        for s in range(3):
+            at = TILES * TILE + (1 + i) * len(MIX_ORDERS) * LANES + s * LANES
+            in_o[s, :, i * LANES : (i + 1) * LANES] = total[:, at : at + LANES]
     for copy in saves:
         copy.wait()
 
 
-def finish(part_a, part_b, small_a, small_b, gains, vec, table, w1, b1, w2, out, gtok):
-    full, rows = gains.shape[1], part_a.shape[0]
-    width, hidden = full // 2, part_a.shape[1] - full // 2 // LANES * PART
+def finish(total, small_a, small_b, gains, vec, table, w1, b1, w2, out, gtok):
+    full, rows = gains.shape[1], total.shape[0]
+    width, hidden = full // 2, TILES * PART
     shape = jax.ShapeDtypeStruct
     vmem, anywhere = pl.BlockSpec(memory_space=pltpu.VMEM), pl.BlockSpec(memory_space=pl.ANY)
     vector = shape((full,), F32)
@@ -1188,11 +1214,11 @@
             shape(w1.shape, F32), shape((b1.shape[1],), F32), shape(w2.shape, F32), shape((w2.shape[0], full), F32),
             vector, vector, vector, shape((rows, width), F32), vector, shape((rows, hidden), F32), shape((rows, hidden), F32),
         ),
-        in_specs=[vmem] * 10 + [anywhere] * 2,
+        in_specs=[vmem] * 9 + [anywhere] * 2,
         out_specs=(anywhere, anywhere) + (vmem,) * 14,
         scratch_shapes=[pltpu.VMEM(out.shape, F32), pltpu.VMEM(gtok.shape, F32), pltpu.SemaphoreType.DMA((4,))],
         compiler_params=pltpu.CompilerParams(vmem_limit_bytes=VMEM_LIMIT),
-    )(part_a, part_b, small_a, small_b, gains, vec, table, w1, b1, w2, out, gtok)
+    )(total, small_a, small_b, gains, vec, table, w1, b1, w2, out, gtok)
 
 
 def on_device(tokens, seg_ids, norm1_gain, in_weight, short_weight, filt_w1, filt_b1, filt_w2, filt_w3,
@@ -1226,12 +1252,12 @@
         n, summed, marks, tok, ids, dist, rest, enter, g, gains, vec, wout, x0, base, car, u, n1, heads,
         (up_weight, up_other), (down_weight, down_other), win, proj)
     if not summed:
-        results = reduce_plain(n, *results[:5])
-    part_a, part_b, small_a, small_b, out, gtok = results
+        results = reduce_plain(n, *results)
+    total, small_a, small_b, out, gtok = results
 
     (out, gtok, gain_one, in_grad, short_grad, w1_grad, b1_grad, w2_grad, w3_grad, bias_grad, tail_gain_grad, rate_grad,
      out_grad, gain_two, up_grad, down_grad) = finish(
-        part_a, part_b, small_a, small_b, gains, vec, table, filt_w1, filt_b1, filt_w2, out, gtok)
+        total, small_a, small_b, gains, vec, table, filt_w1, filt_b1, filt_w2, out, gtok)
     return (
         out, gtok, gain_one, jnp.transpose(in_grad, (1, 0, 2)), short_grad, w1_grad, b1_grad, w2_grad, w3_grad, bias_grad,
         tail_gain_grad, rate_grad, out_grad.T, gain_two, up_grad, down_grad.T,

time: 160 us -> 157 us (0.981)
  Pallas kernels: 154 us -> 151 us
    pallas_call x1, Pallas kernels: 117 us -> 114 us  [backward(): pl.pallas_call(functools.partial(backward_kernel, n, block, reach, summed...]
where the time goes in v4:
time: 157 us; the launch traced here: 156 us
  Pallas kernels  151 us (96%)
  other arithmetic  3.66 us (2%)
    pallas_call x1, Pallas kernels, backward(): pl.pallas_call(functools.partial(backward_kernel, n, block, reach, summed...  114 us
    pallas_call x1, Pallas kernels, forward(): pl.pallas_call(functools.partial(forward_kernel, n, rows, reach), name='f...  31.4 us
    pallas_call x1, Pallas kernels, finish(): pl.pallas_call(finish_kernel, name='finish', out_shape=(shape(out.shape,...  5.66 us

profile of v4, /device:TPU:0, one launch (start us, length us, event | category | flops | bytes accessed | tf_op | source)
XLA Modules:
  0.0 156.4 jit_solution(16348374067670314843)
XLA Ops:
  0.7 1.3 negate_sqrt_fusion.nus
  2.0 0.1 multiply_cosine_fusion
  2.1 0.7 pad_maximum_fusion.table
  2.8 0.9 fusion.1
  3.7 0.1 slice.7
  3.8 0.1 slice.6
  3.9 0.6 pad_add_fusion.marks
  4.5 0.1 concatenate.11
  4.6 0.1 dynamic-slice_convert_fusion
  4.7 0.9 broadcast_in_dim.21.ids
  5.6 31.4 %forward.1 = (bf16[560,768]{1,0:T(8,128)(2,1)}, bf16[512,768]{1,0:T(8,128)(2,1)}, bf16[3,768,768]{2,1,0:T(8,128)(2,1)}, bf16[768,768]{1,0:T(8,128)(2,1)}, bf16[7...) custom-call(s32[64]{0:T(128)} %pad_add_fusion.marks, ...), custom_call_target="tpu_custom_call" | custom-call | tf_op jit(solution)/shard_map/forward/pallas_call | solution.py:444
  36.9 113.7 %backward.1 = (f32[48,4608]{1,0:T(8,128)}, f32[40,768]{1,0:T(8,128)}, f32[16,768]{1,0:T(8,128)}, f32[1024,384]{1,0:T(8,128)}, f32[1024,384]{1,0:T(8,128)}) custom-call(s32[64]{0:T(128)} %pad_add_fusion.marks, bf16[560,768]{1,0:T(8,128)(2,1)} %get-tuple-element.55.tok, f32[640,128]{1,0:T(8,128)} %broadcast_in_dim.21.ids, ...), custom_call_target="tpu_custom_call" | custom-call | tf_op jit(solution)/shard_map/backward/pallas_call | solution.py:1099
  150.6 5.7 %finish.1 = (f32[1024,384]{1,0:T(8,128)}, f32[1024,384]{1,0:T(8,128)}, f32[768]{0:T(1024)}, f32[3,48,384]{2,1,0:T(8,128)}, f32[3,3,768]{2,1,0:T(4,128)}, /*index...) custom-call(f32[48,4608]{1,0:T(8,128)} %get-tuple-element.73.total, ...), custom_call_target="tpu_custom_call" | custom-call | tf_op jit(solution)/shard_map/finish/pallas_call | solution.py:1209
  (5 shorter events, 0.0 us)

commit v5 on v4

--- a/solution.py
+++ b/solution.py
@@ -2,6 +2,7 @@
 
 import jax
 import jax.numpy as jnp
+import numpy as np
 from jax import lax
 from jax.experimental import pallas as pl
 from jax.experimental.pallas import tpu as pltpu
@@ -28,14 +29,11 @@
 
 
 def position_table(filter_len, band_count):
-    places = jnp.arange(filter_len, dtype=F32)
-    harmonics = jnp.arange(1, band_count + 1, dtype=F32)
-    angles = FREQUENCY * places[:, None] * harmonics[None, :]
-    return jnp.concatenate([places[:, None] / filter_len, jnp.cos(angles), jnp.sin(angles)], axis=1)
-
-
-def of(ref, start, size):
-    return pl.ds(pl.multiple_of(start, size), size)
+    places = np.arange(filter_len, dtype=np.float32)
+    harmonics = np.arange(1, band_count + 1, dtype=np.float32)
+    angles = (np.float32(FREQUENCY) * places[:, None] * harmonics[None, :]).astype(np.float64)
+    table = np.concatenate([places[:, None] / filter_len, np.cos(angles), np.sin(angles)], axis=1)
+    return jnp.asarray(table.astype(np.float32))
 
 
 def filter_layers(table, w1, b1, w2):
@@ -554,20 +552,23 @@
             copy.start()
 
     def advance(self, tile, stage, orders, total):
-        for copy in self.copies(tile, stage, orders):
-            copy.wait()
         slot = tile % self.slots
+        arriving = self.copies(tile, stage, orders)
+        following = self.copies(tile, stage + 1, orders) if stage < STAGES - 1 else []
         if stage == 0:
-
-            def add(part, _):
-                for q in range(16):
-                    at = (q >> 3, q >> 2 & 1, q >> 1 & 1, q & 1)
-                    self.held[0][(slot, part, *at)] += self.staged[(tile % 2, 0, part, *at)]
-                return 0
-
-            lax.fori_loop(0, len(orders), add, 0)
-        else:
-            for part, order in enumerate(orders):
+            arriving[0].wait()
+        for part, order in enumerate(orders):
+            if stage == 0:
+
+                def add(i, _):
+                    for q in range(8):
+                        at = (q >> 2 & 1, q >> 1 & 1, q & 1)
+                        self.held[0][(slot, part, i, *at)] += self.staged[(tile % 2, 0, part, i, *at)]
+                    return 0
+
+                lax.fori_loop(0, 2, add, 0)
+            else:
+                arriving[part].wait()
                 mine = self.bits[order[stage - 1]]
                 for e in range(1 << (4 - stage)):
                     inner = [(e >> (3 - stage - k)) & 1 for k in range(4 - stage)]
@@ -576,8 +577,8 @@
                         total(tile, part, source.astype(F32) + self.held[stage][slot, part].astype(F32))
                     else:
                         self.held[stage][(slot, part, *inner)] += source
-        if stage < STAGES - 1:
-            self.start(tile, stage + 1, orders)
+            if following:
+                following[part].start()
 
 
 class Joining:
@@ -618,8 +619,19 @@
 
 TILES = 6
 EPILOGUE, GATE, TAPS, BACK = TILES, TILES + 1, TILES + 2, TILES + 3
+TURN_OF_BACK = TILES + 1
 LAGS = (1, 3, 5, 6, 7)
 HALO = 80
+
+
+def when(condition):
+    if isinstance(condition, bool):
+        return lambda body: body() if condition else None
+    return pl.when(condition)
+
+
+def lanes_at(start):
+    return pl.ds(start if isinstance(start, int) else pl.multiple_of(start, LANES), LANES)
 
 
 def backward_kernel(n, block, reach, summed, marks, tok, ids, dist_s, rest_s, enter, g, gains, vec, wout, x0, base, car, u, n1, heads,
@@ -632,7 +644,8 @@
     (mixed_s, middle_s, n2_s, gn_s, gout_s, out_s, gmid_s, long_s, car_s, glong_s, q_s, gc_s, gp_s, proj_s,
      taps_s, first_s, slots_s, joined_s, halo_s, halo_r, head_s,
      push_send, push_recv, halo_sem, *buffers) = refs
-    step = pl.program_id(0)
+    turn = pl.program_id(0)
+    step = turn + (BACK - TURN_OF_BACK) * (turn // TURN_OF_BACK)
     groups = block // 32
     barrier = pltpu.get_barrier_semaphore()
     pushing = Pushing(n, reach, True, first_s, slots_s, push_send, push_recv)
@@ -856,31 +869,34 @@
         for k in two:
             note(9, i, slice(k * LANES, (k + 1) * LANES), jnp.sum(crossed[k], axis=0, keepdims=True))
 
-    if summed:
-
-        def fed(tile, part, value):
-            grads_o[:, pl.ds(pl.multiple_of(tile * TILE + part * LANES, LANES), LANES)] = value
-
-        def mixed(tile, part, value):
-            at = TILES * TILE + (tile - TILES) * len(MIX_ORDERS) * LANES + part * LANES
-            grads_o[:, pl.ds(pl.multiple_of(at, LANES), LANES)] = value
+    def fed(tile, part, value):
+        grads_o[:, lanes_at(tile * TILE + part * LANES)] = value
+
+    def mixed(tile, part, value):
+        grads_o[:, lanes_at(TILES * TILE + (tile - TILES) * len(MIX_ORDERS) * LANES + part * LANES)] = value
+
+    def advance(step):
+        if not summed:
+            return
+        for stage in range(STAGES - 1, -1, -1):
+            for join, result, begun in joins:
+
+                @when(step - 1 - stage == begun)
+                def _():
+                    join.advance(stage, result)
 
         for stage in range(STAGES - 1, -1, -1):
             since, early = step - 1 - stage, step - LAGS[stage]
 
-            @pl.when((early >= 0) & (early < TILES))
+            @when((early >= 0) & (early < TILES))
             def _():
                 sums.advance(early, stage, FEED_ORDERS, fed)
 
-            @pl.when((since == GATE) | ((since >= BACK) & (since <= last_back)))
+            @when((since == GATE) | ((since >= BACK) & (since <= last_back)))
             def _():
                 sums.advance(since - 1 - since // BACK, stage, MIX_ORDERS, mixed)
 
-            for join, result, begun in joins:
-
-                @pl.when(since == begun)
-                def _():
-                    join.advance(stage, result)
+    advance(step)
 
     @pl.when(step < TILES)
     def _():
@@ -888,15 +904,16 @@
         if summed:
             sums.start(step, 0, FEED_ORDERS)
 
-    @pl.when(step == GATE)
+    @pl.when(step == EPILOGUE)
     def _():
         for i in range(steps):
             piece = contract(gout_s[...], mixed_s[:, i * BLOCK : (i + 1) * BLOCK], ((0,), (0,))).astype(BF16)
             put(TILES, i, [piece[:, half * LANES : (half + 1) * LANES] for half in range(2)])
         if summed:
             sums.start(TILES, 0, MIX_ORDERS)
-
-    @pl.when(step == GATE)
+        advance(GATE)
+
+    @pl.when(step == EPILOGUE)
     def _():
         rates = [vec[4:5, b * LANES : (b + 1) * LANES] for b in range(lane_blocks)]
         tails = [vec[3:4, b * LANES : (b + 1) * LANES] * vec[5:6, b * LANES : (b + 1) * LANES] for b in range(lane_blocks)]
@@ -939,8 +956,9 @@
         @pl.when(pushing.me > 0)
         def _():
             halo_copy.start()
-
-    @pl.when(step == TAPS)
+        advance(TAPS)
+
+    @pl.when(step == EPILOGUE)
     def _():
         taps_s[...] = jnp.zeros_like(taps_s)
 
@@ -1060,8 +1078,10 @@
             def _():
                 join.start(0)
 
-        @pl.when(step == last_back + STAGES)
+        @pl.when(step == last_back + 1)
         def _():
+            for drain in range(2, STAGES + 1):
+                advance(last_back + drain)
             for k, (src, dst) in enumerate(((out_s, out_o), (middle_s, gtok_o))):
                 for copy in shares(k, src, dst):
                     copy.wait()
@@ -1076,7 +1096,7 @@
     reach = min(DOC_MOST // block + 1, 2 * n - 1)
     whole = lambda *shape: pl.BlockSpec(shape, lambda i: (0,) * len(shape), pipeline_mode=pl.Buffered(1))
     tile = lambda i: jnp.minimum(i, TILES - 1)
-    back = lambda i: jnp.clip(i - BACK, 0, steps - 1)
+    back = lambda i: jnp.clip(i - TURN_OF_BACK, 0, steps - 1)
     wide = lambda dtype: pltpu.VMEM((block, full), dtype)
     stacked = lambda count, dtype=F32: pltpu.VMEM((lane_blocks, count, LANES), dtype)
     shape = jax.ShapeDtypeStruct
@@ -1092,14 +1112,14 @@
     else:
         out_shape = [shape((tiles, 2, full, TILE), BF16), shape((FIR + 8, full), F32), shape((16, full), F32)]
         out_shape += [shape((block, full), F32)] * 2
-        place = lambda i: jnp.minimum(i, TILES - 1) + jnp.clip(i - GATE + 1, 0, 1) + jnp.clip(i - BACK + 1, 0, steps)
+        place = lambda i: jnp.minimum(i, TILES - 1) + jnp.clip(i - EPILOGUE + 1, 0, 1) + jnp.clip(i - TURN_OF_BACK + 1, 0, steps)
         out_specs = [pl.BlockSpec((1, 2, full, TILE), lambda i: (place(i), 0, 0, 0)), whole(FIR + 8, full), whole(16, full)]
         out_specs += [whole(block, full)] * 2
         extra = []
     return pl.pallas_call(
         functools.partial(backward_kernel, n, block, reach, summed),
         name="backward",
-        grid=(BACK + steps + (STAGES if summed else 0),),
+        grid=(TURN_OF_BACK + steps + (1 if summed else 0),),
         out_shape=out_shape,
         in_specs=[
             pl.BlockSpec(memory_space=pltpu.SMEM),

time: 157 us -> 155 us (0.987)
  no operation moved by 1% of the time
where the time goes in v5:
time: 155 us
  Pallas kernels  150 us (97%)
  other arithmetic  2.81 us (2%)
    pallas_call x1, Pallas kernels, backward(): pl.pallas_call(functools.partial(backward_kernel, n, block, reach, summed...  113 us
    pallas_call x1, Pallas kernels, forward(): pl.pallas_call(functools.partial(forward_kernel, n, rows, reach), name='f...  31.3 us
    pallas_call x1, Pallas kernels, finish(): pl.pallas_call(finish_kernel, name='finish', out_shape=(shape(out.shape,...  5.66 us

profile of v5, /device:TPU:0, one launch (start us, length us, event | category | flops | bytes accessed | tf_op | source)
XLA Modules:
  0.0 154.9 jit_solution(12656565756826157181)
XLA Ops:
  0.7 1.3 negate_sqrt_fusion.nus
  1.9 0.9 fusion.1
  2.8 0.1 slice.7
  2.9 0.1 slice.6
  3.0 0.6 pad_add_fusion.marks
  3.6 0.1 concatenate.7
  3.7 0.1 dynamic-slice_convert_fusion
  3.8 0.9 broadcast_in_dim.18.ids
  4.7 31.3 %forward.1 = (bf16[560,768]{1,0:T(8,128)(2,1)}, bf16[512,768]{1,0:T(8,128)(2,1)}, bf16[3,768,768]{2,1,0:T(8,128)(2,1)}, bf16[768,768]{1,0:T(8,128)(2,1)}, bf16[7...) custom-call(s32[64]{0:T(128)} %pad_add_fusion.marks, ...), custom_call_target="tpu_custom_call" | custom-call | tf_op jit(solution)/shard_map/forward/pallas_call | solution.py:442
  36.0 113.1 %backward.1 = (f32[48,4608]{1,0:T(8,128)}, f32[40,768]{1,0:T(8,128)}, f32[16,768]{1,0:T(8,128)}, f32[1024,384]{1,0:T(8,128)}, f32[1024,384]{1,0:T(8,128)}) custom-call(s32[64]{0:T(128)} %pad_add_fusion.marks, bf16[560,768]{1,0:T(8,128)(2,1)} %get-tuple-element.55.tok, f32[640,128]{1,0:T(8,128)} %broadcast_in_dim.18.ids, ...), custom_call_target="tpu_custom_call" | custom-call | tf_op jit(solution)/shard_map/backward/pallas_call | solution.py:1119
  149.1 5.7 %finish.1 = (f32[1024,384]{1,0:T(8,128)}, f32[1024,384]{1,0:T(8,128)}, f32[768]{0:T(1024)}, f32[3,48,384]{2,1,0:T(8,128)}, f32[3,3,768]{2,1,0:T(4,128)}, /*index...) custom-call(f32[48,4608]{1,0:T(8,128)} %get-tuple-element.73.total, ...), custom_call_target="tpu_custom_call" | custom-call | tf_op jit(solution)/shard_map/finish/pallas_call | solution.py:1229
  (2 shorter events, 0.0 us)

commit v6 on v5

--- a/solution.py
+++ b/solution.py
@@ -352,7 +352,7 @@
             return tuple(result)
 
         zero = jnp.zeros((8, LANES), F32)
-        final = lax.fori_loop(0, block // 8, scan_group, (zero,) * len(two), unroll=4)
+        final = lax.fori_loop(0, block // 8, scan_group, (zero,) * len(two), unroll=8)
         for b in two:
             end_s[:, lanes[b]] = final[b][0:1, :]
 
@@ -941,7 +941,7 @@
             return tuple(states), tuple(biases), tuple(carries)
 
         many = (zero,) * lane_blocks
-        states, biases, carries = lax.fori_loop(0, block // 8, scan_group, (many, many, many), unroll=2)
+        states, biases, carries = lax.fori_loop(0, block // 8, scan_group, (many, many, many), unroll=4)
         for b in range(lane_blocks):
             lanes = slice(b * LANES, (b + 1) * LANES)
             first_s[:, lanes] = states[b][0:1, :]

time: 155 us -> 155 us (level)
  no operation moved by 1% of the time
where the time goes in v6:
time: 155 us
  Pallas kernels  150 us (97%)
  other arithmetic  2.81 us (2%)
    pallas_call x1, Pallas kernels, backward(): pl.pallas_call(functools.partial(backward_kernel, n, block, reach, summed...  113 us
    pallas_call x1, Pallas kernels, forward(): pl.pallas_call(functools.partial(forward_kernel, n, rows, reach), name='f...  31.1 us
    pallas_call x1, Pallas kernels, finish(): pl.pallas_call(finish_kernel, name='finish', out_shape=(shape(out.shape,...  5.66 us

profile of v6, /device:TPU:0, one launch (start us, length us, event | category | flops | bytes accessed | tf_op | source)
XLA Modules:
  0.0 155.0 jit_solution(11395880005583407762)
XLA Ops:
  0.7 1.3 negate_sqrt_fusion.nus
  1.9 0.9 fusion.1
  2.8 0.1 slice.7
  2.9 0.1 slice.6
  3.0 0.6 pad_add_fusion.marks
  3.6 0.1 concatenate.7
  3.7 0.1 dynamic-slice_convert_fusion
  3.8 0.9 broadcast_in_dim.18.ids
  4.7 31.1 %forward.1 = (bf16[560,768]{1,0:T(8,128)(2,1)}, bf16[512,768]{1,0:T(8,128)(2,1)}, bf16[3,768,768]{2,1,0:T(8,128)(2,1)}, bf16[768,768]{1,0:T(8,128)(2,1)}, bf16[7...) custom-call(s32[64]{0:T(128)} %pad_add_fusion.marks, ...), custom_call_target="tpu_custom_call" | custom-call | tf_op jit(solution)/shard_map/forward/pallas_call | solution.py:442
  35.8 113.4 %backward.1 = (f32[48,4608]{1,0:T(8,128)}, f32[40,768]{1,0:T(8,128)}, f32[16,768]{1,0:T(8,128)}, f32[1024,384]{1,0:T(8,128)}, f32[1024,384]{1,0:T(8,128)}) custom-call(s32[64]{0:T(128)} %pad_add_fusion.marks, bf16[560,768]{1,0:T(8,128)(2,1)} %get-tuple-element.55.tok, f32[640,128]{1,0:T(8,128)} %broadcast_in_dim.18.ids, ...), custom_call_target="tpu_custom_call" | custom-call | tf_op jit(solution)/shard_map/backward/pallas_call | solution.py:1119
  149.1 5.7 %finish.1 = (f32[1024,384]{1,0:T(8,128)}, f32[1024,384]{1,0:T(8,128)}, f32[768]{0:T(1024)}, f32[3,48,384]{2,1,0:T(8,128)}, f32[3,3,768]{2,1,0:T(4,128)}, /*index...) custom-call(f32[48,4608]{1,0:T(8,128)} %get-tuple-element.73.total, ...), custom_call_target="tpu_custom_call" | custom-call | tf_op jit(solution)/shard_map/finish/pallas_call | solution.py:1229
  (2 shorter events, 0.0 us)
